TPU v7x, 768 devices: a whole 4x8x12 slice. The times are simulated.
768 devices in a mesh: pool: 8 (over y_hi, core), col: 96 (over x, z, y_lo).
Axes of the slice: x: 4, y: 8 (y_hi: 4, y_lo: 2; y = y_hi * 2 + y_lo), z: 12, core: 2. Of those that a mesh axis runs over, the one named last changes fastest.
Arguments:
- pair_matrix: bfloat16 [2048, 12288], P('pool', 'col'), may hold values from -1.1953125 to 1.1953125
- band_energy: float32 [8, 4, 4096], P('pool'), may hold values from -2 to 2
- occupation: int32 [8, 4, 4096], P('pool'), may hold values 0 or 1
- pair_first: int32 [8, 256], P('pool'), may hold values from 0 to 4095
- pair_second: int32 [8, 256], P('pool'), may hold values from 0 to 4095
- pair_kpoint: int32 [8, 256], P('pool'), may hold values from 0 to 3
Outputs:
- chi_zero: float32 [12288, 12288], P('pool', 'col')
All inputs are finite; a program needn't handle non-finite values. No bound on the sum of `occupation` on one device may be relied on, other than what follows from the above.
Results may differ from a plain program's by a relative error of at most 0.012.
Values may be sent and summed in bfloat16 or wider, within the bound.
No kernel may reach another device: no remote copies, remote signals or barrier semaphores. Data moves between devices by JAX's collectives and lax.ppermute only.
A program may use at most 32 MiB of HBM per device.

v0:
```python
import jax
import jax.numpy as jnp
from jax import lax
from jax.sharding import PartitionSpec as P


def pool_weight(energy, occupied, first, second, kpoint):
    bands = energy.shape[-1]
    flat_energy = energy.reshape(-1)
    flat_occupied = occupied.reshape(-1).astype(jnp.float32)
    index_first = kpoint * bands + first
    index_second = kpoint * bands + second
    gap = jnp.abs(jnp.take(flat_energy, index_second) - jnp.take(flat_energy, index_first))
    filled = jnp.take(flat_occupied, index_first) - jnp.take(flat_occupied, index_second)
    return 2.0 * filled / (1.0 + gap)


def inner_pairs(left, right):
    return lax.dot_general(
        left, right, (((0,), (0,)), ((), ())), preferred_element_type=jnp.float32
    )


def per_device(pair_matrix, band_energy, occupation, pair_first, pair_second, pair_kpoint):
    weight = pool_weight(
        band_energy[0], occupation[0], pair_first[0], pair_second[0], pair_kpoint[0]
    )
    scaled = (pair_matrix.astype(jnp.float32) * weight[:, None]).astype(jnp.bfloat16)
    partial_rows = inner_pairs(lax.all_gather(pair_matrix, "col", axis=1, tiled=True), scaled)
    chi_zero = lax.psum_scatter(
        partial_rows.astype(jnp.bfloat16), "pool", scatter_dimension=0, tiled=True
    ).astype(jnp.float32)
    return chi_zero


def solution(mesh):
    return jax.shard_map(
        per_device,
        mesh=mesh,
        in_specs=(
            P("pool", "col"),
            P("pool", None, None),
            P("pool", None, None),
            P("pool", None),
            P("pool", None),
            P("pool", None),
        ),
        out_specs=P("pool", "col"),
        check_vma=False,
    )
```

profile of v0, /device:TPU:1, one launch (start us, length us, event | category | flops | bytes accessed | tf_op | source)
XLA Modules:
  0.0 457.7 jit_solution(11983523956986094541)
XLA Ops:
  6.5 0.0 all-gather.2.cloned.1.call-start
  6.5 0.7 all-gather.2.cloned.1.call-update
  7.3 0.0 reduce-scatter.2.cloned.1.call-start
  7.3 0.8 copy.10
  8.1 0.7 multiply_add_fusion
  8.9 1.7 gather_fusion.3
  10.6 1.7 gather_fusion.2
  12.4 0.9 convert_bitcast_fusion
  13.2 1.7 gather_fusion.1
  15.0 1.7 gather_fusion
  16.7 316.6 %all-gather.2.cloned.1.call-done = bf16[256,12288]{1,0:T(8,128)(2,1)} async-done(((bf16[256,128]{1,0:T(8,128)(2,1)}), bf16[256,12288]{1,0:T(8,128)(2,1)}) %all-gather.2.cloned.1.call-update) | async-done | bytes 6291472 | tf_op jit(solution)/shard_map/all_gather | solution.py:29
  333.3 5.6 %fusion = bf16[12288,128]{0,1:T(8,128)(2,1)} fusion(bf16[256,12288]{1,0:T(8,128)(2,1)} %all-gather.2.cloned.1.call-done, bf16[256,128]{1,0:T(8,128)(2,1)} %param.8, f32[256]{0:T(256)S(1)} %fusion.4), kind=kOutput, calls=%fused_computation.5 | convolution fusion | flops 806977536 | bytes 9503744 | tf_op jit(solution)/shard_map/dot_general | solution.py:19
  338.9 0.0 reduce-scatter.2.cloned.1.call-update
  338.9 109.9 %reduce-scatter.2.cloned.1.call-done = bf16[1536,128]{0,1:T(8,128)(2,1)} async-done(((bf16[12288,128]{0,1:T(8,128)(2,1)}), bf16[1536,128]{0,1:T(8,128)(2,1)}) %reduce-scatter.2.cloned.1.call-update) | async-done | bytes 393232 | tf_op jit(solution)/shard_map/reduce_scatter | solution.py:30
  448.8 2.0 copy.8
  (6 shorter events, 0.0 us)
Async XLA Ops:
  6.5 326.7 %all-gather.2.cloned.1.call-start = ((), (), s32[]{:S(2)}) async-start(), calls=%async_computation.1 | async-start | bytes 6356992 | tf_op jit(solution)/shard_map/all_gather | solution.py:29
  7.3 441.6 %reduce-scatter.2.cloned.1.call-start = ((), (), s32[]{:S(2)}) async-start(), calls=%async_computation.2 | async-start | bytes 3538944 | tf_op jit(solution)/shard_map/reduce_scatter | solution.py:30
Sparse Core Ops, SparseCore 0:
  9.6 323.5 all-gather.1
  339.1 109.7 reduce-scatter.1
where the time goes:
time: 460 us; the launch traced here: 458 us
  waiting for transfers between devices  427 us (93%)
  between operations  13.5 us (3%)
  local copies, waits for them, and re-layouts  9.78 us (2%)
  matrix products  5.62 us (1%)
    all_gather x1, waiting for transfers between devices, per_device(): lax.all_gather(pair_matrix, 'col', axis=1, tiled=True)  317 us
    reduce_scatter x1, waiting for transfers between devices, per_device(): lax.psum_scatter(partial_rows.astype(jnp.bfloat16), 'pool', scatter_dimen...  110 us
  transfers between devices with their start and end apart: 2, of which 2 were waited for; matrix products, arithmetic and copies ran while one was open for 2% of the time, Pallas kernels for 0%

commit v1 on v0

v1 whole, which is shorter than its diff:
```python
import jax
import jax.numpy as jnp
from jax import lax
from jax.experimental import pallas as pl
from jax.experimental.pallas import tpu as pltpu
from jax.sharding import PartitionSpec as P

H, K, X, Z, L = 4, 2, 4, 12, 2
COLS = X * Z * L
PAIRS, WIDTH = 256, 128
AXES = ("pool", "col")


def at(h, k, x, z, l):
    return ((h % H) * K + k) * COLS + (x % X) * (Z * L) + (z % Z) * L + l


def table(f):
    return [
        (at(h, k, x, z, l), at(*f(h, k, x, z, l)))
        for h in range(H)
        for k in range(K)
        for x in range(X)
        for z in range(Z)
        for l in range(L)
    ]


def move(value, f):
    return lax.ppermute(value, AXES, table(f))


Z_GROUPS = [[x * Z * L + z * L + l for z in range(Z)] for x in range(X) for l in range(L)]


def scale_kernel(energy, occupied, first, second, kpoint, block, out, energies, filled):
    chunks = energy.shape[-1] // WIDTH
    kpts = energy.shape[-2]
    for c in range(chunks):
        part = pl.ds(c * WIDTH, WIDTH)
        energies[pl.ds(c * kpts, kpts), :] = energy[0, :, part]
        filled[pl.ds(c * kpts, kpts), :] = occupied[0, :, part].astype(jnp.float32)

    def pick(table_ref, band):
        entries = table_ref.shape[0]
        place = (band // WIDTH) * kpts + kpoint[...]
        spot = band % WIDTH
        pairs = band.shape[-1]
        one = (lax.broadcasted_iota(jnp.int32, (entries, pairs), 0) == place).astype(jnp.float32)
        found = lax.dot_general(
            table_ref[...],
            one,
            (((0,), (0,)), ((), ())),
            precision=lax.Precision.HIGHEST,
            preferred_element_type=jnp.float32,
        )
        keep = lax.broadcasted_iota(jnp.int32, (WIDTH, pairs), 0) == spot
        return jnp.sum(jnp.where(keep, found, 0.0), axis=0, keepdims=True)

    a, b = first[...], second[...]
    gap = jnp.abs(pick(energies, b) - pick(energies, a))
    change = pick(filled, a) - pick(filled, b)
    weight = 2.0 * change / (1.0 + gap)
    for i in range(PAIRS // WIDTH):
        rows = pl.ds(i * WIDTH, WIDTH)
        factor = jnp.broadcast_to(weight[:, i * WIDTH : (i + 1) * WIDTH], (WIDTH, WIDTH)).T
        out[rows, :] = (block[rows, :].astype(jnp.float32) * factor).astype(jnp.bfloat16)


def scaled_block(energy, occupied, first, second, kpoint, block):
    entries = energy.shape[1] * energy.shape[2] // WIDTH
    return pl.pallas_call(
        scale_kernel,
        out_shape=jax.ShapeDtypeStruct(block.shape, jnp.bfloat16),
        scratch_shapes=[pltpu.VMEM((entries, WIDTH), jnp.float32)] * 2,
        cost_estimate=pl.CostEstimate(flops=4 * 10**8, bytes_accessed=3 * 10**5, transcendentals=0),
        name="scale",
    )(energy, occupied, first, second, kpoint, block)


def product_kernel(place, rows, c0, c1, c2, c3, out):
    pieces = [jnp.concatenate([rows[3 * s + j] for s in range(H)], axis=0) for j in range(3)]
    left = jnp.concatenate(pieces, axis=1)
    right = jnp.concatenate([c[0] for c in (c0, c1, c2, c3)], axis=1)
    found = lax.dot_general(
        left, right, (((0,), (0,)), ((), ())), preferred_element_type=jnp.float32
    )
    for i in range(X):
        out[(i + place[1]) % X] = found[:, i * WIDTH : (i + 1) * WIDTH].astype(out.dtype)


def product(side, turn, rows, columns, dtype, name):
    depth = columns[0].shape[1]
    place = jnp.stack([side, turn]).astype(jnp.int32)
    return pl.pallas_call(
        product_kernel,
        out_shape=jax.ShapeDtypeStruct((X, 3 * WIDTH, WIDTH), dtype),
        grid_spec=pltpu.PrefetchScalarGridSpec(
            num_scalar_prefetch=1,
            grid=(1,),
            in_specs=[pl.BlockSpec(rows.shape, lambda i, p: (0, 0, 0))]
            + [pl.BlockSpec((1, depth, WIDTH), lambda i, p: (p[0], 0, 0))] * X,
            out_specs=pl.BlockSpec((X, 3 * WIDTH, WIDTH), lambda i, p: (0, 0, 0)),
        ),
        cost_estimate=pl.CostEstimate(flops=4 * 10**8, bytes_accessed=3 * 10**6, transcendentals=0),
        name=name,
    )(place, rows, *columns)


def assemble_kernel(order, f0, f1, f2, f3, out):
    for i, piece in enumerate((f0, f1, f2, f3)):
        t = order[i]
        for j in range(3):
            out[t % 2, j, t // 2] = piece[j * WIDTH : (j + 1) * WIDTH, :].astype(jnp.float32)


def assemble(order, pieces):
    return pl.pallas_call(
        assemble_kernel,
        out_shape=jax.ShapeDtypeStruct((2, 3, 2, WIDTH, WIDTH), jnp.float32),
        in_specs=[pl.BlockSpec(memory_space=pltpu.SMEM)] + [pl.BlockSpec(memory_space=pltpu.VMEM)] * 4,
        out_specs=pl.BlockSpec(memory_space=pltpu.VMEM),
        name="assemble",
    )(order, *pieces)


def per_device(pair_matrix, band_energy, occupation, pair_first, pair_second, pair_kpoint):
    pool, col = lax.axis_index("pool"), lax.axis_index("col")
    k, x, l = pool % K, col // (Z * L), col % L

    around = [
        move(pair_matrix, lambda h, k, x, z, l, s=s: (h - s, k, x, z, l)) for s in range(1, H)
    ]
    scaled = scaled_block(
        band_energy, occupation, pair_first, pair_second, pair_kpoint, pair_matrix
    )
    sent = move(
        scaled, lambda h, k, x, z, l: (x, k, z // 3, 3 * ((h - x) % H) + z % 3, l)
    )
    own = jnp.concatenate([pair_matrix] + around, axis=0)
    other = move(own, lambda h, k, x, z, l: (h, k, x, z, 1 - l))
    both = jnp.stack([own, other])
    columns = [both] + [
        move(both, lambda h, k, x, z, l, s=s: (h, k, x - s, z, l)) for s in range(1, X)
    ]
    rows = lax.all_gather(sent, "col", axis=0, axis_index_groups=Z_GROUPS)

    turn = 2 * l
    give = product(1 - k, turn, rows, columns, jnp.bfloat16, "give")
    taken = move(give, lambda h, k, x, z, l: (h, 1 - k, x, z, l))
    keep = product(k, turn, rows, columns, jnp.float32, "keep")
    total = (keep + taken.astype(jnp.float32)).astype(jnp.bfloat16)
    home = [
        move(total[r], lambda h, k, x, z, l, r=r: (h, x // 2, x + r + 2 * l, z, l ^ k))
        for r in range(X)
    ]
    order = (x - 2 * k - jnp.arange(X, dtype=jnp.int32)) % X
    return assemble(order.astype(jnp.int32), home).reshape(-1, WIDTH)


def solution(mesh):
    return jax.shard_map(
        per_device,
        mesh=mesh,
        in_specs=(
            P("pool", "col"),
            P("pool", None, None),
            P("pool", None, None),
            P("pool", None),
            P("pool", None),
            P("pool", None),
        ),
        out_specs=P("pool", "col"),
        check_vma=False,
    )
```

time: 460 us -> 130 us (0.28)
  waiting for transfers between devices: 427 us -> 11.6 us
  starting transfers between devices: 0.04 us -> 55.1 us
  blocking collectives: 0 us -> 45.2 us
  between operations: 13.5 us -> 0.22 us
  Pallas kernels: 0 us -> 11.4 us
  local copies, waits for them, and re-layouts: 9.78 us -> 2.68 us
  matrix products: 5.62 us -> 0 us
    all_gather x1 -> x0, waiting for transfers between devices: 317 us -> none  [per_device(): lax.all_gather(pair_matrix, 'col', axis=1, tiled=True)]
    reduce_scatter x1 -> x0, waiting for transfers between devices: 110 us -> none  [per_device(): lax.psum_scatter(partial_rows.astype(jnp.bfloat16), 'pool', scatter_dimen...]
    ppermute x0 -> x13, starting transfers between devices: none -> 55.1 us  [move(): return lax.ppermute(value, AXES, table(f))]
    all_gather x0 -> x1, blocking collectives: none -> 45.2 us  [per_device(): rows = lax.all_gather(sent, 'col', axis=0, axis_index_groups=Z_GROUPS)]
    ppermute x0 -> x13, waiting for transfers between devices: none -> 11.6 us  [move(): return lax.ppermute(value, AXES, table(f))]
    pallas_call x0 -> x4, Pallas kernels: none -> 11.4 us  [the longest x2 7.06 us: product(): pl.pallas_call(product_kernel, out_shape=jax.ShapeDtypeStruct((X, 3 * WID...]
    gather x4 -> x0, local copies, waits for them, and re-layouts: 6.89 us -> none  [the longest x1 1.72 us: pool_weight(): jnp.take(flat_energy, index_second) - jnp.take(flat_energy, index_first)]
    dot_general x1 -> x0, matrix products: 5.62 us -> none  [inner_pairs(): lax.dot_general(left, right, (((0,), (0,)), ((), ())), preferred_element_...]
  transfers between devices with their start and end apart: 2 -> 13, of which waited for: 2 -> 4; matrix products, arithmetic and copies ran while one was open for 2% -> 2% of each run, Pallas kernels for 0% -> 5%
where the time goes in v1:
time: 130 us; the launch traced here: 129 us
  starting transfers between devices  55.1 us (42%)
  blocking collectives  45.2 us (35%)
  waiting for transfers between devices  11.6 us (9%)
  Pallas kernels  11.4 us (9%)
  other arithmetic  3.02 us (2%)
  local copies, waits for them, and re-layouts  2.68 us (2%)
    ppermute x13, starting transfers between devices, move(): return lax.ppermute(value, AXES, table(f))  55.1 us
    all_gather x1, blocking collectives, per_device(): rows = lax.all_gather(sent, 'col', axis=0, axis_index_groups=Z_GROUPS)  45.2 us
    ppermute x13, waiting for transfers between devices, move(): return lax.ppermute(value, AXES, table(f))  11.6 us
    pallas_call x2, Pallas kernels, product(): pl.pallas_call(product_kernel, out_shape=jax.ShapeDtypeStruct((X, 3 * WID...  7.06 us
    unnamed x19, local copies, waits for them, and re-layouts  2.64 us
  transfers between devices with their start and end apart: 13, of which 4 were waited for; matrix products, arithmetic and copies ran while one was open for 2% of the time, Pallas kernels for 5%

profile of v1, /device:TPU:1, one launch (start us, length us, event | category | flops | bytes accessed | tf_op | source)
XLA Modules:
  0.0 129.2 jit_solution(13827502690929442525)
XLA Ops:
  0.0 8.3 %collective-permute-start.2 = (bf16[256,128]{1,0:T(8,128)(2,1)}, bf16[256,128]{1,0:T(8,128)(2,1)S(1)}, u32[]{:S(2)}, u32[]{:S(2)}) collective-permute-start(bf16[256,128]{1,0:T(8,128)(2,1)} %block.1), channel_id=1, source_target_pairs={{0,384},{1,385},{2,386},{3,387},{4,388},{5,389},{6,390},{7,391},{8... | collective-permute-start | bytes 196616 | tf_op jit(solution)/shard_map/ppermute | solution.py:30
  8.3 2.0 %collective-permute-start.1 = (bf16[256,128]{1,0:T(8,128)(2,1)}, bf16[256,128]{1,0:T(8,128)(2,1)S(1)}, u32[]{:S(2)}, u32[]{:S(2)}) collective-permute-start(bf16[256,128]{1,0:T(8,128)(2,1)} %block.1), channel_id=1, source_target_pairs={{0,576},{1,577},{2,578},{3,579},{4,580},{5,581},{6,582},{7,583},{8... | collective-permute-start | bytes 196616 | tf_op jit(solution)/shard_map/ppermute | solution.py:30
  10.2 4.2 %collective-permute-start.3 = (bf16[256,128]{1,0:T(8,128)(2,1)}, bf16[256,128]{1,0:T(8,128)(2,1)S(1)}, u32[]{:S(2)}, u32[]{:S(2)}) collective-permute-start(bf16[256,128]{1,0:T(8,128)(2,1)} %block.1), channel_id=1, source_target_pairs={{0,192},{1,193},{2,194},{3,195},{4,196},{5,197},{6,198},{7,199},{8... | collective-permute-start | bytes 196616 | tf_op jit(solution)/shard_map/ppermute | solution.py:30
  14.5 0.9 constant_dynamic-update-slice_fusion.3
  15.3 0.0 collective-permute-done.1
  15.3 0.0 collective-permute-done.2
  15.4 2.4 %collective-permute-done.3 = bf16[256,128]{1,0:T(8,128)(2,1)S(1)} collective-permute-done((bf16[256,128]{1,0:T(8,128)(2,1)}, bf16[256,128]{1,0:T(8,128)(2,1)S(1)}, u32[]{:S(2)}, u32[]{:S(2)}) %collective-permute-start.3) | collective-permute-done | bytes 65568 | tf_op jit(solution)/shard_map/ppermute | solution.py:30
  17.8 3.7 %collective-permute-start.4 = (bf16[1024,128]{1,0:T(8,128)(2,1)S(1)}, bf16[1024,128]{1,0:T(8,128)(2,1)S(1)}, u32[]{:S(2)}, u32[]{:S(2)}) collective-permute-start(bf16[1024,128]{1,0:T(8,128)(2,1)S(1)} %constant_dynamic-update-slice_fusion), channel_id=1, source_target_pairs={{0,1},{1,0},{2,3},{3,2},{4,5},{5,4},{6,7},{7,6},{8,9},{9,8},{10,11... | collective-permute-start | bytes 786440 | tf_op jit(solution)/shard_map/ppermute | solution.py:30
  21.5 4.0 %collective-permute-done.4 = bf16[1024,128]{1,0:T(8,128)(2,1)S(1)} collective-permute-done((bf16[1024,128]{1,0:T(8,128)(2,1)S(1)}, bf16[1024,128]{1,0:T(8,128)(2,1)S(1)}, u32[]{:S(2)}, u32[]{:S(2)}) %collective-permute-start.4) | collective-permute-done | bytes 262176 | tf_op jit(solution)/shard_map/ppermute | solution.py:30
  25.5 0.1 pad_maximum_fusion.c0
  25.5 0.0 copy-start
  25.5 3.7 %collective-permute-start.7 = (bf16[2,1024,128]{2,1,0:T(8,128)(2,1)S(1)}, bf16[2,1024,128]{2,1,0:T(8,128)(2,1)S(1)}, u32[]{:S(2)}, u32[]{:S(2)}) collective-permute-start(bf16[2,1024,128]{2,1,0:T(8,128)(2,1)S(1)} %pad_maximum_fusion.c0), channel_id=1, source_target_pairs={{0,24},{1,25},{2,26},{3,27},{4,28},{5,29},{6,30},{7,31},{8,32},{9,... | collective-permute-start | bytes 1572872 | tf_op jit(solution)/shard_map/ppermute | solution.py:30
  29.3 4.4 %collective-permute-start.6 = (bf16[2,1024,128]{2,1,0:T(8,128)(2,1)S(1)}, bf16[2,1024,128]{2,1,0:T(8,128)(2,1)S(1)}, u32[]{:S(2)}, u32[]{:S(2)}) collective-permute-start(bf16[2,1024,128]{2,1,0:T(8,128)(2,1)S(1)} %pad_maximum_fusion.c0), channel_id=1, source_target_pairs={{0,48},{1,49},{2,50},{3,51},{4,52},{5,53},{6,54},{7,55},{8,56},{9,... | collective-permute-start | bytes 1572872 | tf_op jit(solution)/shard_map/ppermute | solution.py:30
  33.6 3.1 %collective-permute-start.5 = (bf16[2,1024,128]{2,1,0:T(8,128)(2,1)S(1)}, bf16[2,1024,128]{2,1,0:T(8,128)(2,1)S(1)}, u32[]{:S(2)}, u32[]{:S(2)}) collective-permute-start(bf16[2,1024,128]{2,1,0:T(8,128)(2,1)S(1)} %pad_maximum_fusion.c0), channel_id=1, source_target_pairs={{0,72},{1,73},{2,74},{3,75},{4,76},{5,77},{6,78},{7,79},{8,80},{9,... | collective-permute-start | bytes 1572872 | tf_op jit(solution)/shard_map/ppermute | solution.py:30
  36.7 2.4 %scale.1 = bf16[256,128]{1,0:T(8,128)(2,1)} custom-call(f32[1,4,4096]{2,1,0:T(4,128)} %energy.1, s32[1,4,4096]{2,1,0:T(4,128)} %occupied.1, s32[1,256]{1,0:T(1,128)} %first.1, s32[1,256]{1,0:T(1,128)} %second.1, s32[1,256]{1,0:T(1,128)} %kpoint.1, bf16[256,128]{1,0:T(8,128)(2,1)} %block.1), custom_call_target="tpu_custom_call" | custom-call | flops 400000000 | bytes 300000 | tf_op jit(solution)/shard_map/scale/pallas_call | solution.py:72
  39.1 0.0 copy-done
  39.1 1.5 %collective-permute-start = (bf16[256,128]{1,0:T(8,128)(2,1)}, bf16[256,128]{1,0:T(8,128)(2,1)S(1)}, u32[]{:S(2)}, u32[]{:S(2)}) collective-permute-start(bf16[256,128]{1,0:T(8,128)(2,1)} %scale.1), channel_id=1, source_target_pairs={{0,0},{1,1},{2,2},{3,3},{4,4},{5,5},{6,24},{7,25},{8,26},{9,27},{1... | collective-permute-start | bytes 196616 | tf_op jit(solution)/shard_map/ppermute | solution.py:30
  40.5 0.6 pad_add_fusion.1.place
  41.1 0.0 collective-permute-done
  41.1 45.2 %all-gather = bf16[3072,128]{1,0:T(8,128)(2,1)} all-gather(bf16[256,128]{1,0:T(8,128)(2,1)S(1)} %collective-permute-done), channel_id=2, replica_groups={{0,2,4,6,8,10,12,14,16,18,20,22},{1,3,5,7,9,11,13,15,17,19,21,23},{24,2..., dimensions={0}, use_global_device_ids=true | all-gather | bytes 851968 | tf_op jit(solution)/shard_map/all_gather | solution.py:146
  86.4 0.0 collective-permute-done.7.c3
  86.4 0.0 collective-permute-done.6.c2
  86.4 0.0 copy-start.2
  86.4 0.0 collective-permute-done.5.c1
  86.4 0.0 copy-start.3
  86.4 0.8 copy-done.1
  87.2 0.2 copy-done.2
  87.4 0.1 copy-done.3
  87.5 3.5 %give.1 = bf16[4,384,128]{2,1,0:T(8,128)(2,1)} custom-call(s32[2]{0:T(128)} %pad_add_fusion.1.place, bf16[12,256,128]{2,1,0:T(8,128)(2,1)} %bitcast.15, bf16[2,1024,128]{2,1,0:T(8,128)(2,1)} %copy-done, bf16[2,1024,128]{2,1,0:T(8,128)(2,1)} %copy-done.3, bf16[2,1024,128]{2,1,0:T(8,128)(2,1)} %copy-done.2, bf16[2,1024,128]{2,1,0:T(8,128)(2,1)} %copy-done.1), custom_call_target="tpu_custom_call" | custom-call | flops 400000000 | bytes 3000000 | tf_op jit(solution)/shard_map/give/pallas_call | solution.py:95
  91.0 11.3 %collective-permute-start.8 = (bf16[4,384,128]{2,1,0:T(8,128)(2,1)}, bf16[4,384,128]{2,1,0:T(8,128)(2,1)S(1)}, u32[]{:S(2)}, u32[]{:S(2)}) collective-permute-start(bf16[4,384,128]{2,1,0:T(8,128)(2,1)} %give.1), channel_id=1, source_target_pairs={{0,96},{1,97},{2,98},{3,99},{4,100},{5,101},{6,102},{7,103},{8,104... | collective-permute-start | bytes 1179656 | tf_op jit(solution)/shard_map/ppermute | solution.py:30
  102.3 0.6 pad_add_fusion.place
  102.9 3.6 %keep.1 = f32[4,384,128]{2,1,0:T(8,128)} custom-call(s32[2]{0:T(128)} %pad_add_fusion.place, bf16[12,256,128]{2,1,0:T(8,128)(2,1)} %bitcast.16, bf16[2,1024,128]{2,1,0:T(8,128)(2,1)} %copy-done, bf16[2,1024,128]{2,1,0:T(8,128)(2,1)} %copy-done.3, bf16[2,1024,128]{2,1,0:T(8,128)(2,1)} %copy-done.2, bf16[2,1024,128]{2,1,0:T(8,128)(2,1)} %copy-done.1), custom_call_target="tpu_custom_call" | custom-call | flops 400000000 | bytes 3000000 | tf_op jit(solution)/shard_map/keep/pallas_call | solution.py:95
  106.5 0.0 collective-permute-done.8
  106.5 1.2 add_convert_fusion
  107.8 5.6 %collective-permute-start.12 = (bf16[384,128]{1,0:T(8,128)(2,1)S(1)}, bf16[384,128]{1,0:T(8,128)(2,1)S(1)}, u32[]{:S(2)}, u32[]{:S(2)}) collective-permute-start(bf16[384,128]{1,0:T(8,128)(2,1)S(1)} %get-tuple-element.5), channel_id=1, source_target_pairs={{0,72},{1,25},{2,74},{3,27},{4,76},{5,29},{6,78},{7,31},{8,80},{9,... | collective-permute-start | bytes 294920 | tf_op jit(solution)/shard_map/ppermute | solution.py:30
  113.4 3.5 %collective-permute-start.11 = (bf16[384,128]{1,0:T(8,128)(2,1)S(1)}, bf16[384,128]{1,0:T(8,128)(2,1)S(1)}, u32[]{:S(2)}, u32[]{:S(2)}) collective-permute-start(bf16[384,128]{1,0:T(8,128)(2,1)S(1)} %get-tuple-element.6), channel_id=1, source_target_pairs={{0,48},{1,1},{2,50},{3,3},{4,52},{5,5},{6,54},{7,7},{8,56},{9,9},{... | collective-permute-start | bytes 294920 | tf_op jit(solution)/shard_map/ppermute | solution.py:30
  116.9 1.9 %collective-permute-start.10 = (bf16[384,128]{1,0:T(8,128)(2,1)S(1)}, bf16[384,128]{1,0:T(8,128)(2,1)S(1)}, u32[]{:S(2)}, u32[]{:S(2)}) collective-permute-start(bf16[384,128]{1,0:T(8,128)(2,1)S(1)} %get-tuple-element.7), channel_id=1, source_target_pairs={{0,24},{1,73},{2,26},{3,75},{4,28},{5,77},{6,30},{7,79},{8,32},{9,... | collective-permute-start | bytes 294920 | tf_op jit(solution)/shard_map/ppermute | solution.py:30
  118.8 1.9 %collective-permute-start.9 = (bf16[384,128]{1,0:T(8,128)(2,1)S(1)}, bf16[384,128]{1,0:T(8,128)(2,1)S(1)}, u32[]{:S(2)}, u32[]{:S(2)}) collective-permute-start(bf16[384,128]{1,0:T(8,128)(2,1)S(1)} %get-tuple-element.8), channel_id=1, source_target_pairs={{0,0},{1,49},{2,2},{3,51},{4,4},{5,53},{6,6},{7,55},{8,8},{9,57},{... | collective-permute-start | bytes 294920 | tf_op jit(solution)/shard_map/ppermute | solution.py:30
  120.8 0.6 and_select_fusion.order
  121.4 0.0 collective-permute-done.12.f3
  121.4 0.0 collective-permute-done.11.f2
  121.4 0.0 copy-start.5
  121.4 2.7 %collective-permute-done.10.f1 = bf16[384,128]{1,0:T(8,128)(2,1)S(1)} collective-permute-done((bf16[384,128]{1,0:T(8,128)(2,1)S(1)}, bf16[384,128]{1,0:T(8,128)(2,1)S(1)}, u32[]{:S(2)}, u32[]{:S(2)}) %collective-permute-start.10) | collective-permute-done | bytes 98336 | tf_op jit(solution)/shard_map/ppermute | solution.py:30
  124.1 2.5 %collective-permute-done.9.f0 = bf16[384,128]{1,0:T(8,128)(2,1)S(1)} collective-permute-done((bf16[384,128]{1,0:T(8,128)(2,1)S(1)}, bf16[384,128]{1,0:T(8,128)(2,1)S(1)}, u32[]{:S(2)}, u32[]{:S(2)}) %collective-permute-start.9) | collective-permute-done | bytes 98336 | tf_op jit(solution)/shard_map/ppermute | solution.py:30
  126.6 0.0 copy-done.4
  126.6 0.0 copy-done.5
  126.6 0.6 copy-done.7
  127.3 2.0 %assemble.1 = f32[2,3,2,128,128]{4,3,2,1,0:T(8,128)} custom-call(s32[4]{0:T(128)} %and_select_fusion.order, bf16[384,128]{1,0:T(8,128)(2,1)} %copy-done.7, bf16[384,128]{1,0:T(8,128)(2,1)} %copy-done.6, bf16[384,128]{1,0:T(8,128)(2,1)} %copy-done.5, bf16[384,128]{1,0:T(8,128)(2,1)} %copy-done.4), custom_call_target="tpu_custom_call" | custom-call | tf_op jit(solution)/shard_map/assemble/pallas_call | solution.py:118
  (9 shorter events, 0.1 us)
Async XLA Ops:
  0.0 15.3 %collective-permute-start.2 = (bf16[256,128]{1,0:T(8,128)(2,1)}, bf16[256,128]{1,0:T(8,128)(2,1)S(1)}, u32[]{:S(2)}, u32[]{:S(2)}) collective-permute-start(bf16[256,128]{1,0:T(8,128)(2,1)} %block.1), channel_id=1, source_target_pairs={{0,384},{1,385},{2,386},{3,387},{4,388},{5,389},{6,390},{7,391},{8... | collective-permute-start | bytes 196616 | tf_op jit(solution)/shard_map/ppermute | solution.py:30
  8.3 7.1 %collective-permute-start.1 = (bf16[256,128]{1,0:T(8,128)(2,1)}, bf16[256,128]{1,0:T(8,128)(2,1)S(1)}, u32[]{:S(2)}, u32[]{:S(2)}) collective-permute-start(bf16[256,128]{1,0:T(8,128)(2,1)} %block.1), channel_id=1, source_target_pairs={{0,576},{1,577},{2,578},{3,579},{4,580},{5,581},{6,582},{7,583},{8... | collective-permute-start | bytes 196616 | tf_op jit(solution)/shard_map/ppermute | solution.py:30
  10.2 7.5 %collective-permute-start.3 = (bf16[256,128]{1,0:T(8,128)(2,1)}, bf16[256,128]{1,0:T(8,128)(2,1)S(1)}, u32[]{:S(2)}, u32[]{:S(2)}) collective-permute-start(bf16[256,128]{1,0:T(8,128)(2,1)} %block.1), channel_id=1, source_target_pairs={{0,192},{1,193},{2,194},{3,195},{4,196},{5,197},{6,198},{7,199},{8... | collective-permute-start | bytes 196616 | tf_op jit(solution)/shard_map/ppermute | solution.py:30
  17.8 7.7 %collective-permute-start.4 = (bf16[1024,128]{1,0:T(8,128)(2,1)S(1)}, bf16[1024,128]{1,0:T(8,128)(2,1)S(1)}, u32[]{:S(2)}, u32[]{:S(2)}) collective-permute-start(bf16[1024,128]{1,0:T(8,128)(2,1)S(1)} %constant_dynamic-update-slice_fusion), channel_id=1, source_target_pairs={{0,1},{1,0},{2,3},{3,2},{4,5},{5,4},{6,7},{7,6},{8,9},{9,8},{10,11... | collective-permute-start | bytes 786440 | tf_op jit(solution)/shard_map/ppermute | solution.py:30
  25.5 13.5 %copy-start = (bf16[2,1024,128]{2,1,0:T(8,128)(2,1)}, bf16[2,1024,128]{2,1,0:T(8,128)(2,1)S(1)}, u32[]{:S(2)}) copy-start(bf16[2,1024,128]{2,1,0:T(8,128)(2,1)S(1)} %pad_maximum_fusion.c0) | copy-start | bytes 1572868
  25.5 60.9 %collective-permute-start.7 = (bf16[2,1024,128]{2,1,0:T(8,128)(2,1)S(1)}, bf16[2,1024,128]{2,1,0:T(8,128)(2,1)S(1)}, u32[]{:S(2)}, u32[]{:S(2)}) collective-permute-start(bf16[2,1024,128]{2,1,0:T(8,128)(2,1)S(1)} %pad_maximum_fusion.c0), channel_id=1, source_target_pairs={{0,24},{1,25},{2,26},{3,27},{4,28},{5,29},{6,30},{7,31},{8,32},{9,... | collective-permute-start | bytes 1572872 | tf_op jit(solution)/shard_map/ppermute | solution.py:30
  29.3 57.1 %collective-permute-start.6 = (bf16[2,1024,128]{2,1,0:T(8,128)(2,1)S(1)}, bf16[2,1024,128]{2,1,0:T(8,128)(2,1)S(1)}, u32[]{:S(2)}, u32[]{:S(2)}) collective-permute-start(bf16[2,1024,128]{2,1,0:T(8,128)(2,1)S(1)} %pad_maximum_fusion.c0), channel_id=1, source_target_pairs={{0,48},{1,49},{2,50},{3,51},{4,52},{5,53},{6,54},{7,55},{8,56},{9,... | collective-permute-start | bytes 1572872 | tf_op jit(solution)/shard_map/ppermute | solution.py:30
  33.6 52.8 %collective-permute-start.5 = (bf16[2,1024,128]{2,1,0:T(8,128)(2,1)S(1)}, bf16[2,1024,128]{2,1,0:T(8,128)(2,1)S(1)}, u32[]{:S(2)}, u32[]{:S(2)}) collective-permute-start(bf16[2,1024,128]{2,1,0:T(8,128)(2,1)S(1)} %pad_maximum_fusion.c0), channel_id=1, source_target_pairs={{0,72},{1,73},{2,74},{3,75},{4,76},{5,77},{6,78},{7,79},{8,80},{9,... | collective-permute-start | bytes 1572872 | tf_op jit(solution)/shard_map/ppermute | solution.py:30
  39.1 2.1 %collective-permute-start = (bf16[256,128]{1,0:T(8,128)(2,1)}, bf16[256,128]{1,0:T(8,128)(2,1)S(1)}, u32[]{:S(2)}, u32[]{:S(2)}) collective-permute-start(bf16[256,128]{1,0:T(8,128)(2,1)} %scale.1), channel_id=1, source_target_pairs={{0,0},{1,1},{2,2},{3,3},{4,4},{5,5},{6,24},{7,25},{8,26},{9,27},{1... | collective-permute-start | bytes 196616 | tf_op jit(solution)/shard_map/ppermute | solution.py:30
  86.4 0.8 copy-start.1
  86.4 1.0 copy-start.2
  86.4 1.1 copy-start.3
  91.0 15.6 %collective-permute-start.8 = (bf16[4,384,128]{2,1,0:T(8,128)(2,1)}, bf16[4,384,128]{2,1,0:T(8,128)(2,1)S(1)}, u32[]{:S(2)}, u32[]{:S(2)}) collective-permute-start(bf16[4,384,128]{2,1,0:T(8,128)(2,1)} %give.1), channel_id=1, source_target_pairs={{0,96},{1,97},{2,98},{3,99},{4,100},{5,101},{6,102},{7,103},{8,104... | collective-permute-start | bytes 1179656 | tf_op jit(solution)/shard_map/ppermute | solution.py:30
  107.8 13.6 %collective-permute-start.12 = (bf16[384,128]{1,0:T(8,128)(2,1)S(1)}, bf16[384,128]{1,0:T(8,128)(2,1)S(1)}, u32[]{:S(2)}, u32[]{:S(2)}) collective-permute-start(bf16[384,128]{1,0:T(8,128)(2,1)S(1)} %get-tuple-element.5), channel_id=1, source_target_pairs={{0,72},{1,25},{2,74},{3,27},{4,76},{5,29},{6,78},{7,31},{8,80},{9,... | collective-permute-start | bytes 294920 | tf_op jit(solution)/shard_map/ppermute | solution.py:30
  113.4 7.9 %collective-permute-start.11 = (bf16[384,128]{1,0:T(8,128)(2,1)S(1)}, bf16[384,128]{1,0:T(8,128)(2,1)S(1)}, u32[]{:S(2)}, u32[]{:S(2)}) collective-permute-start(bf16[384,128]{1,0:T(8,128)(2,1)S(1)} %get-tuple-element.6), channel_id=1, source_target_pairs={{0,48},{1,1},{2,50},{3,3},{4,52},{5,5},{6,54},{7,7},{8,56},{9,9},{... | collective-permute-start | bytes 294920 | tf_op jit(solution)/shard_map/ppermute | solution.py:30
  116.9 7.1 %collective-permute-start.10 = (bf16[384,128]{1,0:T(8,128)(2,1)S(1)}, bf16[384,128]{1,0:T(8,128)(2,1)S(1)}, u32[]{:S(2)}, u32[]{:S(2)}) collective-permute-start(bf16[384,128]{1,0:T(8,128)(2,1)S(1)} %get-tuple-element.7), channel_id=1, source_target_pairs={{0,24},{1,73},{2,26},{3,75},{4,28},{5,77},{6,30},{7,79},{8,32},{9,... | collective-permute-start | bytes 294920 | tf_op jit(solution)/shard_map/ppermute | solution.py:30
  118.8 7.8 %collective-permute-start.9 = (bf16[384,128]{1,0:T(8,128)(2,1)S(1)}, bf16[384,128]{1,0:T(8,128)(2,1)S(1)}, u32[]{:S(2)}, u32[]{:S(2)}) collective-permute-start(bf16[384,128]{1,0:T(8,128)(2,1)S(1)} %get-tuple-element.8), channel_id=1, source_target_pairs={{0,0},{1,49},{2,2},{3,51},{4,4},{5,53},{6,6},{7,55},{8,8},{9,57},{... | collective-permute-start | bytes 294920 | tf_op jit(solution)/shard_map/ppermute | solution.py:30
  121.4 5.2 %copy-start.4 = (bf16[384,128]{1,0:T(8,128)(2,1)}, bf16[384,128]{1,0:T(8,128)(2,1)S(1)}, u32[]{:S(2)}) copy-start(bf16[384,128]{1,0:T(8,128)(2,1)S(1)} %collective-permute-done.12.f3) | copy-start | bytes 294916
  121.4 5.2 %copy-start.5 = (bf16[384,128]{1,0:T(8,128)(2,1)}, bf16[384,128]{1,0:T(8,128)(2,1)S(1)}, u32[]{:S(2)}) copy-start(bf16[384,128]{1,0:T(8,128)(2,1)S(1)} %collective-permute-done.11.f2) | copy-start | bytes 294916
  124.1 2.6 %copy-start.6 = (bf16[384,128]{1,0:T(8,128)(2,1)}, bf16[384,128]{1,0:T(8,128)(2,1)S(1)}, u32[]{:S(2)}) copy-start(bf16[384,128]{1,0:T(8,128)(2,1)S(1)} %collective-permute-done.10.f1) | copy-start | bytes 294916
  126.6 0.6 copy-start.7

commit v2 on v1

--- a/solution.py
+++ b/solution.py
@@ -1,3 +1,5 @@
+import functools
+
 import jax
 import jax.numpy as jnp
 from jax import lax
@@ -5,10 +7,12 @@
 from jax.experimental.pallas import tpu as pltpu
 from jax.sharding import PartitionSpec as P
 
+
 H, K, X, Z, L = 4, 2, 4, 12, 2
 COLS = X * Z * L
 PAIRS, WIDTH = 256, 128
 AXES = ("pool", "col")
+SHIFT = (2, 1, 0, 3)
 
 
 def at(h, k, x, z, l):
@@ -78,89 +82,116 @@
     )(energy, occupied, first, second, kpoint, block)
 
 
-def product_kernel(place, rows, c0, c1, c2, c3, out):
-    pieces = [jnp.concatenate([rows[3 * s + j] for s in range(H)], axis=0) for j in range(3)]
-    left = jnp.concatenate(pieces, axis=1)
-    right = jnp.concatenate([c[0] for c in (c0, c1, c2, c3)], axis=1)
+def product_kernel(side, place, rows, c0, c1, c2, c3, out):
+    which = place[side]
+    left = jnp.concatenate(
+        [
+            jnp.concatenate([rows[3 * ((place[2] + SHIFT[s]) % H) + j] for s in range(H)], axis=0)
+            for j in range(3)
+        ],
+        axis=1,
+    )
+    right = jnp.concatenate([c[which] for c in (c0, c1, c2, c3)], axis=1)
     found = lax.dot_general(
         left, right, (((0,), (0,)), ((), ())), preferred_element_type=jnp.float32
     )
     for i in range(X):
-        out[(i + place[1]) % X] = found[:, i * WIDTH : (i + 1) * WIDTH].astype(out.dtype)
-
-
-def product(side, turn, rows, columns, dtype, name):
-    depth = columns[0].shape[1]
-    place = jnp.stack([side, turn]).astype(jnp.int32)
-    return pl.pallas_call(
-        product_kernel,
+        out[i] = found[:, i * WIDTH : (i + 1) * WIDTH].astype(out.dtype)
+
+
+SMEM = pl.BlockSpec(memory_space=pltpu.SMEM)
+VMEM = pl.BlockSpec(memory_space=pltpu.VMEM)
+
+
+def product(side, place, rows, columns, dtype):
+    return pl.pallas_call(
+        functools.partial(product_kernel, side),
         out_shape=jax.ShapeDtypeStruct((X, 3 * WIDTH, WIDTH), dtype),
-        grid_spec=pltpu.PrefetchScalarGridSpec(
-            num_scalar_prefetch=1,
-            grid=(1,),
-            in_specs=[pl.BlockSpec(rows.shape, lambda i, p: (0, 0, 0))]
-            + [pl.BlockSpec((1, depth, WIDTH), lambda i, p: (p[0], 0, 0))] * X,
-            out_specs=pl.BlockSpec((X, 3 * WIDTH, WIDTH), lambda i, p: (0, 0, 0)),
-        ),
+        in_specs=[SMEM] + [VMEM] * (1 + X),
+        out_specs=VMEM,
+        compiler_params=pltpu.CompilerParams(vmem_limit_bytes=16 * 2**20),
         cost_estimate=pl.CostEstimate(flops=4 * 10**8, bytes_accessed=3 * 10**6, transcendentals=0),
-        name=name,
     )(place, rows, *columns)
 
 
-def assemble_kernel(order, f0, f1, f2, f3, out):
+def total_kernel(place, keep, taken, *outs):
+    for r, out in enumerate(outs):
+        i = (r + place[3]) % X
+        out[...] = (keep[i] + taken[i].astype(jnp.float32)).astype(out.dtype)
+
+
+def add_partner(place, keep, taken):
+    return pl.pallas_call(
+        total_kernel,
+        out_shape=[jax.ShapeDtypeStruct(keep.shape[1:], jnp.bfloat16)] * X,
+        in_specs=[SMEM, VMEM, VMEM],
+        out_specs=[VMEM] * X,
+        compiler_params=pltpu.CompilerParams(vmem_limit_bytes=8 * 2**20),
+        name="total",
+    )(place, keep, taken)
+
+
+def assemble_kernel(place, f0, f1, f2, f3, out):
     for i, piece in enumerate((f0, f1, f2, f3)):
-        t = order[i]
+        t = place[4 + i]
         for j in range(3):
             out[t % 2, j, t // 2] = piece[j * WIDTH : (j + 1) * WIDTH, :].astype(jnp.float32)
 
 
-def assemble(order, pieces):
+def assemble(place, pieces):
     return pl.pallas_call(
         assemble_kernel,
         out_shape=jax.ShapeDtypeStruct((2, 3, 2, WIDTH, WIDTH), jnp.float32),
-        in_specs=[pl.BlockSpec(memory_space=pltpu.SMEM)] + [pl.BlockSpec(memory_space=pltpu.VMEM)] * 4,
-        out_specs=pl.BlockSpec(memory_space=pltpu.VMEM),
+        in_specs=[SMEM] + [VMEM] * 4,
+        out_specs=VMEM,
+        compiler_params=pltpu.CompilerParams(vmem_limit_bytes=8 * 2**20),
         name="assemble",
-    )(order, *pieces)
-
-
-def per_device(pair_matrix, band_energy, occupation, pair_first, pair_second, pair_kpoint):
+    )(place, *pieces)
+
+
+def blocks(pair_matrix, band_energy, occupation, pair_first, pair_second, pair_kpoint):
     pool, col = lax.axis_index("pool"), lax.axis_index("col")
     k, x, l = pool % K, col // (Z * L), col % L
-
-    around = [
-        move(pair_matrix, lambda h, k, x, z, l, s=s: (h - s, k, x, z, l)) for s in range(1, H)
-    ]
+    place = jnp.stack(
+        [1 - k, k, x, 2 * l] + [(x - 2 * k - r) % X for r in range(X)]
+    ).astype(jnp.int32)
+
+    around = []
+    for s in range(1, H):
+        around.append(move(pair_matrix, lambda h, k, x, z, l, s=s: (h - s, k, x, z, l)))
     scaled = scaled_block(
         band_energy, occupation, pair_first, pair_second, pair_kpoint, pair_matrix
     )
     sent = move(
-        scaled, lambda h, k, x, z, l: (x, k, z // 3, 3 * ((h - x) % H) + z % 3, l)
+        scaled,
+        lambda h, k, x, z, l: (x, k, z // 3, z + 3 * SHIFT[(h - x) % H], l),
     )
     own = jnp.concatenate([pair_matrix] + around, axis=0)
     other = move(own, lambda h, k, x, z, l: (h, k, x, z, 1 - l))
     both = jnp.stack([own, other])
-    columns = [both] + [
-        move(both, lambda h, k, x, z, l, s=s: (h, k, x - s, z, l)) for s in range(1, X)
-    ]
+    columns = [both]
+    for s in range(1, X):
+        columns.append(move(both, lambda h, k, x, z, l, s=s: (h, k, x - s, z, l)))
     rows = lax.all_gather(sent, "col", axis=0, axis_index_groups=Z_GROUPS)
 
-    turn = 2 * l
-    give = product(1 - k, turn, rows, columns, jnp.bfloat16, "give")
+    give = product(0, place, rows, columns, jnp.bfloat16)
     taken = move(give, lambda h, k, x, z, l: (h, 1 - k, x, z, l))
-    keep = product(k, turn, rows, columns, jnp.float32, "keep")
-    total = (keep + taken.astype(jnp.float32)).astype(jnp.bfloat16)
-    home = [
-        move(total[r], lambda h, k, x, z, l, r=r: (h, x // 2, x + r + 2 * l, z, l ^ k))
-        for r in range(X)
-    ]
-    order = (x - 2 * k - jnp.arange(X, dtype=jnp.int32)) % X
-    return assemble(order.astype(jnp.int32), home).reshape(-1, WIDTH)
+    keep = product(1, place, rows, columns, jnp.float32)
+    total = add_partner(place, keep, taken)
+    home = []
+    for r in range(X):
+        home.append(
+            move(
+                total[r],
+                lambda h, k, x, z, l, r=r: (h, x // 2, x + r + 2 * l, z, l ^ k),
+            )
+        )
+    return assemble(place, home).reshape(-1, WIDTH)
 
 
 def solution(mesh):
     return jax.shard_map(
-        per_device,
+        blocks,
         mesh=mesh,
         in_specs=(
             P("pool", "col"),

time: 130 us -> 117 us (0.900)
  blocking collectives: 45.2 us -> 27.5 us
  starting transfers between devices: 55.1 us -> 68.2 us
  Pallas kernels: 11.4 us -> 6.74 us
  other arithmetic: 3.02 us -> 0.05 us
  local copies, waits for them, and re-layouts: 2.68 us -> 0.98 us
  waiting for transfers between devices: 11.6 us -> 12.9 us
    all_gather x1, blocking collectives: 45.2 us -> 27.5 us  [blocks(): rows = lax.all_gather(sent, 'col', axis=0, axis_index_groups=Z_GROUPS)]
    ppermute x13, starting transfers between devices: 55.1 us -> 68.2 us  [move(): return lax.ppermute(value, AXES, table(f))]
    pallas_call x2 -> x3, Pallas kernels: 7.06 us -> 2.91 us  [the longest x2 2.29 us: product(): pl.pallas_call(functools.partial(product_kernel, side), out_shape=jax.Sha...]
    unnamed x19 -> x3, local copies, waits for them, and re-layouts: 2.64 us -> 0.88 us
  transfers between devices with their start and end apart: 13 -> 13, of which waited for: 4 -> 6; matrix products, arithmetic and copies ran while one was open for 2% -> 1% of each run, Pallas kernels for 5% -> 3%
where the time goes in v2:
time: 117 us
  starting transfers between devices  68.2 us (58%)
  blocking collectives  27.5 us (24%)
  waiting for transfers between devices  12.9 us (11%)
  Pallas kernels  6.74 us (6%)
    ppermute x13, starting transfers between devices, move(): return lax.ppermute(value, AXES, table(f))  68.2 us
    all_gather x1, blocking collectives, blocks(): rows = lax.all_gather(sent, 'col', axis=0, axis_index_groups=Z_GROUPS)  27.5 us
    ppermute x13, waiting for transfers between devices, move(): return lax.ppermute(value, AXES, table(f))  12.9 us
    pallas_call x1, Pallas kernels, scaled_block(): pl.pallas_call(scale_kernel, out_shape=jax.ShapeDtypeStruct(block.shape,...  2.36 us
  transfers between devices with their start and end apart: 13, of which 6 were waited for; matrix products, arithmetic and copies ran while one was open for 1% of the time, Pallas kernels for 3%

profile of v2, /device:TPU:1, one launch (start us, length us, event | category | flops | bytes accessed | tf_op | source)
XLA Modules:
  0.0 116.7 jit_solution(10200853002411831885)
XLA Ops:
  0.0 8.3 %collective-permute-start.2 = (bf16[256,128]{1,0:T(8,128)(2,1)}, bf16[256,128]{1,0:T(8,128)(2,1)S(1)}, u32[]{:S(2)}, u32[]{:S(2)}) collective-permute-start(bf16[256,128]{1,0:T(8,128)(2,1)} %block.1), channel_id=1, source_target_pairs={{0,384},{1,385},{2,386},{3,387},{4,388},{5,389},{6,390},{7,391},{8... | collective-permute-start | bytes 196616 | tf_op jit(solution)/shard_map/ppermute | solution.py:34
  8.3 2.0 %collective-permute-start.1 = (bf16[256,128]{1,0:T(8,128)(2,1)}, bf16[256,128]{1,0:T(8,128)(2,1)S(1)}, u32[]{:S(2)}, u32[]{:S(2)}) collective-permute-start(bf16[256,128]{1,0:T(8,128)(2,1)} %block.1), channel_id=1, source_target_pairs={{0,576},{1,577},{2,578},{3,579},{4,580},{5,581},{6,582},{7,583},{8... | collective-permute-start | bytes 196616 | tf_op jit(solution)/shard_map/ppermute | solution.py:34
  10.2 4.2 %collective-permute-start.3 = (bf16[256,128]{1,0:T(8,128)(2,1)}, bf16[256,128]{1,0:T(8,128)(2,1)S(1)}, u32[]{:S(2)}, u32[]{:S(2)}) collective-permute-start(bf16[256,128]{1,0:T(8,128)(2,1)} %block.1), channel_id=1, source_target_pairs={{0,192},{1,193},{2,194},{3,195},{4,196},{5,197},{6,198},{7,199},{8... | collective-permute-start | bytes 196616 | tf_op jit(solution)/shard_map/ppermute | solution.py:34
  14.5 0.9 constant_dynamic-update-slice_fusion.3
  15.3 0.0 collective-permute-done.1
  15.3 0.0 collective-permute-done.2
  15.4 2.4 %collective-permute-done.3 = bf16[256,128]{1,0:T(8,128)(2,1)S(1)} collective-permute-done((bf16[256,128]{1,0:T(8,128)(2,1)}, bf16[256,128]{1,0:T(8,128)(2,1)S(1)}, u32[]{:S(2)}, u32[]{:S(2)}) %collective-permute-start.3) | collective-permute-done | bytes 65568 | tf_op jit(solution)/shard_map/ppermute | solution.py:34
  17.8 3.7 %collective-permute-start.4 = (bf16[1024,128]{1,0:T(8,128)(2,1)S(1)}, bf16[1024,128]{1,0:T(8,128)(2,1)S(1)}, u32[]{:S(2)}, u32[]{:S(2)}) collective-permute-start(bf16[1024,128]{1,0:T(8,128)(2,1)S(1)} %constant_dynamic-update-slice_fusion), channel_id=1, source_target_pairs={{0,1},{1,0},{2,3},{3,2},{4,5},{5,4},{6,7},{7,6},{8,9},{9,8},{10,11... | collective-permute-start | bytes 786440 | tf_op jit(solution)/shard_map/ppermute | solution.py:34
  21.5 4.0 %collective-permute-done.4 = bf16[1024,128]{1,0:T(8,128)(2,1)S(1)} collective-permute-done((bf16[1024,128]{1,0:T(8,128)(2,1)S(1)}, bf16[1024,128]{1,0:T(8,128)(2,1)S(1)}, u32[]{:S(2)}, u32[]{:S(2)}) %collective-permute-start.4) | collective-permute-done | bytes 262176 | tf_op jit(solution)/shard_map/ppermute | solution.py:34
  25.5 0.1 pad_maximum_fusion.c0
  25.5 3.7 %collective-permute-start.7 = (bf16[2,1024,128]{2,1,0:T(8,128)(2,1)S(1)}, bf16[2,1024,128]{2,1,0:T(8,128)(2,1)S(1)}, u32[]{:S(2)}, u32[]{:S(2)}) collective-permute-start(bf16[2,1024,128]{2,1,0:T(8,128)(2,1)S(1)} %pad_maximum_fusion.c0), channel_id=1, source_target_pairs={{0,24},{1,25},{2,26},{3,27},{4,28},{5,29},{6,30},{7,31},{8,32},{9,... | collective-permute-start | bytes 1572872 | tf_op jit(solution)/shard_map/ppermute | solution.py:34
  29.3 4.4 %collective-permute-start.6 = (bf16[2,1024,128]{2,1,0:T(8,128)(2,1)S(1)}, bf16[2,1024,128]{2,1,0:T(8,128)(2,1)S(1)}, u32[]{:S(2)}, u32[]{:S(2)}) collective-permute-start(bf16[2,1024,128]{2,1,0:T(8,128)(2,1)S(1)} %pad_maximum_fusion.c0), channel_id=1, source_target_pairs={{0,48},{1,49},{2,50},{3,51},{4,52},{5,53},{6,54},{7,55},{8,56},{9,... | collective-permute-start | bytes 1572872 | tf_op jit(solution)/shard_map/ppermute | solution.py:34
  33.6 3.1 %collective-permute-start.5 = (bf16[2,1024,128]{2,1,0:T(8,128)(2,1)S(1)}, bf16[2,1024,128]{2,1,0:T(8,128)(2,1)S(1)}, u32[]{:S(2)}, u32[]{:S(2)}) collective-permute-start(bf16[2,1024,128]{2,1,0:T(8,128)(2,1)S(1)} %pad_maximum_fusion.c0), channel_id=1, source_target_pairs={{0,72},{1,73},{2,74},{3,75},{4,76},{5,77},{6,78},{7,79},{8,80},{9,... | collective-permute-start | bytes 1572872 | tf_op jit(solution)/shard_map/ppermute | solution.py:34
  36.7 2.4 %scale.1 = bf16[256,128]{1,0:T(8,128)(2,1)} custom-call(f32[1,4,4096]{2,1,0:T(4,128)} %energy.1, s32[1,4,4096]{2,1,0:T(4,128)} %occupied.1, s32[1,256]{1,0:T(1,128)} %first.1, s32[1,256]{1,0:T(1,128)} %second.1, s32[1,256]{1,0:T(1,128)} %kpoint.1, bf16[256,128]{1,0:T(8,128)(2,1)} %block.1), custom_call_target="tpu_custom_call" | custom-call | flops 400000000 | bytes 300000 | tf_op jit(solution)/shard_map/scale/pallas_call | solution.py:76
  39.1 14.8 %collective-permute-start = (bf16[256,128]{1,0:T(8,128)(2,1)}, bf16[256,128]{1,0:T(8,128)(2,1)S(1)}, u32[]{:S(2)}, u32[]{:S(2)}) collective-permute-start(bf16[256,128]{1,0:T(8,128)(2,1)} %scale.1), channel_id=1, source_target_pairs={{0,12},{1,13},{2,14},{3,15},{4,16},{5,17},{6,42},{7,43},{8,44},{9,... | collective-permute-start | bytes 196616 | tf_op jit(solution)/shard_map/ppermute | solution.py:34
  54.0 0.1 stack.44.place
  54.1 1.4 %collective-permute-done = bf16[256,128]{1,0:T(8,128)(2,1)S(1)} collective-permute-done((bf16[256,128]{1,0:T(8,128)(2,1)}, bf16[256,128]{1,0:T(8,128)(2,1)S(1)}, u32[]{:S(2)}, u32[]{:S(2)}) %collective-permute-start) | collective-permute-done | bytes 65568 | tf_op jit(solution)/shard_map/ppermute | solution.py:34
  55.5 27.5 %all-gather = bf16[3072,128]{1,0:T(8,128)(2,1)S(1)} all-gather(bf16[256,128]{1,0:T(8,128)(2,1)S(1)} %collective-permute-done), channel_id=2, replica_groups={{0,2,4,6,8,10,12,14,16,18,20,22},{1,3,5,7,9,11,13,15,17,19,21,23},{24,2..., dimensions={0}, use_global_device_ids=true | all-gather | bytes 851968 | tf_op jit(solution)/shard_map/all_gather | solution.py:175
  83.0 0.0 collective-permute-done.7.c3
  83.0 0.0 collective-permute-done.6.c2
  83.0 0.0 collective-permute-done.5.c1
  83.0 1.1 shard_map.65
  84.2 11.5 %collective-permute-start.8 = (bf16[4,384,128]{2,1,0:T(8,128)(2,1)S(1)}, bf16[4,384,128]{2,1,0:T(8,128)(2,1)S(1)}, u32[]{:S(2)}, u32[]{:S(2)}) collective-permute-start(bf16[4,384,128]{2,1,0:T(8,128)(2,1)S(1)} %shard_map.65), channel_id=1, source_target_pairs={{0,96},{1,97},{2,98},{3,99},{4,100},{5,101},{6,102},{7,103},{8,104... | collective-permute-start | bytes 1179656 | tf_op jit(solution)/shard_map/ppermute | solution.py:34
  95.7 1.1 shard_map.64.keep
  96.8 0.2 collective-permute-done.8.taken
  97.0 0.6 total.1
  97.6 3.6 %collective-permute-start.9 = (bf16[384,128]{1,0:T(8,128)(2,1)S(1)}, bf16[384,128]{1,0:T(8,128)(2,1)S(1)}, u32[]{:S(2)}, u32[]{:S(2)}) collective-permute-start(bf16[384,128]{1,0:T(8,128)(2,1)S(1)} %get-tuple-element.9), channel_id=1, source_target_pairs={{0,0},{1,49},{2,2},{3,51},{4,4},{5,53},{6,6},{7,55},{8,8},{9,57},{... | collective-permute-start | bytes 294920 | tf_op jit(solution)/shard_map/ppermute | solution.py:34
  101.2 2.8 %collective-permute-start.10 = (bf16[384,128]{1,0:T(8,128)(2,1)S(1)}, bf16[384,128]{1,0:T(8,128)(2,1)S(1)}, u32[]{:S(2)}, u32[]{:S(2)}) collective-permute-start(bf16[384,128]{1,0:T(8,128)(2,1)S(1)} %get-tuple-element.10), channel_id=1, source_target_pairs={{0,24},{1,73},{2,26},{3,75},{4,28},{5,77},{6,30},{7,79},{8,32},{9,... | collective-permute-start | bytes 294920 | tf_op jit(solution)/shard_map/ppermute | solution.py:34
  103.9 3.8 %collective-permute-start.11 = (bf16[384,128]{1,0:T(8,128)(2,1)S(1)}, bf16[384,128]{1,0:T(8,128)(2,1)S(1)}, u32[]{:S(2)}, u32[]{:S(2)}) collective-permute-start(bf16[384,128]{1,0:T(8,128)(2,1)S(1)} %get-tuple-element.11), channel_id=1, source_target_pairs={{0,48},{1,1},{2,50},{3,3},{4,52},{5,5},{6,54},{7,7},{8,56},{9,9},{... | collective-permute-start | bytes 294920 | tf_op jit(solution)/shard_map/ppermute | solution.py:34
  107.7 2.5 %collective-permute-start.12 = (bf16[384,128]{1,0:T(8,128)(2,1)S(1)}, bf16[384,128]{1,0:T(8,128)(2,1)S(1)}, u32[]{:S(2)}, u32[]{:S(2)}) collective-permute-start(bf16[384,128]{1,0:T(8,128)(2,1)S(1)} %get-tuple-element.12), channel_id=1, source_target_pairs={{0,72},{1,25},{2,74},{3,27},{4,76},{5,29},{6,78},{7,31},{8,80},{9,... | collective-permute-start | bytes 294920 | tf_op jit(solution)/shard_map/ppermute | solution.py:34
  110.2 0.0 collective-permute-done.9.f0
  110.3 0.0 collective-permute-done.10.f1
  110.3 1.1 collective-permute-done.11.f2
  111.4 3.8 %collective-permute-done.12.f3 = bf16[384,128]{1,0:T(8,128)(2,1)S(1)} collective-permute-done((bf16[384,128]{1,0:T(8,128)(2,1)S(1)}, bf16[384,128]{1,0:T(8,128)(2,1)S(1)}, u32[]{:S(2)}, u32[]{:S(2)}) %collective-permute-start.12) | collective-permute-done | bytes 98336 | tf_op jit(solution)/shard_map/ppermute | solution.py:34
  115.2 1.5 %assemble.1 = f32[2,3,2,128,128]{4,3,2,1,0:T(8,128)} custom-call(s32[8]{0:T(128)S(1)} %stack.44.place, bf16[384,128]{1,0:T(8,128)(2,1)S(1)} %collective-permute-done.9.f0, bf16[384,128]{1,0:T(8,128)(2,1)S(1)} %collective-permute-done.10.f1, bf16[384,128]{1,0:T(8,128)(2,1)S(1)} %collective-permute-done.11.f2, bf16[384,128]{1,0:T(8,128)(2,1)S(1)} %collective-permute-done.12.f3), custom_call_target="tpu_custom_call" | custom-call | tf_op jit(solution)/shard_map/assemble/pallas_call | solution.py:142
  (3 shorter events, 0.0 us)
Async XLA Ops:
  0.0 15.3 %collective-permute-start.2 = (bf16[256,128]{1,0:T(8,128)(2,1)}, bf16[256,128]{1,0:T(8,128)(2,1)S(1)}, u32[]{:S(2)}, u32[]{:S(2)}) collective-permute-start(bf16[256,128]{1,0:T(8,128)(2,1)} %block.1), channel_id=1, source_target_pairs={{0,384},{1,385},{2,386},{3,387},{4,388},{5,389},{6,390},{7,391},{8... | collective-permute-start | bytes 196616 | tf_op jit(solution)/shard_map/ppermute | solution.py:34
  8.3 7.1 %collective-permute-start.1 = (bf16[256,128]{1,0:T(8,128)(2,1)}, bf16[256,128]{1,0:T(8,128)(2,1)S(1)}, u32[]{:S(2)}, u32[]{:S(2)}) collective-permute-start(bf16[256,128]{1,0:T(8,128)(2,1)} %block.1), channel_id=1, source_target_pairs={{0,576},{1,577},{2,578},{3,579},{4,580},{5,581},{6,582},{7,583},{8... | collective-permute-start | bytes 196616 | tf_op jit(solution)/shard_map/ppermute | solution.py:34
  10.2 7.5 %collective-permute-start.3 = (bf16[256,128]{1,0:T(8,128)(2,1)}, bf16[256,128]{1,0:T(8,128)(2,1)S(1)}, u32[]{:S(2)}, u32[]{:S(2)}) collective-permute-start(bf16[256,128]{1,0:T(8,128)(2,1)} %block.1), channel_id=1, source_target_pairs={{0,192},{1,193},{2,194},{3,195},{4,196},{5,197},{6,198},{7,199},{8... | collective-permute-start | bytes 196616 | tf_op jit(solution)/shard_map/ppermute | solution.py:34
  17.8 7.7 %collective-permute-start.4 = (bf16[1024,128]{1,0:T(8,128)(2,1)S(1)}, bf16[1024,128]{1,0:T(8,128)(2,1)S(1)}, u32[]{:S(2)}, u32[]{:S(2)}) collective-permute-start(bf16[1024,128]{1,0:T(8,128)(2,1)S(1)} %constant_dynamic-update-slice_fusion), channel_id=1, source_target_pairs={{0,1},{1,0},{2,3},{3,2},{4,5},{5,4},{6,7},{7,6},{8,9},{9,8},{10,11... | collective-permute-start | bytes 786440 | tf_op jit(solution)/shard_map/ppermute | solution.py:34
  25.5 57.5 %collective-permute-start.7 = (bf16[2,1024,128]{2,1,0:T(8,128)(2,1)S(1)}, bf16[2,1024,128]{2,1,0:T(8,128)(2,1)S(1)}, u32[]{:S(2)}, u32[]{:S(2)}) collective-permute-start(bf16[2,1024,128]{2,1,0:T(8,128)(2,1)S(1)} %pad_maximum_fusion.c0), channel_id=1, source_target_pairs={{0,24},{1,25},{2,26},{3,27},{4,28},{5,29},{6,30},{7,31},{8,32},{9,... | collective-permute-start | bytes 1572872 | tf_op jit(solution)/shard_map/ppermute | solution.py:34
  29.3 53.8 %collective-permute-start.6 = (bf16[2,1024,128]{2,1,0:T(8,128)(2,1)S(1)}, bf16[2,1024,128]{2,1,0:T(8,128)(2,1)S(1)}, u32[]{:S(2)}, u32[]{:S(2)}) collective-permute-start(bf16[2,1024,128]{2,1,0:T(8,128)(2,1)S(1)} %pad_maximum_fusion.c0), channel_id=1, source_target_pairs={{0,48},{1,49},{2,50},{3,51},{4,52},{5,53},{6,54},{7,55},{8,56},{9,... | collective-permute-start | bytes 1572872 | tf_op jit(solution)/shard_map/ppermute | solution.py:34
  33.6 49.4 %collective-permute-start.5 = (bf16[2,1024,128]{2,1,0:T(8,128)(2,1)S(1)}, bf16[2,1024,128]{2,1,0:T(8,128)(2,1)S(1)}, u32[]{:S(2)}, u32[]{:S(2)}) collective-permute-start(bf16[2,1024,128]{2,1,0:T(8,128)(2,1)S(1)} %pad_maximum_fusion.c0), channel_id=1, source_target_pairs={{0,72},{1,73},{2,74},{3,75},{4,76},{5,77},{6,78},{7,79},{8,80},{9,... | collective-permute-start | bytes 1572872 | tf_op jit(solution)/shard_map/ppermute | solution.py:34
  39.1 16.5 %collective-permute-start = (bf16[256,128]{1,0:T(8,128)(2,1)}, bf16[256,128]{1,0:T(8,128)(2,1)S(1)}, u32[]{:S(2)}, u32[]{:S(2)}) collective-permute-start(bf16[256,128]{1,0:T(8,128)(2,1)} %scale.1), channel_id=1, source_target_pairs={{0,12},{1,13},{2,14},{3,15},{4,16},{5,17},{6,42},{7,43},{8,44},{9,... | collective-permute-start | bytes 196616 | tf_op jit(solution)/shard_map/ppermute | solution.py:34
  84.2 12.8 %collective-permute-start.8 = (bf16[4,384,128]{2,1,0:T(8,128)(2,1)S(1)}, bf16[4,384,128]{2,1,0:T(8,128)(2,1)S(1)}, u32[]{:S(2)}, u32[]{:S(2)}) collective-permute-start(bf16[4,384,128]{2,1,0:T(8,128)(2,1)S(1)} %shard_map.65), channel_id=1, source_target_pairs={{0,96},{1,97},{2,98},{3,99},{4,100},{5,101},{6,102},{7,103},{8,104... | collective-permute-start | bytes 1179656 | tf_op jit(solution)/shard_map/ppermute | solution.py:34
  97.6 12.6 %collective-permute-start.9 = (bf16[384,128]{1,0:T(8,128)(2,1)S(1)}, bf16[384,128]{1,0:T(8,128)(2,1)S(1)}, u32[]{:S(2)}, u32[]{:S(2)}) collective-permute-start(bf16[384,128]{1,0:T(8,128)(2,1)S(1)} %get-tuple-element.9), channel_id=1, source_target_pairs={{0,0},{1,49},{2,2},{3,51},{4,4},{5,53},{6,6},{7,55},{8,8},{9,57},{... | collective-permute-start | bytes 294920 | tf_op jit(solution)/shard_map/ppermute | solution.py:34
  101.2 9.1 %collective-permute-start.10 = (bf16[384,128]{1,0:T(8,128)(2,1)S(1)}, bf16[384,128]{1,0:T(8,128)(2,1)S(1)}, u32[]{:S(2)}, u32[]{:S(2)}) collective-permute-start(bf16[384,128]{1,0:T(8,128)(2,1)S(1)} %get-tuple-element.10), channel_id=1, source_target_pairs={{0,24},{1,73},{2,26},{3,75},{4,28},{5,77},{6,30},{7,79},{8,32},{9,... | collective-permute-start | bytes 294920 | tf_op jit(solution)/shard_map/ppermute | solution.py:34
  103.9 7.4 %collective-permute-start.11 = (bf16[384,128]{1,0:T(8,128)(2,1)S(1)}, bf16[384,128]{1,0:T(8,128)(2,1)S(1)}, u32[]{:S(2)}, u32[]{:S(2)}) collective-permute-start(bf16[384,128]{1,0:T(8,128)(2,1)S(1)} %get-tuple-element.11), channel_id=1, source_target_pairs={{0,48},{1,1},{2,50},{3,3},{4,52},{5,5},{6,54},{7,7},{8,56},{9,9},{... | collective-permute-start | bytes 294920 | tf_op jit(solution)/shard_map/ppermute | solution.py:34
  107.7 7.5 %collective-permute-start.12 = (bf16[384,128]{1,0:T(8,128)(2,1)S(1)}, bf16[384,128]{1,0:T(8,128)(2,1)S(1)}, u32[]{:S(2)}, u32[]{:S(2)}) collective-permute-start(bf16[384,128]{1,0:T(8,128)(2,1)S(1)} %get-tuple-element.12), channel_id=1, source_target_pairs={{0,72},{1,25},{2,74},{3,27},{4,76},{5,29},{6,78},{7,31},{8,80},{9,... | collective-permute-start | bytes 294920 | tf_op jit(solution)/shard_map/ppermute | solution.py:34

commit v3 on v2

--- a/solution.py
+++ b/solution.py
@@ -12,7 +12,7 @@
 COLS = X * Z * L
 PAIRS, WIDTH = 256, 128
 AXES = ("pool", "col")
-SHIFT = (2, 1, 0, 3)
+NEAR = ((9, 5, 8), (11, 1, 6), (0, 2, 4), (10, 3, 7))
 
 
 def at(h, k, x, z, l):
@@ -34,6 +34,12 @@
     return lax.ppermute(value, AXES, table(f))
 
 
+def spread(h, k, x, z, l):
+    side, (j, a) = z // 6, divmod(z % 6, 2)
+    return x, k, 2 * side + a, NEAR[(h - x) % H][j] + 6 * side + a, l
+
+
+H_GROUPS = [[h * K + k for h in range(H)] for k in range(K)]
 Z_GROUPS = [[x * Z * L + z * L + l for z in range(Z)] for x in range(X) for l in range(L)]
 
 
@@ -84,14 +90,25 @@
 
 def product_kernel(side, place, rows, c0, c1, c2, c3, out):
     which = place[side]
+
+    def columns(c, s):
+        start = pl.multiple_of(((place[8] + s) % H) * PAIRS, PAIRS)
+        return c[which, pl.ds(start, PAIRS), :]
+
     left = jnp.concatenate(
         [
-            jnp.concatenate([rows[3 * ((place[2] + SHIFT[s]) % H) + j] for s in range(H)], axis=0)
+            jnp.concatenate([rows[(NEAR[s][j] + place[2]) % Z] for s in range(H)], axis=0)
             for j in range(3)
         ],
         axis=1,
     )
-    right = jnp.concatenate([c[which] for c in (c0, c1, c2, c3)], axis=1)
+    right = jnp.concatenate(
+        [
+            jnp.concatenate([columns(c, s) for s in range(H)], axis=0)
+            for c in (c0, c1, c2, c3)
+        ],
+        axis=1,
+    )
     found = lax.dot_general(
         left, right, (((0,), (0,)), ((), ())), preferred_element_type=jnp.float32
     )
@@ -135,13 +152,13 @@
     for i, piece in enumerate((f0, f1, f2, f3)):
         t = place[4 + i]
         for j in range(3):
-            out[t % 2, j, t // 2] = piece[j * WIDTH : (j + 1) * WIDTH, :].astype(jnp.float32)
+            out[j, t % 2, t // 2] = piece[j * WIDTH : (j + 1) * WIDTH, :].astype(jnp.float32)
 
 
 def assemble(place, pieces):
     return pl.pallas_call(
         assemble_kernel,
-        out_shape=jax.ShapeDtypeStruct((2, 3, 2, WIDTH, WIDTH), jnp.float32),
+        out_shape=jax.ShapeDtypeStruct((3, 2, 2, WIDTH, WIDTH), jnp.float32),
         in_specs=[SMEM] + [VMEM] * 4,
         out_specs=VMEM,
         compiler_params=pltpu.CompilerParams(vmem_limit_bytes=8 * 2**20),
@@ -153,20 +170,18 @@
     pool, col = lax.axis_index("pool"), lax.axis_index("col")
     k, x, l = pool % K, col // (Z * L), col % L
     place = jnp.stack(
-        [1 - k, k, x, 2 * l] + [(x - 2 * k - r) % X for r in range(X)]
+        [1 - k, k, 6 * (x // 2) + x % 2, 2 * l]
+        + [(x - 2 * k - r) % X for r in range(X)]
+        + [pool // K]
     ).astype(jnp.int32)
 
-    around = []
-    for s in range(1, H):
-        around.append(move(pair_matrix, lambda h, k, x, z, l, s=s: (h - s, k, x, z, l)))
+    own = lax.all_gather(
+        pair_matrix, "pool", axis=0, tiled=True, axis_index_groups=H_GROUPS
+    )
     scaled = scaled_block(
         band_energy, occupation, pair_first, pair_second, pair_kpoint, pair_matrix
     )
-    sent = move(
-        scaled,
-        lambda h, k, x, z, l: (x, k, z // 3, z + 3 * SHIFT[(h - x) % H], l),
-    )
-    own = jnp.concatenate([pair_matrix] + around, axis=0)
+    sent = move(scaled, spread)
     other = move(own, lambda h, k, x, z, l: (h, k, x, z, 1 - l))
     both = jnp.stack([own, other])
     columns = [both]

time: 117 us -> 114 us (0.974)
  starting transfers between devices: 68.2 us -> 54.5 us
  blocking collectives: 27.5 us -> 40.2 us
  waiting for transfers between devices: 12.9 us -> 11.6 us
    all_gather x0 -> x1, blocking collectives: none -> 15 us  [blocks(): lax.all_gather(pair_matrix, 'pool', axis=0, tiled=True, axis_index_groups...]
    ppermute x13 -> x10, starting transfers between devices: 68.2 us -> 54.5 us  [move(): return lax.ppermute(value, AXES, table(f))]
    all_gather x1, blocking collectives: 27.5 us -> 25.2 us  [blocks(): rows = lax.all_gather(sent, 'col', axis=0, axis_index_groups=Z_GROUPS)]
    ppermute x13 -> x10, waiting for transfers between devices: 12.9 us -> 11.6 us  [move(): return lax.ppermute(value, AXES, table(f))]
  transfers between devices with their start and end apart: 13 -> 10, of which waited for: 6 -> 5; matrix products, arithmetic and copies ran while one was open for 1% -> 0% of each run, Pallas kernels for 3% -> 3%
where the time goes in v3:
time: 114 us; the launch traced here: 113 us
  starting transfers between devices  54.5 us (48%)
  blocking collectives  40.2 us (35%)
  waiting for transfers between devices  11.6 us (10%)
  Pallas kernels  6.75 us (6%)
    ppermute x10, starting transfers between devices, move(): return lax.ppermute(value, AXES, table(f))  54.5 us
    all_gather x1, blocking collectives, blocks(): rows = lax.all_gather(sent, 'col', axis=0, axis_index_groups=Z_GROUPS)  25.2 us
    all_gather x1, blocking collectives, blocks(): lax.all_gather(pair_matrix, 'pool', axis=0, tiled=True, axis_index_groups...  15 us
    ppermute x10, waiting for transfers between devices, move(): return lax.ppermute(value, AXES, table(f))  11.6 us
    pallas_call x1, Pallas kernels, scaled_block(): pl.pallas_call(scale_kernel, out_shape=jax.ShapeDtypeStruct(block.shape,...  2.35 us
    pallas_call x2, Pallas kernels, product(): pl.pallas_call(functools.partial(product_kernel, side), out_shape=jax.Sha...  2.3 us
  transfers between devices with their start and end apart: 10, of which 5 were waited for; matrix products, arithmetic and copies ran while one was open for 0% of the time, Pallas kernels for 3%

profile of v3, /device:TPU:1, one launch (start us, length us, event | category | flops | bytes accessed | tf_op | source)
XLA Modules:
  0.0 113.5 jit_solution(3870307038376673421)
XLA Ops:
  0.0 15.0 %all_gather.11 = bf16[1024,128]{1,0:T(8,128)(2,1)S(1)} all-gather(bf16[256,128]{1,0:T(8,128)(2,1)} %block.1), channel_id=1, replica_groups={{0,192,384,576},{96,288,480,672},{1,193,385,577},{97,289,481,673},{2,19..., dimensions={0}, use_global_device_ids=true | all-gather | bytes 327680 | tf_op jit(solution)/shard_map/all_gather | solution.py:178
  15.0 2.2 %collective-permute-start.1 = (bf16[1024,128]{1,0:T(8,128)(2,1)S(1)}, bf16[1024,128]{1,0:T(8,128)(2,1)S(1)}, u32[]{:S(2)}, u32[]{:S(2)}) collective-permute-start(bf16[1024,128]{1,0:T(8,128)(2,1)S(1)} %all_gather.11), channel_id=1, source_target_pairs={{0,1},{1,0},{2,3},{3,2},{4,5},{5,4},{6,7},{7,6},{8,9},{9,8},{10,11... | collective-permute-start | bytes 786440 | tf_op jit(solution)/shard_map/ppermute | solution.py:34
  17.2 4.9 %collective-permute-done.1 = bf16[1024,128]{1,0:T(8,128)(2,1)S(1)} collective-permute-done((bf16[1024,128]{1,0:T(8,128)(2,1)S(1)}, bf16[1024,128]{1,0:T(8,128)(2,1)S(1)}, u32[]{:S(2)}, u32[]{:S(2)}) %collective-permute-start.1) | collective-permute-done | bytes 262176 | tf_op jit(solution)/shard_map/ppermute | solution.py:34
  22.1 0.1 pad_maximum_fusion.c0
  22.2 3.0 %collective-permute-start.4 = (bf16[2,1024,128]{2,1,0:T(8,128)(2,1)S(1)}, bf16[2,1024,128]{2,1,0:T(8,128)(2,1)S(1)}, u32[]{:S(2)}, u32[]{:S(2)}) collective-permute-start(bf16[2,1024,128]{2,1,0:T(8,128)(2,1)S(1)} %pad_maximum_fusion.c0), channel_id=1, source_target_pairs={{0,24},{1,25},{2,26},{3,27},{4,28},{5,29},{6,30},{7,31},{8,32},{9,... | collective-permute-start | bytes 1572872 | tf_op jit(solution)/shard_map/ppermute | solution.py:34
  25.2 4.4 %collective-permute-start.3 = (bf16[2,1024,128]{2,1,0:T(8,128)(2,1)S(1)}, bf16[2,1024,128]{2,1,0:T(8,128)(2,1)S(1)}, u32[]{:S(2)}, u32[]{:S(2)}) collective-permute-start(bf16[2,1024,128]{2,1,0:T(8,128)(2,1)S(1)} %pad_maximum_fusion.c0), channel_id=1, source_target_pairs={{0,48},{1,49},{2,50},{3,51},{4,52},{5,53},{6,54},{7,55},{8,56},{9,... | collective-permute-start | bytes 1572872 | tf_op jit(solution)/shard_map/ppermute | solution.py:34
  29.6 3.1 %collective-permute-start.2 = (bf16[2,1024,128]{2,1,0:T(8,128)(2,1)S(1)}, bf16[2,1024,128]{2,1,0:T(8,128)(2,1)S(1)}, u32[]{:S(2)}, u32[]{:S(2)}) collective-permute-start(bf16[2,1024,128]{2,1,0:T(8,128)(2,1)S(1)} %pad_maximum_fusion.c0), channel_id=1, source_target_pairs={{0,72},{1,73},{2,74},{3,75},{4,76},{5,77},{6,78},{7,79},{8,80},{9,... | collective-permute-start | bytes 1572872 | tf_op jit(solution)/shard_map/ppermute | solution.py:34
  32.7 2.4 %scale.1 = bf16[256,128]{1,0:T(8,128)(2,1)} custom-call(f32[1,4,4096]{2,1,0:T(4,128)} %energy.1, s32[1,4,4096]{2,1,0:T(4,128)} %occupied.1, s32[1,256]{1,0:T(1,128)} %first.1, s32[1,256]{1,0:T(1,128)} %second.1, s32[1,256]{1,0:T(1,128)} %kpoint.1, bf16[256,128]{1,0:T(8,128)(2,1)} %block.1), custom_call_target="tpu_custom_call" | custom-call | flops 400000000 | bytes 300000 | tf_op jit(solution)/shard_map/scale/pallas_call | solution.py:82
  35.0 14.3 %collective-permute-start = (bf16[256,128]{1,0:T(8,128)(2,1)}, bf16[256,128]{1,0:T(8,128)(2,1)S(1)}, u32[]{:S(2)}, u32[]{:S(2)}) collective-permute-start(bf16[256,128]{1,0:T(8,128)(2,1)} %scale.1), channel_id=1, source_target_pairs={{0,18},{1,19},{2,44},{3,45},{4,10},{5,11},{6,36},{7,37},{8,16},{9,... | collective-permute-start | bytes 196616 | tf_op jit(solution)/shard_map/ppermute | solution.py:34
  49.5 0.1 stack.48.place
  49.6 1.4 %collective-permute-done = bf16[256,128]{1,0:T(8,128)(2,1)S(1)} collective-permute-done((bf16[256,128]{1,0:T(8,128)(2,1)}, bf16[256,128]{1,0:T(8,128)(2,1)S(1)}, u32[]{:S(2)}, u32[]{:S(2)}) %collective-permute-start) | collective-permute-done | bytes 65568 | tf_op jit(solution)/shard_map/ppermute | solution.py:34
  50.9 25.2 %all-gather = bf16[3072,128]{1,0:T(8,128)(2,1)S(1)} all-gather(bf16[256,128]{1,0:T(8,128)(2,1)S(1)} %collective-permute-done), channel_id=2, replica_groups={{0,2,4,6,8,10,12,14,16,18,20,22},{1,3,5,7,9,11,13,15,17,19,21,23},{24,2..., dimensions={0}, use_global_device_ids=true | all-gather | bytes 851968 | tf_op jit(solution)/shard_map/all_gather | solution.py:190
  76.1 0.0 collective-permute-done.4.c3
  76.1 0.0 collective-permute-done.3.c2
  76.1 0.0 collective-permute-done.2.c1
  76.1 1.2 %shard_map.65 = bf16[4,384,128]{2,1,0:T(8,128)(2,1)S(1)} custom-call(s32[9]{0:T(128)S(1)} %stack.48.place, bf16[12,256,128]{2,1,0:T(8,128)(2,1)S(1)} %bitcast.13, bf16[2,1024,128]{2,1,0:T(8,128)(2,1)S(1)} %pad_maximum_fusion.c0, bf16[2,1024,128]{2,1,0:T(8,128)(2,1)S(1)} %collective-permute-done.2.c1, bf16[2,1024,128]{2,1,0:T(8,128)(2,1)S(1)} %collective-permute-done.3.c2, ...), custom_call_target="tpu_custom_call" | custom-call | flops 400000000 | bytes 3000000 | tf_op jit(solution)/shard_map/pallas_call | solution.py:124
  77.3 13.0 %collective-permute-start.5 = (bf16[4,384,128]{2,1,0:T(8,128)(2,1)S(1)}, bf16[4,384,128]{2,1,0:T(8,128)(2,1)S(1)}, u32[]{:S(2)}, u32[]{:S(2)}) collective-permute-start(bf16[4,384,128]{2,1,0:T(8,128)(2,1)S(1)} %shard_map.65), channel_id=1, source_target_pairs={{0,96},{1,97},{2,98},{3,99},{4,100},{5,101},{6,102},{7,103},{8,104... | collective-permute-start | bytes 1179656 | tf_op jit(solution)/shard_map/ppermute | solution.py:34
  90.3 1.1 %shard_map.64.keep = f32[4,384,128]{2,1,0:T(8,128)S(1)} custom-call(s32[9]{0:T(128)S(1)} %stack.48.place, bf16[12,256,128]{2,1,0:T(8,128)(2,1)S(1)} %bitcast.14, bf16[2,1024,128]{2,1,0:T(8,128)(2,1)S(1)} %pad_maximum_fusion.c0, bf16[2,1024,128]{2,1,0:T(8,128)(2,1)S(1)} %collective-permute-done.2.c1, bf16[2,1024,128]{2,1,0:T(8,128)(2,1)S(1)} %collective-permute-done.3.c2, ...), custom_call_target="tpu_custom_call" | custom-call | flops 400000000 | bytes 3000000 | tf_op jit(solution)/shard_map/pallas_call | solution.py:124
  91.4 0.2 collective-permute-done.5.taken
  91.6 0.6 total.1
  92.2 2.8 %collective-permute-start.6 = (bf16[384,128]{1,0:T(8,128)(2,1)S(1)}, bf16[384,128]{1,0:T(8,128)(2,1)S(1)}, u32[]{:S(2)}, u32[]{:S(2)}) collective-permute-start(bf16[384,128]{1,0:T(8,128)(2,1)S(1)} %get-tuple-element.9), channel_id=1, source_target_pairs={{0,0},{1,49},{2,2},{3,51},{4,4},{5,53},{6,6},{7,55},{8,8},{9,57},{... | collective-permute-start | bytes 294920 | tf_op jit(solution)/shard_map/ppermute | solution.py:34
  95.0 5.7 %collective-permute-start.7 = (bf16[384,128]{1,0:T(8,128)(2,1)S(1)}, bf16[384,128]{1,0:T(8,128)(2,1)S(1)}, u32[]{:S(2)}, u32[]{:S(2)}) collective-permute-start(bf16[384,128]{1,0:T(8,128)(2,1)S(1)} %get-tuple-element.10), channel_id=1, source_target_pairs={{0,24},{1,73},{2,26},{3,75},{4,28},{5,77},{6,30},{7,79},{8,32},{9,... | collective-permute-start | bytes 294920 | tf_op jit(solution)/shard_map/ppermute | solution.py:34
  100.8 3.7 %collective-permute-start.8 = (bf16[384,128]{1,0:T(8,128)(2,1)S(1)}, bf16[384,128]{1,0:T(8,128)(2,1)S(1)}, u32[]{:S(2)}, u32[]{:S(2)}) collective-permute-start(bf16[384,128]{1,0:T(8,128)(2,1)S(1)} %get-tuple-element.11), channel_id=1, source_target_pairs={{0,48},{1,1},{2,50},{3,3},{4,52},{5,5},{6,54},{7,7},{8,56},{9,9},{... | collective-permute-start | bytes 294920 | tf_op jit(solution)/shard_map/ppermute | solution.py:34
  104.5 2.3 %collective-permute-start.9 = (bf16[384,128]{1,0:T(8,128)(2,1)S(1)}, bf16[384,128]{1,0:T(8,128)(2,1)S(1)}, u32[]{:S(2)}, u32[]{:S(2)}) collective-permute-start(bf16[384,128]{1,0:T(8,128)(2,1)S(1)} %get-tuple-element.12), channel_id=1, source_target_pairs={{0,72},{1,25},{2,74},{3,27},{4,76},{5,29},{6,78},{7,31},{8,80},{9,... | collective-permute-start | bytes 294920 | tf_op jit(solution)/shard_map/ppermute | solution.py:34
  106.8 0.0 collective-permute-done.6.f0
  106.9 0.0 collective-permute-done.7.f1
  106.9 1.4 %collective-permute-done.8.f2 = bf16[384,128]{1,0:T(8,128)(2,1)S(1)} collective-permute-done((bf16[384,128]{1,0:T(8,128)(2,1)S(1)}, bf16[384,128]{1,0:T(8,128)(2,1)S(1)}, u32[]{:S(2)}, u32[]{:S(2)}) %collective-permute-start.8) | collective-permute-done | bytes 98336 | tf_op jit(solution)/shard_map/ppermute | solution.py:34
  108.2 3.8 %collective-permute-done.9.f3 = bf16[384,128]{1,0:T(8,128)(2,1)S(1)} collective-permute-done((bf16[384,128]{1,0:T(8,128)(2,1)S(1)}, bf16[384,128]{1,0:T(8,128)(2,1)S(1)}, u32[]{:S(2)}, u32[]{:S(2)}) %collective-permute-start.9) | collective-permute-done | bytes 98336 | tf_op jit(solution)/shard_map/ppermute | solution.py:34
  112.0 1.5 %assemble.1 = f32[3,2,2,128,128]{4,3,2,1,0:T(8,128)} custom-call(s32[9]{0:T(128)S(1)} %stack.48.place, bf16[384,128]{1,0:T(8,128)(2,1)S(1)} %collective-permute-done.6.f0, bf16[384,128]{1,0:T(8,128)(2,1)S(1)} %collective-permute-done.7.f1, bf16[384,128]{1,0:T(8,128)(2,1)S(1)} %collective-permute-done.8.f2, bf16[384,128]{1,0:T(8,128)(2,1)S(1)} %collective-permute-done.9.f3), custom_call_target="tpu_custom_call" | custom-call | tf_op jit(solution)/shard_map/assemble/pallas_call | solution.py:159
Async XLA Ops:
  15.0 7.1 %collective-permute-start.1 = (bf16[1024,128]{1,0:T(8,128)(2,1)S(1)}, bf16[1024,128]{1,0:T(8,128)(2,1)S(1)}, u32[]{:S(2)}, u32[]{:S(2)}) collective-permute-start(bf16[1024,128]{1,0:T(8,128)(2,1)S(1)} %all_gather.11), channel_id=1, source_target_pairs={{0,1},{1,0},{2,3},{3,2},{4,5},{5,4},{6,7},{7,6},{8,9},{9,8},{10,11... | collective-permute-start | bytes 786440 | tf_op jit(solution)/shard_map/ppermute | solution.py:34
  22.2 53.9 %collective-permute-start.4 = (bf16[2,1024,128]{2,1,0:T(8,128)(2,1)S(1)}, bf16[2,1024,128]{2,1,0:T(8,128)(2,1)S(1)}, u32[]{:S(2)}, u32[]{:S(2)}) collective-permute-start(bf16[2,1024,128]{2,1,0:T(8,128)(2,1)S(1)} %pad_maximum_fusion.c0), channel_id=1, source_target_pairs={{0,24},{1,25},{2,26},{3,27},{4,28},{5,29},{6,30},{7,31},{8,32},{9,... | collective-permute-start | bytes 1572872 | tf_op jit(solution)/shard_map/ppermute | solution.py:34
  25.2 50.9 %collective-permute-start.3 = (bf16[2,1024,128]{2,1,0:T(8,128)(2,1)S(1)}, bf16[2,1024,128]{2,1,0:T(8,128)(2,1)S(1)}, u32[]{:S(2)}, u32[]{:S(2)}) collective-permute-start(bf16[2,1024,128]{2,1,0:T(8,128)(2,1)S(1)} %pad_maximum_fusion.c0), channel_id=1, source_target_pairs={{0,48},{1,49},{2,50},{3,51},{4,52},{5,53},{6,54},{7,55},{8,56},{9,... | collective-permute-start | bytes 1572872 | tf_op jit(solution)/shard_map/ppermute | solution.py:34
  29.6 46.5 %collective-permute-start.2 = (bf16[2,1024,128]{2,1,0:T(8,128)(2,1)S(1)}, bf16[2,1024,128]{2,1,0:T(8,128)(2,1)S(1)}, u32[]{:S(2)}, u32[]{:S(2)}) collective-permute-start(bf16[2,1024,128]{2,1,0:T(8,128)(2,1)S(1)} %pad_maximum_fusion.c0), channel_id=1, source_target_pairs={{0,72},{1,73},{2,74},{3,75},{4,76},{5,77},{6,78},{7,79},{8,80},{9,... | collective-permute-start | bytes 1572872 | tf_op jit(solution)/shard_map/ppermute | solution.py:34
  35.0 15.9 %collective-permute-start = (bf16[256,128]{1,0:T(8,128)(2,1)}, bf16[256,128]{1,0:T(8,128)(2,1)S(1)}, u32[]{:S(2)}, u32[]{:S(2)}) collective-permute-start(bf16[256,128]{1,0:T(8,128)(2,1)} %scale.1), channel_id=1, source_target_pairs={{0,18},{1,19},{2,44},{3,45},{4,10},{5,11},{6,36},{7,37},{8,16},{9,... | collective-permute-start | bytes 196616 | tf_op jit(solution)/shard_map/ppermute | solution.py:34
  77.3 14.3 %collective-permute-start.5 = (bf16[4,384,128]{2,1,0:T(8,128)(2,1)S(1)}, bf16[4,384,128]{2,1,0:T(8,128)(2,1)S(1)}, u32[]{:S(2)}, u32[]{:S(2)}) collective-permute-start(bf16[4,384,128]{2,1,0:T(8,128)(2,1)S(1)} %shard_map.65), channel_id=1, source_target_pairs={{0,96},{1,97},{2,98},{3,99},{4,100},{5,101},{6,102},{7,103},{8,104... | collective-permute-start | bytes 1179656 | tf_op jit(solution)/shard_map/ppermute | solution.py:34
  92.2 14.6 %collective-permute-start.6 = (bf16[384,128]{1,0:T(8,128)(2,1)S(1)}, bf16[384,128]{1,0:T(8,128)(2,1)S(1)}, u32[]{:S(2)}, u32[]{:S(2)}) collective-permute-start(bf16[384,128]{1,0:T(8,128)(2,1)S(1)} %get-tuple-element.9), channel_id=1, source_target_pairs={{0,0},{1,49},{2,2},{3,51},{4,4},{5,53},{6,6},{7,55},{8,8},{9,57},{... | collective-permute-start | bytes 294920 | tf_op jit(solution)/shard_map/ppermute | solution.py:34
  95.0 11.8 %collective-permute-start.7 = (bf16[384,128]{1,0:T(8,128)(2,1)S(1)}, bf16[384,128]{1,0:T(8,128)(2,1)S(1)}, u32[]{:S(2)}, u32[]{:S(2)}) collective-permute-start(bf16[384,128]{1,0:T(8,128)(2,1)S(1)} %get-tuple-element.10), channel_id=1, source_target_pairs={{0,24},{1,73},{2,26},{3,75},{4,28},{5,77},{6,30},{7,79},{8,32},{9,... | collective-permute-start | bytes 294920 | tf_op jit(solution)/shard_map/ppermute | solution.py:34
  100.8 7.4 %collective-permute-start.8 = (bf16[384,128]{1,0:T(8,128)(2,1)S(1)}, bf16[384,128]{1,0:T(8,128)(2,1)S(1)}, u32[]{:S(2)}, u32[]{:S(2)}) collective-permute-start(bf16[384,128]{1,0:T(8,128)(2,1)S(1)} %get-tuple-element.11), channel_id=1, source_target_pairs={{0,48},{1,1},{2,50},{3,3},{4,52},{5,5},{6,54},{7,7},{8,56},{9,9},{... | collective-permute-start | bytes 294920 | tf_op jit(solution)/shard_map/ppermute | solution.py:34
  104.5 7.5 %collective-permute-start.9 = (bf16[384,128]{1,0:T(8,128)(2,1)S(1)}, bf16[384,128]{1,0:T(8,128)(2,1)S(1)}, u32[]{:S(2)}, u32[]{:S(2)}) collective-permute-start(bf16[384,128]{1,0:T(8,128)(2,1)S(1)} %get-tuple-element.12), channel_id=1, source_target_pairs={{0,72},{1,25},{2,74},{3,27},{4,76},{5,29},{6,78},{7,31},{8,80},{9,... | collective-permute-start | bytes 294920 | tf_op jit(solution)/shard_map/ppermute | solution.py:34

commit v4 on v2

--- a/solution.py
+++ b/solution.py
@@ -12,7 +12,7 @@
 COLS = X * Z * L
 PAIRS, WIDTH = 256, 128
 AXES = ("pool", "col")
-SHIFT = (2, 1, 0, 3)
+NEAR = ((9, 5, 8), (11, 1, 6), (0, 2, 4), (10, 3, 7))
 
 
 def at(h, k, x, z, l):
@@ -32,6 +32,11 @@
 
 def move(value, f):
     return lax.ppermute(value, AXES, table(f))
+
+
+def spread(h, k, x, z, l):
+    side, (j, a) = z // 6, divmod(z % 6, 2)
+    return x, k, 2 * side + a, NEAR[(h - x) % H][j] + 6 * side + a, l
 
 
 Z_GROUPS = [[x * Z * L + z * L + l for z in range(Z)] for x in range(X) for l in range(L)]
@@ -86,7 +91,7 @@
     which = place[side]
     left = jnp.concatenate(
         [
-            jnp.concatenate([rows[3 * ((place[2] + SHIFT[s]) % H) + j] for s in range(H)], axis=0)
+            jnp.concatenate([rows[(NEAR[s][j] + place[2]) % Z] for s in range(H)], axis=0)
             for j in range(3)
         ],
         axis=1,
@@ -131,29 +136,44 @@
     )(place, keep, taken)
 
 
-def assemble_kernel(place, f0, f1, f2, f3, out):
-    for i, piece in enumerate((f0, f1, f2, f3)):
-        t = place[4 + i]
+def settle_kernel(start, count, place, *refs):
+    pieces, (out, wide, sems) = refs[:count], refs[-3:]
+    copies = []
+    for i, piece in enumerate(pieces):
+        t = place[4 + start + i]
         for j in range(3):
-            out[t % 2, j, t // 2] = piece[j * WIDTH : (j + 1) * WIDTH, :].astype(jnp.float32)
-
-
-def assemble(place, pieces):
-    return pl.pallas_call(
-        assemble_kernel,
-        out_shape=jax.ShapeDtypeStruct((2, 3, 2, WIDTH, WIDTH), jnp.float32),
-        in_specs=[SMEM] + [VMEM] * 4,
-        out_specs=VMEM,
+            wide[i, j] = piece[j * WIDTH : (j + 1) * WIDTH, :].astype(jnp.float32)
+            copies.append(
+                pltpu.make_async_copy(wide.at[i, j], out.at[j, t % 2, t // 2], sems.at[i, j])
+            )
+            copies[-1].start()
+    for copy in copies:
+        copy.wait()
+
+
+def settle(place, start, pieces, out=None):
+    count = len(pieces)
+    given = [] if out is None else [out]
+    return pl.pallas_call(
+        functools.partial(settle_kernel, start, count),
+        out_shape=jax.ShapeDtypeStruct((3, 2, 2, WIDTH, WIDTH), jnp.float32),
+        in_specs=[SMEM] + [VMEM] * count + [pl.BlockSpec(memory_space=pl.ANY)] * len(given),
+        out_specs=pl.BlockSpec(memory_space=pl.ANY),
+        scratch_shapes=[
+            pltpu.VMEM((count, 3, WIDTH, WIDTH), jnp.float32),
+            pltpu.SemaphoreType.DMA((count, 3)),
+        ],
+        input_output_aliases={1 + count: 0} if given else {},
         compiler_params=pltpu.CompilerParams(vmem_limit_bytes=8 * 2**20),
-        name="assemble",
-    )(place, *pieces)
+    )(place, *pieces, *given)
 
 
 def blocks(pair_matrix, band_energy, occupation, pair_first, pair_second, pair_kpoint):
     pool, col = lax.axis_index("pool"), lax.axis_index("col")
     k, x, l = pool % K, col // (Z * L), col % L
     place = jnp.stack(
-        [1 - k, k, x, 2 * l] + [(x - 2 * k - r) % X for r in range(X)]
+        [1 - k, k, 6 * (x // 2) + x % 2, 2 * l]
+        + [(x - 2 * k - r) % X for r in range(X)]
     ).astype(jnp.int32)
 
     around = []
@@ -162,10 +182,7 @@
     scaled = scaled_block(
         band_energy, occupation, pair_first, pair_second, pair_kpoint, pair_matrix
     )
-    sent = move(
-        scaled,
-        lambda h, k, x, z, l: (x, k, z // 3, z + 3 * SHIFT[(h - x) % H], l),
-    )
+    sent = move(scaled, spread)
     own = jnp.concatenate([pair_matrix] + around, axis=0)
     other = move(own, lambda h, k, x, z, l: (h, k, x, z, 1 - l))
     both = jnp.stack([own, other])
@@ -186,7 +203,8 @@
                 lambda h, k, x, z, l, r=r: (h, x // 2, x + r + 2 * l, z, l ^ k),
             )
         )
-    return assemble(place, home).reshape(-1, WIDTH)
+    most = settle(place, 0, home[:3])
+    return settle(place, 3, home[3:], most).reshape(-1, WIDTH)
 
 
 def solution(mesh):

time: 117 us -> 116 us (level)
  blocking collectives: 27.5 us -> 24.8 us
  starting transfers between devices: 68.2 us -> 70.1 us
  waiting for transfers between devices: 12.9 us -> 11.4 us
  Pallas kernels: 6.74 us -> 7.96 us
    all_gather x1, blocking collectives: 27.5 us -> 24.8 us  [blocks(): rows = lax.all_gather(sent, 'col', axis=0, axis_index_groups=Z_GROUPS)]
    ppermute x13, starting transfers between devices: 68.2 us -> 70.1 us  [move(): return lax.ppermute(value, AXES, table(f))]
    ppermute x13, waiting for transfers between devices: 12.9 us -> 11.4 us  [move(): return lax.ppermute(value, AXES, table(f))]
    pallas_call x1 -> x2, Pallas kernels: 1.48 us -> 2.68 us  [settle(): pl.pallas_call(functools.partial(settle_kernel, start, count), out_shape=...]
  transfers between devices with their start and end apart: 13 -> 13, of which waited for: 6 -> 6; matrix products, arithmetic and copies ran while one was open for 1% -> 1% of each run, Pallas kernels for 3% -> 4%
where the time goes in v4:
time: 116 us
  starting transfers between devices  70.1 us (60%)
  blocking collectives  24.8 us (21%)
  waiting for transfers between devices  11.4 us (10%)
  Pallas kernels  7.96 us (7%)
    ppermute x13, starting transfers between devices, move(): return lax.ppermute(value, AXES, table(f))  70.1 us
    all_gather x1, blocking collectives, blocks(): rows = lax.all_gather(sent, 'col', axis=0, axis_index_groups=Z_GROUPS)  24.8 us
    ppermute x13, waiting for transfers between devices, move(): return lax.ppermute(value, AXES, table(f))  11.4 us
    pallas_call x2, Pallas kernels, settle(): pl.pallas_call(functools.partial(settle_kernel, start, count), out_shape=...  2.68 us
    pallas_call x1, Pallas kernels, scaled_block(): pl.pallas_call(scale_kernel, out_shape=jax.ShapeDtypeStruct(block.shape,...  2.36 us
  transfers between devices with their start and end apart: 13, of which 6 were waited for; matrix products, arithmetic and copies ran while one was open for 1% of the time, Pallas kernels for 4%

profile of v4, /device:TPU:1, one launch (start us, length us, event | category | flops | bytes accessed | tf_op | source)
XLA Modules:
  0.0 115.6 jit_solution(10485222000864838518)
XLA Ops:
  0.0 8.3 %collective-permute-start.2 = (bf16[256,128]{1,0:T(8,128)(2,1)}, bf16[256,128]{1,0:T(8,128)(2,1)S(1)}, u32[]{:S(2)}, u32[]{:S(2)}) collective-permute-start(bf16[256,128]{1,0:T(8,128)(2,1)} %block.1), channel_id=1, source_target_pairs={{0,384},{1,385},{2,386},{3,387},{4,388},{5,389},{6,390},{7,391},{8... | collective-permute-start | bytes 196616 | tf_op jit(solution)/shard_map/ppermute | solution.py:34
  8.3 2.0 %collective-permute-start.1 = (bf16[256,128]{1,0:T(8,128)(2,1)}, bf16[256,128]{1,0:T(8,128)(2,1)S(1)}, u32[]{:S(2)}, u32[]{:S(2)}) collective-permute-start(bf16[256,128]{1,0:T(8,128)(2,1)} %block.1), channel_id=1, source_target_pairs={{0,576},{1,577},{2,578},{3,579},{4,580},{5,581},{6,582},{7,583},{8... | collective-permute-start | bytes 196616 | tf_op jit(solution)/shard_map/ppermute | solution.py:34
  10.2 4.2 %collective-permute-start.3 = (bf16[256,128]{1,0:T(8,128)(2,1)}, bf16[256,128]{1,0:T(8,128)(2,1)S(1)}, u32[]{:S(2)}, u32[]{:S(2)}) collective-permute-start(bf16[256,128]{1,0:T(8,128)(2,1)} %block.1), channel_id=1, source_target_pairs={{0,192},{1,193},{2,194},{3,195},{4,196},{5,197},{6,198},{7,199},{8... | collective-permute-start | bytes 196616 | tf_op jit(solution)/shard_map/ppermute | solution.py:34
  14.5 0.9 constant_dynamic-update-slice_fusion.3
  15.3 0.0 collective-permute-done.1
  15.3 0.0 collective-permute-done.2
  15.4 2.4 %collective-permute-done.3 = bf16[256,128]{1,0:T(8,128)(2,1)S(1)} collective-permute-done((bf16[256,128]{1,0:T(8,128)(2,1)}, bf16[256,128]{1,0:T(8,128)(2,1)S(1)}, u32[]{:S(2)}, u32[]{:S(2)}) %collective-permute-start.3) | collective-permute-done | bytes 65568 | tf_op jit(solution)/shard_map/ppermute | solution.py:34
  17.8 3.7 %collective-permute-start.4 = (bf16[1024,128]{1,0:T(8,128)(2,1)S(1)}, bf16[1024,128]{1,0:T(8,128)(2,1)S(1)}, u32[]{:S(2)}, u32[]{:S(2)}) collective-permute-start(bf16[1024,128]{1,0:T(8,128)(2,1)S(1)} %constant_dynamic-update-slice_fusion), channel_id=1, source_target_pairs={{0,1},{1,0},{2,3},{3,2},{4,5},{5,4},{6,7},{7,6},{8,9},{9,8},{10,11... | collective-permute-start | bytes 786440 | tf_op jit(solution)/shard_map/ppermute | solution.py:34
  21.5 4.0 %collective-permute-done.4 = bf16[1024,128]{1,0:T(8,128)(2,1)S(1)} collective-permute-done((bf16[1024,128]{1,0:T(8,128)(2,1)S(1)}, bf16[1024,128]{1,0:T(8,128)(2,1)S(1)}, u32[]{:S(2)}, u32[]{:S(2)}) %collective-permute-start.4) | collective-permute-done | bytes 262176 | tf_op jit(solution)/shard_map/ppermute | solution.py:34
  25.5 0.1 pad_maximum_fusion.c0
  25.5 3.7 %collective-permute-start.7 = (bf16[2,1024,128]{2,1,0:T(8,128)(2,1)S(1)}, bf16[2,1024,128]{2,1,0:T(8,128)(2,1)S(1)}, u32[]{:S(2)}, u32[]{:S(2)}) collective-permute-start(bf16[2,1024,128]{2,1,0:T(8,128)(2,1)S(1)} %pad_maximum_fusion.c0), channel_id=1, source_target_pairs={{0,24},{1,25},{2,26},{3,27},{4,28},{5,29},{6,30},{7,31},{8,32},{9,... | collective-permute-start | bytes 1572872 | tf_op jit(solution)/shard_map/ppermute | solution.py:34
  29.3 4.4 %collective-permute-start.6 = (bf16[2,1024,128]{2,1,0:T(8,128)(2,1)S(1)}, bf16[2,1024,128]{2,1,0:T(8,128)(2,1)S(1)}, u32[]{:S(2)}, u32[]{:S(2)}) collective-permute-start(bf16[2,1024,128]{2,1,0:T(8,128)(2,1)S(1)} %pad_maximum_fusion.c0), channel_id=1, source_target_pairs={{0,48},{1,49},{2,50},{3,51},{4,52},{5,53},{6,54},{7,55},{8,56},{9,... | collective-permute-start | bytes 1572872 | tf_op jit(solution)/shard_map/ppermute | solution.py:34
  33.6 3.1 %collective-permute-start.5 = (bf16[2,1024,128]{2,1,0:T(8,128)(2,1)S(1)}, bf16[2,1024,128]{2,1,0:T(8,128)(2,1)S(1)}, u32[]{:S(2)}, u32[]{:S(2)}) collective-permute-start(bf16[2,1024,128]{2,1,0:T(8,128)(2,1)S(1)} %pad_maximum_fusion.c0), channel_id=1, source_target_pairs={{0,72},{1,73},{2,74},{3,75},{4,76},{5,77},{6,78},{7,79},{8,80},{9,... | collective-permute-start | bytes 1572872 | tf_op jit(solution)/shard_map/ppermute | solution.py:34
  36.7 2.4 %scale.1 = bf16[256,128]{1,0:T(8,128)(2,1)} custom-call(f32[1,4,4096]{2,1,0:T(4,128)} %energy.1, s32[1,4,4096]{2,1,0:T(4,128)} %occupied.1, s32[1,256]{1,0:T(1,128)} %first.1, s32[1,256]{1,0:T(1,128)} %second.1, s32[1,256]{1,0:T(1,128)} %kpoint.1, bf16[256,128]{1,0:T(8,128)(2,1)} %block.1), custom_call_target="tpu_custom_call" | custom-call | flops 400000000 | bytes 300000 | tf_op jit(solution)/shard_map/scale/pallas_call | solution.py:81
  39.1 14.3 %collective-permute-start = (bf16[256,128]{1,0:T(8,128)(2,1)}, bf16[256,128]{1,0:T(8,128)(2,1)S(1)}, u32[]{:S(2)}, u32[]{:S(2)}) collective-permute-start(bf16[256,128]{1,0:T(8,128)(2,1)} %scale.1), channel_id=1, source_target_pairs={{0,18},{1,19},{2,44},{3,45},{4,10},{5,11},{6,36},{7,37},{8,16},{9,... | collective-permute-start | bytes 196616 | tf_op jit(solution)/shard_map/ppermute | solution.py:34
  53.5 0.1 stack.44.place
  53.6 1.4 %collective-permute-done = bf16[256,128]{1,0:T(8,128)(2,1)S(1)} collective-permute-done((bf16[256,128]{1,0:T(8,128)(2,1)}, bf16[256,128]{1,0:T(8,128)(2,1)S(1)}, u32[]{:S(2)}, u32[]{:S(2)}) %collective-permute-start) | collective-permute-done | bytes 65568 | tf_op jit(solution)/shard_map/ppermute | solution.py:34
  55.0 24.8 %all-gather = bf16[3072,128]{1,0:T(8,128)(2,1)S(1)} all-gather(bf16[256,128]{1,0:T(8,128)(2,1)S(1)} %collective-permute-done), channel_id=2, replica_groups={{0,2,4,6,8,10,12,14,16,18,20,22},{1,3,5,7,9,11,13,15,17,19,21,23},{24,2..., dimensions={0}, use_global_device_ids=true | all-gather | bytes 851968 | tf_op jit(solution)/shard_map/all_gather | solution.py:192
  79.8 0.0 collective-permute-done.7.c3
  79.8 0.0 collective-permute-done.6.c2
  79.8 0.0 collective-permute-done.5.c1
  79.8 1.2 shard_map.65
  80.9 11.4 %collective-permute-start.8 = (bf16[4,384,128]{2,1,0:T(8,128)(2,1)S(1)}, bf16[4,384,128]{2,1,0:T(8,128)(2,1)S(1)}, u32[]{:S(2)}, u32[]{:S(2)}) collective-permute-start(bf16[4,384,128]{2,1,0:T(8,128)(2,1)S(1)} %shard_map.65), channel_id=1, source_target_pairs={{0,96},{1,97},{2,98},{3,99},{4,100},{5,101},{6,102},{7,103},{8,104... | collective-permute-start | bytes 1179656 | tf_op jit(solution)/shard_map/ppermute | solution.py:34
  92.3 1.2 %shard_map.64.keep = f32[4,384,128]{2,1,0:T(8,128)S(1)} custom-call(s32[8]{0:T(128)S(1)} %stack.44.place, bf16[12,256,128]{2,1,0:T(8,128)(2,1)S(1)} %bitcast.13, bf16[2,1024,128]{2,1,0:T(8,128)(2,1)S(1)} %pad_maximum_fusion.c0, bf16[2,1024,128]{2,1,0:T(8,128)(2,1)S(1)} %collective-permute-done.5.c1, bf16[2,1024,128]{2,1,0:T(8,128)(2,1)S(1)} %collective-permute-done.6.c2, ...), custom_call_target="tpu_custom_call" | custom-call | flops 400000000 | bytes 3000000 | tf_op jit(solution)/shard_map/pallas_call | solution.py:112
  93.5 0.2 collective-permute-done.8.taken
  93.7 0.6 total.1
  94.3 4.0 %collective-permute-start.10 = (bf16[384,128]{1,0:T(8,128)(2,1)S(1)}, bf16[384,128]{1,0:T(8,128)(2,1)S(1)}, u32[]{:S(2)}, u32[]{:S(2)}) collective-permute-start(bf16[384,128]{1,0:T(8,128)(2,1)S(1)} %get-tuple-element.10), channel_id=1, source_target_pairs={{0,0},{1,49},{2,2},{3,51},{4,4},{5,53},{6,6},{7,55},{8,8},{9,57},{... | collective-permute-start | bytes 294920 | tf_op jit(solution)/shard_map/ppermute | solution.py:34
  98.3 5.1 %collective-permute-start.11 = (bf16[384,128]{1,0:T(8,128)(2,1)S(1)}, bf16[384,128]{1,0:T(8,128)(2,1)S(1)}, u32[]{:S(2)}, u32[]{:S(2)}) collective-permute-start(bf16[384,128]{1,0:T(8,128)(2,1)S(1)} %get-tuple-element.11), channel_id=1, source_target_pairs={{0,24},{1,73},{2,26},{3,75},{4,28},{5,77},{6,30},{7,79},{8,32},{9,... | collective-permute-start | bytes 294920 | tf_op jit(solution)/shard_map/ppermute | solution.py:34
  103.4 3.5 %collective-permute-start.12 = (bf16[384,128]{1,0:T(8,128)(2,1)S(1)}, bf16[384,128]{1,0:T(8,128)(2,1)S(1)}, u32[]{:S(2)}, u32[]{:S(2)}) collective-permute-start(bf16[384,128]{1,0:T(8,128)(2,1)S(1)} %get-tuple-element.12), channel_id=1, source_target_pairs={{0,48},{1,1},{2,50},{3,3},{4,52},{5,5},{6,54},{7,7},{8,56},{9,9},{... | collective-permute-start | bytes 294920 | tf_op jit(solution)/shard_map/ppermute | solution.py:34
  106.9 2.5 %collective-permute-start.9 = (bf16[384,128]{1,0:T(8,128)(2,1)S(1)}, bf16[384,128]{1,0:T(8,128)(2,1)S(1)}, u32[]{:S(2)}, u32[]{:S(2)}) collective-permute-start(bf16[384,128]{1,0:T(8,128)(2,1)S(1)} %get-tuple-element.9), channel_id=1, source_target_pairs={{0,72},{1,25},{2,74},{3,27},{4,76},{5,29},{6,78},{7,31},{8,80},{9,... | collective-permute-start | bytes 294920 | tf_op jit(solution)/shard_map/ppermute | solution.py:34
  109.4 0.0 collective-permute-done.10.refs_0_
  109.5 0.0 collective-permute-done.11.refs_1_
  109.5 1.4 %collective-permute-done.12.refs_2_ = bf16[384,128]{1,0:T(8,128)(2,1)S(1)} collective-permute-done((bf16[384,128]{1,0:T(8,128)(2,1)S(1)}, bf16[384,128]{1,0:T(8,128)(2,1)S(1)}, u32[]{:S(2)}, u32[]{:S(2)}) %collective-permute-start.12) | collective-permute-done | bytes 98336 | tf_op jit(solution)/shard_map/ppermute | solution.py:34
  110.8 1.4 %shard_map.66.refs_1_ = f32[3,2,2,128,128]{4,3,2,1,0:T(8,128)} custom-call(s32[8]{0:T(128)S(1)} %stack.44.place, bf16[384,128]{1,0:T(8,128)(2,1)S(1)} %collective-permute-done.10.refs_0_, bf16[384,128]{1,0:T(8,128)(2,1)S(1)} %collective-permute-done.11.refs_1_, bf16[384,128]{1,0:T(8,128)(2,1)S(1)} %collective-permute-done.12.refs_2_), custom_call_target="tpu_custom_call" | custom-call | tf_op jit(solution)/shard_map/pallas_call | solution.py:157
  112.2 2.1 %collective-permute-done.9.refs_0_ = bf16[384,128]{1,0:T(8,128)(2,1)S(1)} collective-permute-done((bf16[384,128]{1,0:T(8,128)(2,1)S(1)}, bf16[384,128]{1,0:T(8,128)(2,1)S(1)}, u32[]{:S(2)}, u32[]{:S(2)}) %collective-permute-start.9) | collective-permute-done | bytes 98336 | tf_op jit(solution)/shard_map/ppermute | solution.py:34
  114.4 1.2 %shard_map.67 = f32[3,2,2,128,128]{4,3,2,1,0:T(8,128)} custom-call(s32[8]{0:T(128)S(1)} %stack.44.place, bf16[384,128]{1,0:T(8,128)(2,1)S(1)} %collective-permute-done.9.refs_0_, f32[3,2,2,128,128]{4,3,2,1,0:T(8,128)} %shard_map.66.refs_1_), custom_call_target="tpu_custom_call", output_to_operand_aliasing={{}: (2, {})} | custom-call | tf_op jit(solution)/shard_map/pallas_call | solution.py:157
  (3 shorter events, 0.0 us)
Async XLA Ops:
  0.0 15.3 %collective-permute-start.2 = (bf16[256,128]{1,0:T(8,128)(2,1)}, bf16[256,128]{1,0:T(8,128)(2,1)S(1)}, u32[]{:S(2)}, u32[]{:S(2)}) collective-permute-start(bf16[256,128]{1,0:T(8,128)(2,1)} %block.1), channel_id=1, source_target_pairs={{0,384},{1,385},{2,386},{3,387},{4,388},{5,389},{6,390},{7,391},{8... | collective-permute-start | bytes 196616 | tf_op jit(solution)/shard_map/ppermute | solution.py:34
  8.3 7.1 %collective-permute-start.1 = (bf16[256,128]{1,0:T(8,128)(2,1)}, bf16[256,128]{1,0:T(8,128)(2,1)S(1)}, u32[]{:S(2)}, u32[]{:S(2)}) collective-permute-start(bf16[256,128]{1,0:T(8,128)(2,1)} %block.1), channel_id=1, source_target_pairs={{0,576},{1,577},{2,578},{3,579},{4,580},{5,581},{6,582},{7,583},{8... | collective-permute-start | bytes 196616 | tf_op jit(solution)/shard_map/ppermute | solution.py:34
  10.2 7.5 %collective-permute-start.3 = (bf16[256,128]{1,0:T(8,128)(2,1)}, bf16[256,128]{1,0:T(8,128)(2,1)S(1)}, u32[]{:S(2)}, u32[]{:S(2)}) collective-permute-start(bf16[256,128]{1,0:T(8,128)(2,1)} %block.1), channel_id=1, source_target_pairs={{0,192},{1,193},{2,194},{3,195},{4,196},{5,197},{6,198},{7,199},{8... | collective-permute-start | bytes 196616 | tf_op jit(solution)/shard_map/ppermute | solution.py:34
  17.8 7.7 %collective-permute-start.4 = (bf16[1024,128]{1,0:T(8,128)(2,1)S(1)}, bf16[1024,128]{1,0:T(8,128)(2,1)S(1)}, u32[]{:S(2)}, u32[]{:S(2)}) collective-permute-start(bf16[1024,128]{1,0:T(8,128)(2,1)S(1)} %constant_dynamic-update-slice_fusion), channel_id=1, source_target_pairs={{0,1},{1,0},{2,3},{3,2},{4,5},{5,4},{6,7},{7,6},{8,9},{9,8},{10,11... | collective-permute-start | bytes 786440 | tf_op jit(solution)/shard_map/ppermute | solution.py:34
  25.5 54.3 %collective-permute-start.7 = (bf16[2,1024,128]{2,1,0:T(8,128)(2,1)S(1)}, bf16[2,1024,128]{2,1,0:T(8,128)(2,1)S(1)}, u32[]{:S(2)}, u32[]{:S(2)}) collective-permute-start(bf16[2,1024,128]{2,1,0:T(8,128)(2,1)S(1)} %pad_maximum_fusion.c0), channel_id=1, source_target_pairs={{0,24},{1,25},{2,26},{3,27},{4,28},{5,29},{6,30},{7,31},{8,32},{9,... | collective-permute-start | bytes 1572872 | tf_op jit(solution)/shard_map/ppermute | solution.py:34
  29.3 50.5 %collective-permute-start.6 = (bf16[2,1024,128]{2,1,0:T(8,128)(2,1)S(1)}, bf16[2,1024,128]{2,1,0:T(8,128)(2,1)S(1)}, u32[]{:S(2)}, u32[]{:S(2)}) collective-permute-start(bf16[2,1024,128]{2,1,0:T(8,128)(2,1)S(1)} %pad_maximum_fusion.c0), channel_id=1, source_target_pairs={{0,48},{1,49},{2,50},{3,51},{4,52},{5,53},{6,54},{7,55},{8,56},{9,... | collective-permute-start | bytes 1572872 | tf_op jit(solution)/shard_map/ppermute | solution.py:34
  33.6 46.2 %collective-permute-start.5 = (bf16[2,1024,128]{2,1,0:T(8,128)(2,1)S(1)}, bf16[2,1024,128]{2,1,0:T(8,128)(2,1)S(1)}, u32[]{:S(2)}, u32[]{:S(2)}) collective-permute-start(bf16[2,1024,128]{2,1,0:T(8,128)(2,1)S(1)} %pad_maximum_fusion.c0), channel_id=1, source_target_pairs={{0,72},{1,73},{2,74},{3,75},{4,76},{5,77},{6,78},{7,79},{8,80},{9,... | collective-permute-start | bytes 1572872 | tf_op jit(solution)/shard_map/ppermute | solution.py:34
  39.1 15.9 %collective-permute-start = (bf16[256,128]{1,0:T(8,128)(2,1)}, bf16[256,128]{1,0:T(8,128)(2,1)S(1)}, u32[]{:S(2)}, u32[]{:S(2)}) collective-permute-start(bf16[256,128]{1,0:T(8,128)(2,1)} %scale.1), channel_id=1, source_target_pairs={{0,18},{1,19},{2,44},{3,45},{4,10},{5,11},{6,36},{7,37},{8,16},{9,... | collective-permute-start | bytes 196616 | tf_op jit(solution)/shard_map/ppermute | solution.py:34
  80.9 12.7 %collective-permute-start.8 = (bf16[4,384,128]{2,1,0:T(8,128)(2,1)S(1)}, bf16[4,384,128]{2,1,0:T(8,128)(2,1)S(1)}, u32[]{:S(2)}, u32[]{:S(2)}) collective-permute-start(bf16[4,384,128]{2,1,0:T(8,128)(2,1)S(1)} %shard_map.65), channel_id=1, source_target_pairs={{0,96},{1,97},{2,98},{3,99},{4,100},{5,101},{6,102},{7,103},{8,104... | collective-permute-start | bytes 1179656 | tf_op jit(solution)/shard_map/ppermute | solution.py:34
  94.3 15.2 %collective-permute-start.10 = (bf16[384,128]{1,0:T(8,128)(2,1)S(1)}, bf16[384,128]{1,0:T(8,128)(2,1)S(1)}, u32[]{:S(2)}, u32[]{:S(2)}) collective-permute-start(bf16[384,128]{1,0:T(8,128)(2,1)S(1)} %get-tuple-element.10), channel_id=1, source_target_pairs={{0,0},{1,49},{2,2},{3,51},{4,4},{5,53},{6,6},{7,55},{8,8},{9,57},{... | collective-permute-start | bytes 294920 | tf_op jit(solution)/shard_map/ppermute | solution.py:34
  98.3 11.2 %collective-permute-start.11 = (bf16[384,128]{1,0:T(8,128)(2,1)S(1)}, bf16[384,128]{1,0:T(8,128)(2,1)S(1)}, u32[]{:S(2)}, u32[]{:S(2)}) collective-permute-start(bf16[384,128]{1,0:T(8,128)(2,1)S(1)} %get-tuple-element.11), channel_id=1, source_target_pairs={{0,24},{1,73},{2,26},{3,75},{4,28},{5,77},{6,30},{7,79},{8,32},{9,... | collective-permute-start | bytes 294920 | tf_op jit(solution)/shard_map/ppermute | solution.py:34
  103.4 7.4 %collective-permute-start.12 = (bf16[384,128]{1,0:T(8,128)(2,1)S(1)}, bf16[384,128]{1,0:T(8,128)(2,1)S(1)}, u32[]{:S(2)}, u32[]{:S(2)}) collective-permute-start(bf16[384,128]{1,0:T(8,128)(2,1)S(1)} %get-tuple-element.12), channel_id=1, source_target_pairs={{0,48},{1,1},{2,50},{3,3},{4,52},{5,5},{6,54},{7,7},{8,56},{9,9},{... | collective-permute-start | bytes 294920 | tf_op jit(solution)/shard_map/ppermute | solution.py:34
  106.9 7.5 %collective-permute-start.9 = (bf16[384,128]{1,0:T(8,128)(2,1)S(1)}, bf16[384,128]{1,0:T(8,128)(2,1)S(1)}, u32[]{:S(2)}, u32[]{:S(2)}) collective-permute-start(bf16[384,128]{1,0:T(8,128)(2,1)S(1)} %get-tuple-element.9), channel_id=1, source_target_pairs={{0,72},{1,25},{2,74},{3,27},{4,76},{5,29},{6,78},{7,31},{8,80},{9,... | collective-permute-start | bytes 294920 | tf_op jit(solution)/shard_map/ppermute | solution.py:34

commit v5 on v3

--- a/solution.py
+++ b/solution.py
@@ -39,7 +39,12 @@
     return x, k, 2 * side + a, NEAR[(h - x) % H][j] + 6 * side + a, l
 
 
-H_GROUPS = [[h * K + k for h in range(H)] for k in range(K)]
+Y_GROUPS = [
+    [at(h, k, x, z, l) for h in range(H) for l in range(L)]
+    for k in range(K)
+    for x in range(X)
+    for z in range(Z)
+]
 Z_GROUPS = [[x * Z * L + z * L + l for z in range(Z)] for x in range(X) for l in range(L)]
 
 
@@ -92,8 +97,7 @@
     which = place[side]
 
     def columns(c, s):
-        start = pl.multiple_of(((place[8] + s) % H) * PAIRS, PAIRS)
-        return c[which, pl.ds(start, PAIRS), :]
+        return c[((place[8] + s) % H) * L + which]
 
     left = jnp.concatenate(
         [
@@ -170,20 +174,16 @@
     pool, col = lax.axis_index("pool"), lax.axis_index("col")
     k, x, l = pool % K, col // (Z * L), col % L
     place = jnp.stack(
-        [1 - k, k, 6 * (x // 2) + x % 2, 2 * l]
+        [(l + 1 - k) % L, (l + k) % L, 6 * (x // 2) + x % 2, 2 * l]
         + [(x - 2 * k - r) % X for r in range(X)]
         + [pool // K]
     ).astype(jnp.int32)
 
-    own = lax.all_gather(
-        pair_matrix, "pool", axis=0, tiled=True, axis_index_groups=H_GROUPS
-    )
+    sent = move(pair_matrix, spread)
     scaled = scaled_block(
         band_energy, occupation, pair_first, pair_second, pair_kpoint, pair_matrix
     )
-    sent = move(scaled, spread)
-    other = move(own, lambda h, k, x, z, l: (h, k, x, z, 1 - l))
-    both = jnp.stack([own, other])
+    both = lax.all_gather(scaled, AXES, axis=0, axis_index_groups=Y_GROUPS)
     columns = [both]
     for s in range(1, X):
         columns.append(move(both, lambda h, k, x, z, l, s=s: (h, k, x - s, z, l)))

time: 114 us -> 115 us (level)
  blocking collectives: 40.2 us -> 49.3 us
  waiting for transfers between devices: 11.6 us -> 6.29 us
  starting transfers between devices: 54.5 us -> 52.2 us
    all_gather x1, blocking collectives: 15 us -> 22.7 us  [blocks(): both = lax.all_gather(scaled, AXES, axis=0, axis_index_groups=Y_GROUPS)]
    ppermute x10 -> x9, waiting for transfers between devices: 11.6 us -> 6.29 us  [move(): return lax.ppermute(value, AXES, table(f))]
    ppermute x10 -> x9, starting transfers between devices: 54.5 us -> 52.2 us  [move(): return lax.ppermute(value, AXES, table(f))]
    all_gather x1, blocking collectives: 25.2 us -> 26.6 us  [blocks(): rows = lax.all_gather(sent, 'col', axis=0, axis_index_groups=Z_GROUPS)]
  transfers between devices with their start and end apart: 10 -> 9, of which waited for: 5 -> 4; matrix products, arithmetic and copies ran while one was open for 0% -> 0% of each run, Pallas kernels for 3% -> 1%
where the time goes in v5:
time: 115 us
  starting transfers between devices  52.2 us (45%)
  blocking collectives  49.3 us (43%)
  Pallas kernels  6.75 us (6%)
  waiting for transfers between devices  6.29 us (5%)
    ppermute x9, starting transfers between devices, move(): return lax.ppermute(value, AXES, table(f))  52.2 us
    all_gather x1, blocking collectives, blocks(): rows = lax.all_gather(sent, 'col', axis=0, axis_index_groups=Z_GROUPS)  26.6 us
    all_gather x1, blocking collectives, blocks(): both = lax.all_gather(scaled, AXES, axis=0, axis_index_groups=Y_GROUPS)  22.7 us
    ppermute x9, waiting for transfers between devices, move(): return lax.ppermute(value, AXES, table(f))  6.29 us
    pallas_call x1, Pallas kernels, scaled_block(): pl.pallas_call(scale_kernel, out_shape=jax.ShapeDtypeStruct(block.shape,...  2.35 us
    pallas_call x2, Pallas kernels, product(): pl.pallas_call(functools.partial(product_kernel, side), out_shape=jax.Sha...  2.3 us
  transfers between devices with their start and end apart: 9, of which 4 were waited for; matrix products, arithmetic and copies ran while one was open for 0% of the time, Pallas kernels for 1%

profile of v5, /device:TPU:1, one launch (start us, length us, event | category | flops | bytes accessed | tf_op | source)
XLA Modules:
  0.0 115.0 jit_solution(10209412417649175655)
XLA Ops:
  0.0 2.3 %scale.1 = bf16[256,128]{1,0:T(8,128)(2,1)} custom-call(f32[1,4,4096]{2,1,0:T(4,128)} %energy.1, s32[1,4,4096]{2,1,0:T(4,128)} %occupied.1, s32[1,256]{1,0:T(1,128)} %first.1, s32[1,256]{1,0:T(1,128)} %second.1, s32[1,256]{1,0:T(1,128)} %kpoint.1, bf16[256,128]{1,0:T(8,128)(2,1)} %block.1), custom_call_target="tpu_custom_call" | custom-call | flops 400000000 | bytes 300000 | tf_op jit(solution)/shard_map/scale/pallas_call | solution.py:87
  2.3 0.0 copy-start
  2.4 22.7 %all-gather.1 = bf16[2048,128]{1,0:T(8,128)(2,1)S(1)} all-gather(bf16[256,128]{1,0:T(8,128)(2,1)} %scale.1), channel_id=3, replica_groups={{0,1,192,193,384,385,576,577},{2,3,194,195,386,387,578,579},{4,5,196,19..., dimensions={0}, use_global_device_ids=true | all-gather | bytes 589824 | tf_op jit(solution)/shard_map/all_gather | solution.py:186
  25.0 3.0 %collective-permute-start.3 = (bf16[8,256,128]{2,1,0:T(8,128)(2,1)S(1)}, bf16[8,256,128]{2,1,0:T(8,128)(2,1)S(1)}, u32[]{:S(2)}, u32[]{:S(2)}) collective-permute-start(bf16[8,256,128]{2,1,0:T(8,128)(2,1)S(1)} %bitcast.14), channel_id=1, source_target_pairs={{0,24},{1,25},{2,26},{3,27},{4,28},{5,29},{6,30},{7,31},{8,32},{9,... | collective-permute-start | bytes 1572872 | tf_op jit(solution)/shard_map/ppermute | solution.py:34
  28.0 4.4 %collective-permute-start.2 = (bf16[8,256,128]{2,1,0:T(8,128)(2,1)S(1)}, bf16[8,256,128]{2,1,0:T(8,128)(2,1)S(1)}, u32[]{:S(2)}, u32[]{:S(2)}) collective-permute-start(bf16[8,256,128]{2,1,0:T(8,128)(2,1)S(1)} %bitcast.15), channel_id=1, source_target_pairs={{0,48},{1,49},{2,50},{3,51},{4,52},{5,53},{6,54},{7,55},{8,56},{9,... | collective-permute-start | bytes 1572872 | tf_op jit(solution)/shard_map/ppermute | solution.py:34
  32.4 3.0 %collective-permute-start.1 = (bf16[8,256,128]{2,1,0:T(8,128)(2,1)S(1)}, bf16[8,256,128]{2,1,0:T(8,128)(2,1)S(1)}, u32[]{:S(2)}, u32[]{:S(2)}) collective-permute-start(bf16[8,256,128]{2,1,0:T(8,128)(2,1)S(1)} %bitcast.16), channel_id=1, source_target_pairs={{0,72},{1,73},{2,74},{3,75},{4,76},{5,77},{6,78},{7,79},{8,80},{9,... | collective-permute-start | bytes 1572872 | tf_op jit(solution)/shard_map/ppermute | solution.py:34
  35.4 0.0 copy-done
  35.4 14.3 %collective-permute-start = (bf16[256,128]{1,0:T(8,128)(2,1)S(1)}, bf16[256,128]{1,0:T(8,128)(2,1)S(1)}, u32[]{:S(2)}, u32[]{:S(2)}) collective-permute-start(bf16[256,128]{1,0:T(8,128)(2,1)S(1)} %copy-done), channel_id=1, source_target_pairs={{0,18},{1,19},{2,44},{3,45},{4,10},{5,11},{6,36},{7,37},{8,16},{9,... | collective-permute-start | bytes 196616 | tf_op jit(solution)/shard_map/ppermute | solution.py:34
  49.9 0.1 stack.39.place
  50.0 1.0 collective-permute-done
  51.0 26.6 %all-gather = bf16[3072,128]{1,0:T(8,128)(2,1)S(1)} all-gather(bf16[256,128]{1,0:T(8,128)(2,1)S(1)} %collective-permute-done), channel_id=2, replica_groups={{0,2,4,6,8,10,12,14,16,18,20,22},{1,3,5,7,9,11,13,15,17,19,21,23},{24,2..., dimensions={0}, use_global_device_ids=true | all-gather | bytes 851968 | tf_op jit(solution)/shard_map/all_gather | solution.py:190
  77.7 0.0 collective-permute-done.3.c3
  77.7 0.0 collective-permute-done.2.c2
  77.7 0.0 collective-permute-done.1.c1
  77.7 1.2 %shard_map.65 = bf16[4,384,128]{2,1,0:T(8,128)(2,1)S(1)} custom-call(s32[9]{0:T(128)S(1)} %stack.39.place, bf16[12,256,128]{2,1,0:T(8,128)(2,1)S(1)} %bitcast.12, bf16[8,256,128]{2,1,0:T(8,128)(2,1)S(1)} %bitcast.17, bf16[8,256,128]{2,1,0:T(8,128)(2,1)S(1)} %collective-permute-done.1.c1, bf16[8,256,128]{2,1,0:T(8,128)(2,1)S(1)} %collective-permute-done.2.c2, ...), custom_call_target="tpu_custom_call" | custom-call | flops 400000000 | bytes 3000000 | tf_op jit(solution)/shard_map/pallas_call | solution.py:128
  78.8 13.1 %collective-permute-start.4 = (bf16[4,384,128]{2,1,0:T(8,128)(2,1)S(1)}, bf16[4,384,128]{2,1,0:T(8,128)(2,1)S(1)}, u32[]{:S(2)}, u32[]{:S(2)}) collective-permute-start(bf16[4,384,128]{2,1,0:T(8,128)(2,1)S(1)} %shard_map.65), channel_id=1, source_target_pairs={{0,96},{1,97},{2,98},{3,99},{4,100},{5,101},{6,102},{7,103},{8,104... | collective-permute-start | bytes 1179656 | tf_op jit(solution)/shard_map/ppermute | solution.py:34
  91.9 1.1 shard_map.64.keep
  93.1 0.2 collective-permute-done.4.taken
  93.3 0.6 total.1
  93.9 3.3 %collective-permute-start.5 = (bf16[384,128]{1,0:T(8,128)(2,1)S(1)}, bf16[384,128]{1,0:T(8,128)(2,1)S(1)}, u32[]{:S(2)}, u32[]{:S(2)}) collective-permute-start(bf16[384,128]{1,0:T(8,128)(2,1)S(1)} %get-tuple-element.9), channel_id=1, source_target_pairs={{0,0},{1,49},{2,2},{3,51},{4,4},{5,53},{6,6},{7,55},{8,8},{9,57},{... | collective-permute-start | bytes 294920 | tf_op jit(solution)/shard_map/ppermute | solution.py:34
  97.2 4.8 %collective-permute-start.6 = (bf16[384,128]{1,0:T(8,128)(2,1)S(1)}, bf16[384,128]{1,0:T(8,128)(2,1)S(1)}, u32[]{:S(2)}, u32[]{:S(2)}) collective-permute-start(bf16[384,128]{1,0:T(8,128)(2,1)S(1)} %get-tuple-element.10), channel_id=1, source_target_pairs={{0,24},{1,73},{2,26},{3,75},{4,28},{5,77},{6,30},{7,79},{8,32},{9,... | collective-permute-start | bytes 294920 | tf_op jit(solution)/shard_map/ppermute | solution.py:34
  102.0 4.0 %collective-permute-start.7 = (bf16[384,128]{1,0:T(8,128)(2,1)S(1)}, bf16[384,128]{1,0:T(8,128)(2,1)S(1)}, u32[]{:S(2)}, u32[]{:S(2)}) collective-permute-start(bf16[384,128]{1,0:T(8,128)(2,1)S(1)} %get-tuple-element.11), channel_id=1, source_target_pairs={{0,48},{1,1},{2,50},{3,3},{4,52},{5,5},{6,54},{7,7},{8,56},{9,9},{... | collective-permute-start | bytes 294920 | tf_op jit(solution)/shard_map/ppermute | solution.py:34
  106.0 2.4 %collective-permute-start.8 = (bf16[384,128]{1,0:T(8,128)(2,1)S(1)}, bf16[384,128]{1,0:T(8,128)(2,1)S(1)}, u32[]{:S(2)}, u32[]{:S(2)}) collective-permute-start(bf16[384,128]{1,0:T(8,128)(2,1)S(1)} %get-tuple-element.12), channel_id=1, source_target_pairs={{0,72},{1,25},{2,74},{3,27},{4,76},{5,29},{6,78},{7,31},{8,80},{9,... | collective-permute-start | bytes 294920 | tf_op jit(solution)/shard_map/ppermute | solution.py:34
  108.4 0.0 collective-permute-done.5.f0
  108.4 0.0 collective-permute-done.6.f1
  108.4 1.1 collective-permute-done.7.f2
  109.5 4.0 %collective-permute-done.8.f3 = bf16[384,128]{1,0:T(8,128)(2,1)S(1)} collective-permute-done((bf16[384,128]{1,0:T(8,128)(2,1)S(1)}, bf16[384,128]{1,0:T(8,128)(2,1)S(1)}, u32[]{:S(2)}, u32[]{:S(2)}) %collective-permute-start.8) | collective-permute-done | bytes 98336 | tf_op jit(solution)/shard_map/ppermute | solution.py:34
  113.5 1.5 %assemble.1 = f32[3,2,2,128,128]{4,3,2,1,0:T(8,128)} custom-call(s32[9]{0:T(128)S(1)} %stack.39.place, bf16[384,128]{1,0:T(8,128)(2,1)S(1)} %collective-permute-done.5.f0, bf16[384,128]{1,0:T(8,128)(2,1)S(1)} %collective-permute-done.6.f1, bf16[384,128]{1,0:T(8,128)(2,1)S(1)} %collective-permute-done.7.f2, bf16[384,128]{1,0:T(8,128)(2,1)S(1)} %collective-permute-done.8.f3), custom_call_target="tpu_custom_call" | custom-call | tf_op jit(solution)/shard_map/assemble/pallas_call | solution.py:163
Async XLA Ops:
  2.3 33.1 %copy-start = (bf16[256,128]{1,0:T(8,128)(2,1)S(1)}, bf16[256,128]{1,0:T(8,128)(2,1)}, u32[]{:S(2)}) copy-start(bf16[256,128]{1,0:T(8,128)(2,1)} %block.1) | copy-start | bytes 196612
  25.0 52.6 %collective-permute-start.3 = (bf16[8,256,128]{2,1,0:T(8,128)(2,1)S(1)}, bf16[8,256,128]{2,1,0:T(8,128)(2,1)S(1)}, u32[]{:S(2)}, u32[]{:S(2)}) collective-permute-start(bf16[8,256,128]{2,1,0:T(8,128)(2,1)S(1)} %bitcast.14), channel_id=1, source_target_pairs={{0,24},{1,25},{2,26},{3,27},{4,28},{5,29},{6,30},{7,31},{8,32},{9,... | collective-permute-start | bytes 1572872 | tf_op jit(solution)/shard_map/ppermute | solution.py:34
  28.0 49.7 %collective-permute-start.2 = (bf16[8,256,128]{2,1,0:T(8,128)(2,1)S(1)}, bf16[8,256,128]{2,1,0:T(8,128)(2,1)S(1)}, u32[]{:S(2)}, u32[]{:S(2)}) collective-permute-start(bf16[8,256,128]{2,1,0:T(8,128)(2,1)S(1)} %bitcast.15), channel_id=1, source_target_pairs={{0,48},{1,49},{2,50},{3,51},{4,52},{5,53},{6,54},{7,55},{8,56},{9,... | collective-permute-start | bytes 1572872 | tf_op jit(solution)/shard_map/ppermute | solution.py:34
  32.4 45.3 %collective-permute-start.1 = (bf16[8,256,128]{2,1,0:T(8,128)(2,1)S(1)}, bf16[8,256,128]{2,1,0:T(8,128)(2,1)S(1)}, u32[]{:S(2)}, u32[]{:S(2)}) collective-permute-start(bf16[8,256,128]{2,1,0:T(8,128)(2,1)S(1)} %bitcast.16), channel_id=1, source_target_pairs={{0,72},{1,73},{2,74},{3,75},{4,76},{5,77},{6,78},{7,79},{8,80},{9,... | collective-permute-start | bytes 1572872 | tf_op jit(solution)/shard_map/ppermute | solution.py:34
  35.4 15.6 %collective-permute-start = (bf16[256,128]{1,0:T(8,128)(2,1)S(1)}, bf16[256,128]{1,0:T(8,128)(2,1)S(1)}, u32[]{:S(2)}, u32[]{:S(2)}) collective-permute-start(bf16[256,128]{1,0:T(8,128)(2,1)S(1)} %copy-done), channel_id=1, source_target_pairs={{0,18},{1,19},{2,44},{3,45},{4,10},{5,11},{6,36},{7,37},{8,16},{9,... | collective-permute-start | bytes 196616 | tf_op jit(solution)/shard_map/ppermute | solution.py:34
  78.8 14.4 %collective-permute-start.4 = (bf16[4,384,128]{2,1,0:T(8,128)(2,1)S(1)}, bf16[4,384,128]{2,1,0:T(8,128)(2,1)S(1)}, u32[]{:S(2)}, u32[]{:S(2)}) collective-permute-start(bf16[4,384,128]{2,1,0:T(8,128)(2,1)S(1)} %shard_map.65), channel_id=1, source_target_pairs={{0,96},{1,97},{2,98},{3,99},{4,100},{5,101},{6,102},{7,103},{8,104... | collective-permute-start | bytes 1179656 | tf_op jit(solution)/shard_map/ppermute | solution.py:34
  93.9 14.5 %collective-permute-start.5 = (bf16[384,128]{1,0:T(8,128)(2,1)S(1)}, bf16[384,128]{1,0:T(8,128)(2,1)S(1)}, u32[]{:S(2)}, u32[]{:S(2)}) collective-permute-start(bf16[384,128]{1,0:T(8,128)(2,1)S(1)} %get-tuple-element.9), channel_id=1, source_target_pairs={{0,0},{1,49},{2,2},{3,51},{4,4},{5,53},{6,6},{7,55},{8,8},{9,57},{... | collective-permute-start | bytes 294920 | tf_op jit(solution)/shard_map/ppermute | solution.py:34
  97.2 11.2 %collective-permute-start.6 = (bf16[384,128]{1,0:T(8,128)(2,1)S(1)}, bf16[384,128]{1,0:T(8,128)(2,1)S(1)}, u32[]{:S(2)}, u32[]{:S(2)}) collective-permute-start(bf16[384,128]{1,0:T(8,128)(2,1)S(1)} %get-tuple-element.10), channel_id=1, source_target_pairs={{0,24},{1,73},{2,26},{3,75},{4,28},{5,77},{6,30},{7,79},{8,32},{9,... | collective-permute-start | bytes 294920 | tf_op jit(solution)/shard_map/ppermute | solution.py:34
  102.0 7.4 %collective-permute-start.7 = (bf16[384,128]{1,0:T(8,128)(2,1)S(1)}, bf16[384,128]{1,0:T(8,128)(2,1)S(1)}, u32[]{:S(2)}, u32[]{:S(2)}) collective-permute-start(bf16[384,128]{1,0:T(8,128)(2,1)S(1)} %get-tuple-element.11), channel_id=1, source_target_pairs={{0,48},{1,1},{2,50},{3,3},{4,52},{5,5},{6,54},{7,7},{8,56},{9,9},{... | collective-permute-start | bytes 294920 | tf_op jit(solution)/shard_map/ppermute | solution.py:34
  106.0 7.5 %collective-permute-start.8 = (bf16[384,128]{1,0:T(8,128)(2,1)S(1)}, bf16[384,128]{1,0:T(8,128)(2,1)S(1)}, u32[]{:S(2)}, u32[]{:S(2)}) collective-permute-start(bf16[384,128]{1,0:T(8,128)(2,1)S(1)} %get-tuple-element.12), channel_id=1, source_target_pairs={{0,72},{1,25},{2,74},{3,27},{4,76},{5,29},{6,78},{7,31},{8,80},{9,... | collective-permute-start | bytes 294920 | tf_op jit(solution)/shard_map/ppermute | solution.py:34

commit v6 on v5

--- a/solution.py
+++ b/solution.py
@@ -39,16 +39,11 @@
     return x, k, 2 * side + a, NEAR[(h - x) % H][j] + 6 * side + a, l
 
 
-Y_GROUPS = [
-    [at(h, k, x, z, l) for h in range(H) for l in range(L)]
-    for k in range(K)
-    for x in range(X)
-    for z in range(Z)
-]
+H_GROUPS = [[h * K + k for h in range(H)] for k in range(K)]
 Z_GROUPS = [[x * Z * L + z * L + l for z in range(Z)] for x in range(X) for l in range(L)]
 
 
-def scale_kernel(energy, occupied, first, second, kpoint, block, out, energies, filled):
+def scale_kernel(energy, occupied, first, second, kpoint, own, other, out, energies, filled):
     chunks = energy.shape[-1] // WIDTH
     kpts = energy.shape[-2]
     for c in range(chunks):
@@ -79,18 +74,20 @@
     for i in range(PAIRS // WIDTH):
         rows = pl.ds(i * WIDTH, WIDTH)
         factor = jnp.broadcast_to(weight[:, i * WIDTH : (i + 1) * WIDTH], (WIDTH, WIDTH)).T
-        out[rows, :] = (block[rows, :].astype(jnp.float32) * factor).astype(jnp.bfloat16)
-
-
-def scaled_block(energy, occupied, first, second, kpoint, block):
+        for n, block in enumerate((own, other)):
+            out[n, rows, :] = (block[rows, :].astype(jnp.float32) * factor).astype(jnp.bfloat16)
+
+
+def scaled_blocks(energy, occupied, first, second, kpoint, own, other):
     entries = energy.shape[1] * energy.shape[2] // WIDTH
     return pl.pallas_call(
         scale_kernel,
-        out_shape=jax.ShapeDtypeStruct(block.shape, jnp.bfloat16),
+        out_shape=jax.ShapeDtypeStruct((2,) + own.shape, jnp.bfloat16),
         scratch_shapes=[pltpu.VMEM((entries, WIDTH), jnp.float32)] * 2,
+        compiler_params=pltpu.CompilerParams(vmem_limit_bytes=8 * 2**20),
         cost_estimate=pl.CostEstimate(flops=4 * 10**8, bytes_accessed=3 * 10**5, transcendentals=0),
         name="scale",
-    )(energy, occupied, first, second, kpoint, block)
+    )(energy, occupied, first, second, kpoint, own, other)
 
 
 def product_kernel(side, place, rows, c0, c1, c2, c3, out):
@@ -174,16 +171,17 @@
     pool, col = lax.axis_index("pool"), lax.axis_index("col")
     k, x, l = pool % K, col // (Z * L), col % L
     place = jnp.stack(
-        [(l + 1 - k) % L, (l + k) % L, 6 * (x // 2) + x % 2, 2 * l]
+        [1 - k, k, 6 * (x // 2) + x % 2, 2 * l]
         + [(x - 2 * k - r) % X for r in range(X)]
         + [pool // K]
     ).astype(jnp.int32)
 
+    other = move(pair_matrix, lambda h, k, x, z, l: (h, k, x, z, 1 - l))
     sent = move(pair_matrix, spread)
-    scaled = scaled_block(
-        band_energy, occupation, pair_first, pair_second, pair_kpoint, pair_matrix
-    )
-    both = lax.all_gather(scaled, AXES, axis=0, axis_index_groups=Y_GROUPS)
+    scaled = scaled_blocks(
+        band_energy, occupation, pair_first, pair_second, pair_kpoint, pair_matrix, other
+    )
+    both = lax.all_gather(scaled, "pool", axis=0, tiled=True, axis_index_groups=H_GROUPS)
     columns = [both]
     for s in range(1, X):
         columns.append(move(both, lambda h, k, x, z, l, s=s: (h, k, x - s, z, l)))

time: 115 us -> 117 us (1.017)
  blocking collectives: 49.3 us -> 40.4 us
  starting transfers between devices: 52.2 us -> 57.7 us
  local copies, waits for them, and re-layouts: 0.09 us -> 3.8 us
  waiting for transfers between devices: 6.29 us -> 8.4 us
    all_gather x1, blocking collectives: 22.7 us -> 15.1 us  [blocks(): lax.all_gather(scaled, 'pool', axis=0, tiled=True, axis_index_groups=H_GR...]
    ppermute x9 -> x10, starting transfers between devices: 52.2 us -> 57.7 us  [move(): return lax.ppermute(value, AXES, table(f))]
    unnamed x2 -> x10, local copies, waits for them, and re-layouts: 0.01 us -> 3.71 us
    ppermute x9 -> x10, waiting for transfers between devices: 6.29 us -> 8.4 us  [move(): return lax.ppermute(value, AXES, table(f))]
    all_gather x1, blocking collectives: 26.6 us -> 25.3 us  [blocks(): rows = lax.all_gather(sent, 'col', axis=0, axis_index_groups=Z_GROUPS)]
  transfers between devices with their start and end apart: 9 -> 10, of which waited for: 4 -> 5; matrix products, arithmetic and copies ran while one was open for 0% -> 0% of each run, Pallas kernels for 1% -> 1%
where the time goes in v6:
time: 117 us
  starting transfers between devices  57.7 us (49%)
  blocking collectives  40.4 us (35%)
  waiting for transfers between devices  8.4 us (7%)
  Pallas kernels  6 us (5%)
  local copies, waits for them, and re-layouts  3.8 us (3%)
    ppermute x10, starting transfers between devices, move(): return lax.ppermute(value, AXES, table(f))  57.7 us
    all_gather x1, blocking collectives, blocks(): rows = lax.all_gather(sent, 'col', axis=0, axis_index_groups=Z_GROUPS)  25.3 us
    all_gather x1, blocking collectives, blocks(): lax.all_gather(scaled, 'pool', axis=0, tiled=True, axis_index_groups=H_GR...  15.1 us
    ppermute x10, waiting for transfers between devices, move(): return lax.ppermute(value, AXES, table(f))  8.4 us
    unnamed x10, local copies, waits for them, and re-layouts  3.71 us
  transfers between devices with their start and end apart: 10, of which 5 were waited for; matrix products, arithmetic and copies ran while one was open for 0% of the time, Pallas kernels for 1%

profile of v6, /device:TPU:1, one launch (start us, length us, event | category | flops | bytes accessed | tf_op | source)
XLA Modules:
  0.0 116.5 jit_solution(5340988916657948157)
XLA Ops:
  0.0 4.0 %collective-permute-start.1 = (bf16[256,128]{1,0:T(8,128)(2,1)}, bf16[256,128]{1,0:T(8,128)(2,1)S(1)}, u32[]{:S(2)}, u32[]{:S(2)}) collective-permute-start(bf16[256,128]{1,0:T(8,128)(2,1)} %own.1), channel_id=1, source_target_pairs={{0,1},{1,0},{2,3},{3,2},{4,5},{5,4},{6,7},{7,6},{8,9},{9,8},{10,11... | collective-permute-start | bytes 196616 | tf_op jit(solution)/shard_map/ppermute | solution.py:34
  4.0 1.9 %collective-permute-done.1.other = bf16[256,128]{1,0:T(8,128)(2,1)S(1)} collective-permute-done((bf16[256,128]{1,0:T(8,128)(2,1)}, bf16[256,128]{1,0:T(8,128)(2,1)S(1)}, u32[]{:S(2)}, u32[]{:S(2)}) %collective-permute-start.1) | collective-permute-done | bytes 65568 | tf_op jit(solution)/shard_map/ppermute | solution.py:34
  5.9 0.0 copy-start
  5.9 0.8 copy-done
  6.7 0.0 copy-start.1
  6.7 0.8 copy-done.1
  7.6 0.0 copy-start.2
  7.6 0.7 copy-done.2
  8.2 0.0 copy-start.3
  8.2 0.7 copy-done.3
  8.9 0.0 copy-start.4
  8.9 0.7 copy-done.4
  9.6 1.6 %scale.1 = bf16[2,256,128]{2,1,0:T(8,128)(2,1)S(1)} custom-call(f32[1,4,4096]{2,1,0:T(4,128)S(1)} %copy-done, s32[1,4,4096]{2,1,0:T(4,128)S(1)} %copy-done.1, s32[1,256]{1,0:T(1,128)S(1)} %copy-done.2, s32[1,256]{1,0:T(1,128)S(1)} %copy-done.3, s32[1,256]{1,0:T(1,128)S(1)} %copy-done.4, bf16[256,128]{1,0:T(8,128)(2,1)} %own.1, ...), custom_call_target="tpu_custom_call" | custom-call | flops 400000000 | bytes 300000 | tf_op jit(solution)/shard_map/scale/pallas_call | solution.py:83
  11.2 15.1 %all_gather.11.c0 = bf16[8,256,128]{2,1,0:T(8,128)(2,1)S(1)} all-gather(bf16[2,256,128]{2,1,0:T(8,128)(2,1)S(1)} %scale.1), channel_id=1, replica_groups={{0,192,384,576},{96,288,480,672},{1,193,385,577},{97,289,481,673},{2,19..., dimensions={0}, use_global_device_ids=true | all-gather | bytes 655360 | tf_op jit(solution)/shard_map/all_gather | solution.py:184
  26.3 4.5 %collective-permute-start.4 = (bf16[8,256,128]{2,1,0:T(8,128)(2,1)S(1)}, bf16[8,256,128]{2,1,0:T(8,128)(2,1)S(1)}, u32[]{:S(2)}, u32[]{:S(2)}) collective-permute-start(bf16[8,256,128]{2,1,0:T(8,128)(2,1)S(1)} %all_gather.11.c0), channel_id=1, source_target_pairs={{0,24},{1,25},{2,26},{3,27},{4,28},{5,29},{6,30},{7,31},{8,32},{9,... | collective-permute-start | bytes 1572872 | tf_op jit(solution)/shard_map/ppermute | solution.py:34
  30.8 4.4 %collective-permute-start.3 = (bf16[8,256,128]{2,1,0:T(8,128)(2,1)S(1)}, bf16[8,256,128]{2,1,0:T(8,128)(2,1)S(1)}, u32[]{:S(2)}, u32[]{:S(2)}) collective-permute-start(bf16[8,256,128]{2,1,0:T(8,128)(2,1)S(1)} %all_gather.11.c0), channel_id=1, source_target_pairs={{0,48},{1,49},{2,50},{3,51},{4,52},{5,53},{6,54},{7,55},{8,56},{9,... | collective-permute-start | bytes 1572872 | tf_op jit(solution)/shard_map/ppermute | solution.py:34
  35.1 3.1 %collective-permute-start.2 = (bf16[8,256,128]{2,1,0:T(8,128)(2,1)S(1)}, bf16[8,256,128]{2,1,0:T(8,128)(2,1)S(1)}, u32[]{:S(2)}, u32[]{:S(2)}) collective-permute-start(bf16[8,256,128]{2,1,0:T(8,128)(2,1)S(1)} %all_gather.11.c0), channel_id=1, source_target_pairs={{0,72},{1,73},{2,74},{3,75},{4,76},{5,77},{6,78},{7,79},{8,80},{9,... | collective-permute-start | bytes 1572872 | tf_op jit(solution)/shard_map/ppermute | solution.py:34
  38.2 14.3 %collective-permute-start = (bf16[256,128]{1,0:T(8,128)(2,1)}, bf16[256,128]{1,0:T(8,128)(2,1)S(1)}, u32[]{:S(2)}, u32[]{:S(2)}) collective-permute-start(bf16[256,128]{1,0:T(8,128)(2,1)} %own.1), channel_id=1, source_target_pairs={{0,18},{1,19},{2,44},{3,45},{4,10},{5,11},{6,36},{7,37},{8,16},{9,... | collective-permute-start | bytes 196616 | tf_op jit(solution)/shard_map/ppermute | solution.py:34
  52.6 0.1 stack.39.place
  52.7 1.4 %collective-permute-done = bf16[256,128]{1,0:T(8,128)(2,1)S(1)} collective-permute-done((bf16[256,128]{1,0:T(8,128)(2,1)}, bf16[256,128]{1,0:T(8,128)(2,1)S(1)}, u32[]{:S(2)}, u32[]{:S(2)}) %collective-permute-start) | collective-permute-done | bytes 65568 | tf_op jit(solution)/shard_map/ppermute | solution.py:34
  54.1 25.3 %all-gather = bf16[3072,128]{1,0:T(8,128)(2,1)S(1)} all-gather(bf16[256,128]{1,0:T(8,128)(2,1)S(1)} %collective-permute-done), channel_id=2, replica_groups={{0,2,4,6,8,10,12,14,16,18,20,22},{1,3,5,7,9,11,13,15,17,19,21,23},{24,2..., dimensions={0}, use_global_device_ids=true | all-gather | bytes 851968 | tf_op jit(solution)/shard_map/all_gather | solution.py:188
  79.4 0.0 collective-permute-done.4.c3
  79.4 0.0 collective-permute-done.3.c2
  79.4 0.0 collective-permute-done.2.c1
  79.4 1.2 shard_map.65
  80.6 13.1 %collective-permute-start.5 = (bf16[4,384,128]{2,1,0:T(8,128)(2,1)S(1)}, bf16[4,384,128]{2,1,0:T(8,128)(2,1)S(1)}, u32[]{:S(2)}, u32[]{:S(2)}) collective-permute-start(bf16[4,384,128]{2,1,0:T(8,128)(2,1)S(1)} %shard_map.65), channel_id=1, source_target_pairs={{0,96},{1,97},{2,98},{3,99},{4,100},{5,101},{6,102},{7,103},{8,104... | collective-permute-start | bytes 1179656 | tf_op jit(solution)/shard_map/ppermute | solution.py:34
  93.6 1.1 shard_map.64.keep
  94.8 0.2 collective-permute-done.5.taken
  95.0 0.6 total.1
  95.6 1.9 %collective-permute-start.6 = (bf16[384,128]{1,0:T(8,128)(2,1)S(1)}, bf16[384,128]{1,0:T(8,128)(2,1)S(1)}, u32[]{:S(2)}, u32[]{:S(2)}) collective-permute-start(bf16[384,128]{1,0:T(8,128)(2,1)S(1)} %get-tuple-element.9), channel_id=1, source_target_pairs={{0,0},{1,49},{2,2},{3,51},{4,4},{5,53},{6,6},{7,55},{8,8},{9,57},{... | collective-permute-start | bytes 294920 | tf_op jit(solution)/shard_map/ppermute | solution.py:34
  97.5 6.0 %collective-permute-start.7 = (bf16[384,128]{1,0:T(8,128)(2,1)S(1)}, bf16[384,128]{1,0:T(8,128)(2,1)S(1)}, u32[]{:S(2)}, u32[]{:S(2)}) collective-permute-start(bf16[384,128]{1,0:T(8,128)(2,1)S(1)} %get-tuple-element.10), channel_id=1, source_target_pairs={{0,24},{1,73},{2,26},{3,75},{4,28},{5,77},{6,30},{7,79},{8,32},{9,... | collective-permute-start | bytes 294920 | tf_op jit(solution)/shard_map/ppermute | solution.py:34
  103.6 4.0 %collective-permute-start.8 = (bf16[384,128]{1,0:T(8,128)(2,1)S(1)}, bf16[384,128]{1,0:T(8,128)(2,1)S(1)}, u32[]{:S(2)}, u32[]{:S(2)}) collective-permute-start(bf16[384,128]{1,0:T(8,128)(2,1)S(1)} %get-tuple-element.11), channel_id=1, source_target_pairs={{0,48},{1,1},{2,50},{3,3},{4,52},{5,5},{6,54},{7,7},{8,56},{9,9},{... | collective-permute-start | bytes 294920 | tf_op jit(solution)/shard_map/ppermute | solution.py:34
  107.6 2.5 %collective-permute-start.9 = (bf16[384,128]{1,0:T(8,128)(2,1)S(1)}, bf16[384,128]{1,0:T(8,128)(2,1)S(1)}, u32[]{:S(2)}, u32[]{:S(2)}) collective-permute-start(bf16[384,128]{1,0:T(8,128)(2,1)S(1)} %get-tuple-element.12), channel_id=1, source_target_pairs={{0,72},{1,25},{2,74},{3,27},{4,76},{5,29},{6,78},{7,31},{8,80},{9,... | collective-permute-start | bytes 294920 | tf_op jit(solution)/shard_map/ppermute | solution.py:34
  110.0 0.0 collective-permute-done.6.f0
  110.0 0.0 collective-permute-done.7.f1
  110.0 1.0 collective-permute-done.8.f2
  111.0 4.0 %collective-permute-done.9.f3 = bf16[384,128]{1,0:T(8,128)(2,1)S(1)} collective-permute-done((bf16[384,128]{1,0:T(8,128)(2,1)S(1)}, bf16[384,128]{1,0:T(8,128)(2,1)S(1)}, u32[]{:S(2)}, u32[]{:S(2)}) %collective-permute-start.9) | collective-permute-done | bytes 98336 | tf_op jit(solution)/shard_map/ppermute | solution.py:34
  115.0 1.5 %assemble.1 = f32[3,2,2,128,128]{4,3,2,1,0:T(8,128)} custom-call(s32[9]{0:T(128)S(1)} %stack.39.place, bf16[384,128]{1,0:T(8,128)(2,1)S(1)} %collective-permute-done.6.f0, bf16[384,128]{1,0:T(8,128)(2,1)S(1)} %collective-permute-done.7.f1, bf16[384,128]{1,0:T(8,128)(2,1)S(1)} %collective-permute-done.8.f2, bf16[384,128]{1,0:T(8,128)(2,1)S(1)} %collective-permute-done.9.f3), custom_call_target="tpu_custom_call" | custom-call | tf_op jit(solution)/shard_map/assemble/pallas_call | solution.py:160
Async XLA Ops:
  0.0 5.9 %collective-permute-start.1 = (bf16[256,128]{1,0:T(8,128)(2,1)}, bf16[256,128]{1,0:T(8,128)(2,1)S(1)}, u32[]{:S(2)}, u32[]{:S(2)}) collective-permute-start(bf16[256,128]{1,0:T(8,128)(2,1)} %own.1), channel_id=1, source_target_pairs={{0,1},{1,0},{2,3},{3,2},{4,5},{5,4},{6,7},{7,6},{8,9},{9,8},{10,11... | collective-permute-start | bytes 196616 | tf_op jit(solution)/shard_map/ppermute | solution.py:34
  5.9 0.8 copy-start
  6.7 0.8 copy-start.1
  7.6 0.7 copy-start.2
  8.2 0.7 copy-start.3
  8.9 0.7 copy-start.4
  26.3 53.1 %collective-permute-start.4 = (bf16[8,256,128]{2,1,0:T(8,128)(2,1)S(1)}, bf16[8,256,128]{2,1,0:T(8,128)(2,1)S(1)}, u32[]{:S(2)}, u32[]{:S(2)}) collective-permute-start(bf16[8,256,128]{2,1,0:T(8,128)(2,1)S(1)} %all_gather.11.c0), channel_id=1, source_target_pairs={{0,24},{1,25},{2,26},{3,27},{4,28},{5,29},{6,30},{7,31},{8,32},{9,... | collective-permute-start | bytes 1572872 | tf_op jit(solution)/shard_map/ppermute | solution.py:34
  30.8 48.6 %collective-permute-start.3 = (bf16[8,256,128]{2,1,0:T(8,128)(2,1)S(1)}, bf16[8,256,128]{2,1,0:T(8,128)(2,1)S(1)}, u32[]{:S(2)}, u32[]{:S(2)}) collective-permute-start(bf16[8,256,128]{2,1,0:T(8,128)(2,1)S(1)} %all_gather.11.c0), channel_id=1, source_target_pairs={{0,48},{1,49},{2,50},{3,51},{4,52},{5,53},{6,54},{7,55},{8,56},{9,... | collective-permute-start | bytes 1572872 | tf_op jit(solution)/shard_map/ppermute | solution.py:34
  35.1 44.3 %collective-permute-start.2 = (bf16[8,256,128]{2,1,0:T(8,128)(2,1)S(1)}, bf16[8,256,128]{2,1,0:T(8,128)(2,1)S(1)}, u32[]{:S(2)}, u32[]{:S(2)}) collective-permute-start(bf16[8,256,128]{2,1,0:T(8,128)(2,1)S(1)} %all_gather.11.c0), channel_id=1, source_target_pairs={{0,72},{1,73},{2,74},{3,75},{4,76},{5,77},{6,78},{7,79},{8,80},{9,... | collective-permute-start | bytes 1572872 | tf_op jit(solution)/shard_map/ppermute | solution.py:34
  38.2 15.9 %collective-permute-start = (bf16[256,128]{1,0:T(8,128)(2,1)}, bf16[256,128]{1,0:T(8,128)(2,1)S(1)}, u32[]{:S(2)}, u32[]{:S(2)}) collective-permute-start(bf16[256,128]{1,0:T(8,128)(2,1)} %own.1), channel_id=1, source_target_pairs={{0,18},{1,19},{2,44},{3,45},{4,10},{5,11},{6,36},{7,37},{8,16},{9,... | collective-permute-start | bytes 196616 | tf_op jit(solution)/shard_map/ppermute | solution.py:34
  80.6 14.4 %collective-permute-start.5 = (bf16[4,384,128]{2,1,0:T(8,128)(2,1)S(1)}, bf16[4,384,128]{2,1,0:T(8,128)(2,1)S(1)}, u32[]{:S(2)}, u32[]{:S(2)}) collective-permute-start(bf16[4,384,128]{2,1,0:T(8,128)(2,1)S(1)} %shard_map.65), channel_id=1, source_target_pairs={{0,96},{1,97},{2,98},{3,99},{4,100},{5,101},{6,102},{7,103},{8,104... | collective-permute-start | bytes 1179656 | tf_op jit(solution)/shard_map/ppermute | solution.py:34
  95.6 14.5 %collective-permute-start.6 = (bf16[384,128]{1,0:T(8,128)(2,1)S(1)}, bf16[384,128]{1,0:T(8,128)(2,1)S(1)}, u32[]{:S(2)}, u32[]{:S(2)}) collective-permute-start(bf16[384,128]{1,0:T(8,128)(2,1)S(1)} %get-tuple-element.9), channel_id=1, source_target_pairs={{0,0},{1,49},{2,2},{3,51},{4,4},{5,53},{6,6},{7,55},{8,8},{9,57},{... | collective-permute-start | bytes 294920 | tf_op jit(solution)/shard_map/ppermute | solution.py:34
  97.5 12.5 %collective-permute-start.7 = (bf16[384,128]{1,0:T(8,128)(2,1)S(1)}, bf16[384,128]{1,0:T(8,128)(2,1)S(1)}, u32[]{:S(2)}, u32[]{:S(2)}) collective-permute-start(bf16[384,128]{1,0:T(8,128)(2,1)S(1)} %get-tuple-element.10), channel_id=1, source_target_pairs={{0,24},{1,73},{2,26},{3,75},{4,28},{5,77},{6,30},{7,79},{8,32},{9,... | collective-permute-start | bytes 294920 | tf_op jit(solution)/shard_map/ppermute | solution.py:34
  103.6 7.4 %collective-permute-start.8 = (bf16[384,128]{1,0:T(8,128)(2,1)S(1)}, bf16[384,128]{1,0:T(8,128)(2,1)S(1)}, u32[]{:S(2)}, u32[]{:S(2)}) collective-permute-start(bf16[384,128]{1,0:T(8,128)(2,1)S(1)} %get-tuple-element.11), channel_id=1, source_target_pairs={{0,48},{1,1},{2,50},{3,3},{4,52},{5,5},{6,54},{7,7},{8,56},{9,9},{... | collective-permute-start | bytes 294920 | tf_op jit(solution)/shard_map/ppermute | solution.py:34
  107.6 7.5 %collective-permute-start.9 = (bf16[384,128]{1,0:T(8,128)(2,1)S(1)}, bf16[384,128]{1,0:T(8,128)(2,1)S(1)}, u32[]{:S(2)}, u32[]{:S(2)}) collective-permute-start(bf16[384,128]{1,0:T(8,128)(2,1)S(1)} %get-tuple-element.12), channel_id=1, source_target_pairs={{0,72},{1,25},{2,74},{3,27},{4,76},{5,29},{6,78},{7,31},{8,80},{9,... | collective-permute-start | bytes 294920 | tf_op jit(solution)/shard_map/ppermute | solution.py:34

commit v7 on v6

--- a/solution.py
+++ b/solution.py
@@ -39,7 +39,6 @@
     return x, k, 2 * side + a, NEAR[(h - x) % H][j] + 6 * side + a, l
 
 
-H_GROUPS = [[h * K + k for h in range(H)] for k in range(K)]
 Z_GROUPS = [[x * Z * L + z * L + l for z in range(Z)] for x in range(X) for l in range(L)]
 
 
@@ -84,7 +83,6 @@
         scale_kernel,
         out_shape=jax.ShapeDtypeStruct((2,) + own.shape, jnp.bfloat16),
         scratch_shapes=[pltpu.VMEM((entries, WIDTH), jnp.float32)] * 2,
-        compiler_params=pltpu.CompilerParams(vmem_limit_bytes=8 * 2**20),
         cost_estimate=pl.CostEstimate(flops=4 * 10**8, bytes_accessed=3 * 10**5, transcendentals=0),
         name="scale",
     )(energy, occupied, first, second, kpoint, own, other)
@@ -94,7 +92,7 @@
     which = place[side]
 
     def columns(c, s):
-        return c[((place[8] + s) % H) * L + which]
+        return c[s * L + which]
 
     left = jnp.concatenate(
         [
@@ -173,7 +171,6 @@
     place = jnp.stack(
         [1 - k, k, 6 * (x // 2) + x % 2, 2 * l]
         + [(x - 2 * k - r) % X for r in range(X)]
-        + [pool // K]
     ).astype(jnp.int32)
 
     other = move(pair_matrix, lambda h, k, x, z, l: (h, k, x, z, 1 - l))
@@ -181,7 +178,10 @@
     scaled = scaled_blocks(
         band_energy, occupation, pair_first, pair_second, pair_kpoint, pair_matrix, other
     )
-    both = lax.all_gather(scaled, "pool", axis=0, tiled=True, axis_index_groups=H_GROUPS)
+    around = [scaled]
+    for s in range(1, H):
+        around.append(move(scaled, lambda h, k, x, z, l, s=s: (h - s, k, x, z, l)))
+    both = jnp.concatenate(around, axis=0)
     columns = [both]
     for s in range(1, X):
         columns.append(move(both, lambda h, k, x, z, l, s=s: (h, k, x - s, z, l)))

time: 117 us -> 119 us (1.017)
  blocking collectives: 40.4 us -> 25.6 us
  starting transfers between devices: 57.7 us -> 71.1 us
  waiting for transfers between devices: 8.4 us -> 12.8 us
  local copies, waits for them, and re-layouts: 3.8 us -> 0.71 us
    all_gather x1 -> x0, blocking collectives: 15.1 us -> none  [blocks(): lax.all_gather(scaled, 'pool', axis=0, tiled=True, axis_index_groups=H_GR...]
    ppermute x10 -> x13, starting transfers between devices: 57.7 us -> 71.1 us  [move(): return lax.ppermute(value, AXES, table(f))]
    ppermute x10 -> x13, waiting for transfers between devices: 8.4 us -> 12.8 us  [move(): return lax.ppermute(value, AXES, table(f))]
    unnamed x10 -> x4, local copies, waits for them, and re-layouts: 3.71 us -> 0.62 us
  transfers between devices with their start and end apart: 10 -> 13, of which waited for: 5 -> 6; matrix products, arithmetic and copies ran while one was open for 0% -> 0% of each run, Pallas kernels for 1% -> 1%
where the time goes in v7:
time: 119 us; the launch traced here: 118 us
  starting transfers between devices  71.1 us (60%)
  blocking collectives  25.6 us (22%)
  waiting for transfers between devices  12.8 us (11%)
  Pallas kernels  6.81 us (6%)
    ppermute x13, starting transfers between devices, move(): return lax.ppermute(value, AXES, table(f))  71.1 us
    all_gather x1, blocking collectives, blocks(): rows = lax.all_gather(sent, 'col', axis=0, axis_index_groups=Z_GROUPS)  25.6 us
    ppermute x13, waiting for transfers between devices, move(): return lax.ppermute(value, AXES, table(f))  12.8 us
    pallas_call x1, Pallas kernels, scaled_blocks(): pl.pallas_call(scale_kernel, out_shape=jax.ShapeDtypeStruct((2,) + own.sh...  2.4 us
  transfers between devices with their start and end apart: 13, of which 6 were waited for; matrix products, arithmetic and copies ran while one was open for 0% of the time, Pallas kernels for 1%

profile of v7, /device:TPU:1, one launch (start us, length us, event | category | flops | bytes accessed | tf_op | source)
XLA Modules:
  0.0 118.3 jit_solution(13141623097955569368)
XLA Ops:
  0.0 4.0 %collective-permute-start.1 = (bf16[256,128]{1,0:T(8,128)(2,1)}, bf16[256,128]{1,0:T(8,128)(2,1)S(1)}, u32[]{:S(2)}, u32[]{:S(2)}) collective-permute-start(bf16[256,128]{1,0:T(8,128)(2,1)} %own.1), channel_id=1, source_target_pairs={{0,1},{1,0},{2,3},{3,2},{4,5},{5,4},{6,7},{7,6},{8,9},{9,8},{10,11... | collective-permute-start | bytes 196616 | tf_op jit(solution)/shard_map/ppermute | solution.py:34
  4.0 1.9 %collective-permute-done.1.other = bf16[256,128]{1,0:T(8,128)(2,1)S(1)} collective-permute-done((bf16[256,128]{1,0:T(8,128)(2,1)}, bf16[256,128]{1,0:T(8,128)(2,1)S(1)}, u32[]{:S(2)}, u32[]{:S(2)}) %collective-permute-start.1) | collective-permute-done | bytes 65568 | tf_op jit(solution)/shard_map/ppermute | solution.py:34
  5.9 0.0 copy-start.1
  5.9 0.6 copy-done.1
  6.5 2.4 %scale.1 = bf16[2,256,128]{2,1,0:T(8,128)(2,1)} custom-call(f32[1,4,4096]{2,1,0:T(4,128)} %energy.1, s32[1,4,4096]{2,1,0:T(4,128)} %occupied.1, s32[1,256]{1,0:T(1,128)} %first.1, s32[1,256]{1,0:T(1,128)} %second.1, s32[1,256]{1,0:T(1,128)} %kpoint.1, bf16[256,128]{1,0:T(8,128)(2,1)} %own.1, bf16[256,128]{1,0:T(8,128)(2,1)} %copy-done.1), custom_call_target="tpu_custom_call" | custom-call | flops 400000000 | bytes 300000 | tf_op jit(solution)/shard_map/scale/pallas_call | solution.py:82
  8.9 0.0 copy-start
  8.9 4.5 %collective-permute-start.4 = (bf16[2,256,128]{2,1,0:T(8,128)(2,1)}, bf16[2,256,128]{2,1,0:T(8,128)(2,1)S(1)}, u32[]{:S(2)}, u32[]{:S(2)}) collective-permute-start(bf16[2,256,128]{2,1,0:T(8,128)(2,1)} %scale.1), channel_id=1, source_target_pairs={{0,192},{1,193},{2,194},{3,195},{4,196},{5,197},{6,198},{7,199},{8... | collective-permute-start | bytes 393224 | tf_op jit(solution)/shard_map/ppermute | solution.py:34
  13.4 5.7 %collective-permute-start.3 = (bf16[2,256,128]{2,1,0:T(8,128)(2,1)}, bf16[2,256,128]{2,1,0:T(8,128)(2,1)S(1)}, u32[]{:S(2)}, u32[]{:S(2)}) collective-permute-start(bf16[2,256,128]{2,1,0:T(8,128)(2,1)} %scale.1), channel_id=1, source_target_pairs={{0,384},{1,385},{2,386},{3,387},{4,388},{5,389},{6,390},{7,391},{8... | collective-permute-start | bytes 393224 | tf_op jit(solution)/shard_map/ppermute | solution.py:34
  19.1 5.0 %collective-permute-start.2 = (bf16[2,256,128]{2,1,0:T(8,128)(2,1)}, bf16[2,256,128]{2,1,0:T(8,128)(2,1)S(1)}, u32[]{:S(2)}, u32[]{:S(2)}) collective-permute-start(bf16[2,256,128]{2,1,0:T(8,128)(2,1)} %scale.1), channel_id=1, source_target_pairs={{0,576},{1,577},{2,578},{3,579},{4,580},{5,581},{6,582},{7,583},{8... | collective-permute-start | bytes 393224 | tf_op jit(solution)/shard_map/ppermute | solution.py:34
  24.0 0.0 collective-permute-done.4
  24.1 1.0 collective-permute-done.3
  25.1 3.4 %collective-permute-done.2 = bf16[2,256,128]{2,1,0:T(8,128)(2,1)S(1)} collective-permute-done((bf16[2,256,128]{2,1,0:T(8,128)(2,1)}, bf16[2,256,128]{2,1,0:T(8,128)(2,1)S(1)}, u32[]{:S(2)}, u32[]{:S(2)}) %collective-permute-start.2) | collective-permute-done | bytes 131104 | tf_op jit(solution)/shard_map/ppermute | solution.py:34
  28.5 1.0 pad_maximum_fusion.c0
  29.5 7.4 %collective-permute-start.7 = (bf16[8,256,128]{2,1,0:T(8,128)(2,1)S(1)}, bf16[8,256,128]{2,1,0:T(8,128)(2,1)S(1)}, u32[]{:S(2)}, u32[]{:S(2)}) collective-permute-start(bf16[8,256,128]{2,1,0:T(8,128)(2,1)S(1)} %pad_maximum_fusion.c0), channel_id=1, source_target_pairs={{0,24},{1,25},{2,26},{3,27},{4,28},{5,29},{6,30},{7,31},{8,32},{9,... | collective-permute-start | bytes 1572872 | tf_op jit(solution)/shard_map/ppermute | solution.py:34
  36.8 4.4 %collective-permute-start.6 = (bf16[8,256,128]{2,1,0:T(8,128)(2,1)S(1)}, bf16[8,256,128]{2,1,0:T(8,128)(2,1)S(1)}, u32[]{:S(2)}, u32[]{:S(2)}) collective-permute-start(bf16[8,256,128]{2,1,0:T(8,128)(2,1)S(1)} %pad_maximum_fusion.c0), channel_id=1, source_target_pairs={{0,48},{1,49},{2,50},{3,51},{4,52},{5,53},{6,54},{7,55},{8,56},{9,... | collective-permute-start | bytes 1572872 | tf_op jit(solution)/shard_map/ppermute | solution.py:34
  41.2 3.1 %collective-permute-start.5 = (bf16[8,256,128]{2,1,0:T(8,128)(2,1)S(1)}, bf16[8,256,128]{2,1,0:T(8,128)(2,1)S(1)}, u32[]{:S(2)}, u32[]{:S(2)}) collective-permute-start(bf16[8,256,128]{2,1,0:T(8,128)(2,1)S(1)} %pad_maximum_fusion.c0), channel_id=1, source_target_pairs={{0,72},{1,73},{2,74},{3,75},{4,76},{5,77},{6,78},{7,79},{8,80},{9,... | collective-permute-start | bytes 1572872 | tf_op jit(solution)/shard_map/ppermute | solution.py:34
  44.3 0.0 copy-done
  44.3 14.3 %collective-permute-start = (bf16[256,128]{1,0:T(8,128)(2,1)S(1)}, bf16[256,128]{1,0:T(8,128)(2,1)S(1)}, u32[]{:S(2)}, u32[]{:S(2)}) collective-permute-start(bf16[256,128]{1,0:T(8,128)(2,1)S(1)} %copy-done), channel_id=1, source_target_pairs={{0,18},{1,19},{2,44},{3,45},{4,10},{5,11},{6,36},{7,37},{8,16},{9,... | collective-permute-start | bytes 196616 | tf_op jit(solution)/shard_map/ppermute | solution.py:34
  58.7 0.1 stack.35.place
  58.8 1.1 collective-permute-done
  59.9 25.6 %all-gather = bf16[3072,128]{1,0:T(8,128)(2,1)S(1)} all-gather(bf16[256,128]{1,0:T(8,128)(2,1)S(1)} %collective-permute-done), channel_id=2, replica_groups={{0,2,4,6,8,10,12,14,16,18,20,22},{1,3,5,7,9,11,13,15,17,19,21,23},{24,2..., dimensions={0}, use_global_device_ids=true | all-gather | bytes 851968 | tf_op jit(solution)/shard_map/all_gather | solution.py:188
  85.5 0.0 collective-permute-done.7.c3
  85.5 0.0 collective-permute-done.6.c2
  85.5 0.0 collective-permute-done.5.c1
  85.5 1.2 shard_map.65
  86.7 8.5 %collective-permute-start.8 = (bf16[4,384,128]{2,1,0:T(8,128)(2,1)S(1)}, bf16[4,384,128]{2,1,0:T(8,128)(2,1)S(1)}, u32[]{:S(2)}, u32[]{:S(2)}) collective-permute-start(bf16[4,384,128]{2,1,0:T(8,128)(2,1)S(1)} %shard_map.65), channel_id=1, source_target_pairs={{0,96},{1,97},{2,98},{3,99},{4,100},{5,101},{6,102},{7,103},{8,104... | collective-permute-start | bytes 1179656 | tf_op jit(solution)/shard_map/ppermute | solution.py:34
  95.2 1.2 shard_map.64.keep
  96.4 0.2 collective-permute-done.8.taken
  96.5 0.6 total.1
  97.1 1.9 %collective-permute-start.9 = (bf16[384,128]{1,0:T(8,128)(2,1)S(1)}, bf16[384,128]{1,0:T(8,128)(2,1)S(1)}, u32[]{:S(2)}, u32[]{:S(2)}) collective-permute-start(bf16[384,128]{1,0:T(8,128)(2,1)S(1)} %get-tuple-element.9), channel_id=1, source_target_pairs={{0,0},{1,49},{2,2},{3,51},{4,4},{5,53},{6,6},{7,55},{8,8},{9,57},{... | collective-permute-start | bytes 294920 | tf_op jit(solution)/shard_map/ppermute | solution.py:34
  99.1 3.9 %collective-permute-start.10 = (bf16[384,128]{1,0:T(8,128)(2,1)S(1)}, bf16[384,128]{1,0:T(8,128)(2,1)S(1)}, u32[]{:S(2)}, u32[]{:S(2)}) collective-permute-start(bf16[384,128]{1,0:T(8,128)(2,1)S(1)} %get-tuple-element.10), channel_id=1, source_target_pairs={{0,24},{1,73},{2,26},{3,75},{4,28},{5,77},{6,30},{7,79},{8,32},{9,... | collective-permute-start | bytes 294920 | tf_op jit(solution)/shard_map/ppermute | solution.py:34
  102.9 6.3 %collective-permute-start.11 = (bf16[384,128]{1,0:T(8,128)(2,1)S(1)}, bf16[384,128]{1,0:T(8,128)(2,1)S(1)}, u32[]{:S(2)}, u32[]{:S(2)}) collective-permute-start(bf16[384,128]{1,0:T(8,128)(2,1)S(1)} %get-tuple-element.11), channel_id=1, source_target_pairs={{0,48},{1,1},{2,50},{3,3},{4,52},{5,5},{6,54},{7,7},{8,56},{9,9},{... | collective-permute-start | bytes 294920 | tf_op jit(solution)/shard_map/ppermute | solution.py:34
  109.3 2.2 %collective-permute-start.12 = (bf16[384,128]{1,0:T(8,128)(2,1)S(1)}, bf16[384,128]{1,0:T(8,128)(2,1)S(1)}, u32[]{:S(2)}, u32[]{:S(2)}) collective-permute-start(bf16[384,128]{1,0:T(8,128)(2,1)S(1)} %get-tuple-element.12), channel_id=1, source_target_pairs={{0,72},{1,25},{2,74},{3,27},{4,76},{5,29},{6,78},{7,31},{8,80},{9,... | collective-permute-start | bytes 294920 | tf_op jit(solution)/shard_map/ppermute | solution.py:34
  111.5 0.0 collective-permute-done.9.f0
  111.5 0.0 collective-permute-done.10.f1
  111.5 0.0 collective-permute-done.11.f2
  111.5 5.2 %collective-permute-done.12.f3 = bf16[384,128]{1,0:T(8,128)(2,1)S(1)} collective-permute-done((bf16[384,128]{1,0:T(8,128)(2,1)S(1)}, bf16[384,128]{1,0:T(8,128)(2,1)S(1)}, u32[]{:S(2)}, u32[]{:S(2)}) %collective-permute-start.12) | collective-permute-done | bytes 98336 | tf_op jit(solution)/shard_map/ppermute | solution.py:34
  116.8 1.5 %assemble.1 = f32[3,2,2,128,128]{4,3,2,1,0:T(8,128)} custom-call(s32[8]{0:T(128)S(1)} %stack.35.place, bf16[384,128]{1,0:T(8,128)(2,1)S(1)} %collective-permute-done.9.f0, bf16[384,128]{1,0:T(8,128)(2,1)S(1)} %collective-permute-done.10.f1, bf16[384,128]{1,0:T(8,128)(2,1)S(1)} %collective-permute-done.11.f2, bf16[384,128]{1,0:T(8,128)(2,1)S(1)} %collective-permute-done.12.f3), custom_call_target="tpu_custom_call" | custom-call | tf_op jit(solution)/shard_map/assemble/pallas_call | solution.py:158
Async XLA Ops:
  0.0 5.9 %collective-permute-start.1 = (bf16[256,128]{1,0:T(8,128)(2,1)}, bf16[256,128]{1,0:T(8,128)(2,1)S(1)}, u32[]{:S(2)}, u32[]{:S(2)}) collective-permute-start(bf16[256,128]{1,0:T(8,128)(2,1)} %own.1), channel_id=1, source_target_pairs={{0,1},{1,0},{2,3},{3,2},{4,5},{5,4},{6,7},{7,6},{8,9},{9,8},{10,11... | collective-permute-start | bytes 196616 | tf_op jit(solution)/shard_map/ppermute | solution.py:34
  5.9 0.6 copy-start.1
  8.9 35.4 %copy-start = (bf16[256,128]{1,0:T(8,128)(2,1)S(1)}, bf16[256,128]{1,0:T(8,128)(2,1)}, u32[]{:S(2)}) copy-start(bf16[256,128]{1,0:T(8,128)(2,1)} %own.1) | copy-start | bytes 196612
  8.9 15.1 %collective-permute-start.4 = (bf16[2,256,128]{2,1,0:T(8,128)(2,1)}, bf16[2,256,128]{2,1,0:T(8,128)(2,1)S(1)}, u32[]{:S(2)}, u32[]{:S(2)}) collective-permute-start(bf16[2,256,128]{2,1,0:T(8,128)(2,1)} %scale.1), channel_id=1, source_target_pairs={{0,192},{1,193},{2,194},{3,195},{4,196},{5,197},{6,198},{7,199},{8... | collective-permute-start | bytes 393224 | tf_op jit(solution)/shard_map/ppermute | solution.py:34
  13.4 11.7 %collective-permute-start.3 = (bf16[2,256,128]{2,1,0:T(8,128)(2,1)}, bf16[2,256,128]{2,1,0:T(8,128)(2,1)S(1)}, u32[]{:S(2)}, u32[]{:S(2)}) collective-permute-start(bf16[2,256,128]{2,1,0:T(8,128)(2,1)} %scale.1), channel_id=1, source_target_pairs={{0,384},{1,385},{2,386},{3,387},{4,388},{5,389},{6,390},{7,391},{8... | collective-permute-start | bytes 393224 | tf_op jit(solution)/shard_map/ppermute | solution.py:34
  19.1 9.5 %collective-permute-start.2 = (bf16[2,256,128]{2,1,0:T(8,128)(2,1)}, bf16[2,256,128]{2,1,0:T(8,128)(2,1)S(1)}, u32[]{:S(2)}, u32[]{:S(2)}) collective-permute-start(bf16[2,256,128]{2,1,0:T(8,128)(2,1)} %scale.1), channel_id=1, source_target_pairs={{0,576},{1,577},{2,578},{3,579},{4,580},{5,581},{6,582},{7,583},{8... | collective-permute-start | bytes 393224 | tf_op jit(solution)/shard_map/ppermute | solution.py:34
  29.5 56.0 %collective-permute-start.7 = (bf16[8,256,128]{2,1,0:T(8,128)(2,1)S(1)}, bf16[8,256,128]{2,1,0:T(8,128)(2,1)S(1)}, u32[]{:S(2)}, u32[]{:S(2)}) collective-permute-start(bf16[8,256,128]{2,1,0:T(8,128)(2,1)S(1)} %pad_maximum_fusion.c0), channel_id=1, source_target_pairs={{0,24},{1,25},{2,26},{3,27},{4,28},{5,29},{6,30},{7,31},{8,32},{9,... | collective-permute-start | bytes 1572872 | tf_op jit(solution)/shard_map/ppermute | solution.py:34
  36.8 48.6 %collective-permute-start.6 = (bf16[8,256,128]{2,1,0:T(8,128)(2,1)S(1)}, bf16[8,256,128]{2,1,0:T(8,128)(2,1)S(1)}, u32[]{:S(2)}, u32[]{:S(2)}) collective-permute-start(bf16[8,256,128]{2,1,0:T(8,128)(2,1)S(1)} %pad_maximum_fusion.c0), channel_id=1, source_target_pairs={{0,48},{1,49},{2,50},{3,51},{4,52},{5,53},{6,54},{7,55},{8,56},{9,... | collective-permute-start | bytes 1572872 | tf_op jit(solution)/shard_map/ppermute | solution.py:34
  41.2 44.3 %collective-permute-start.5 = (bf16[8,256,128]{2,1,0:T(8,128)(2,1)S(1)}, bf16[8,256,128]{2,1,0:T(8,128)(2,1)S(1)}, u32[]{:S(2)}, u32[]{:S(2)}) collective-permute-start(bf16[8,256,128]{2,1,0:T(8,128)(2,1)S(1)} %pad_maximum_fusion.c0), channel_id=1, source_target_pairs={{0,72},{1,73},{2,74},{3,75},{4,76},{5,77},{6,78},{7,79},{8,80},{9,... | collective-permute-start | bytes 1572872 | tf_op jit(solution)/shard_map/ppermute | solution.py:34
  44.3 15.6 %collective-permute-start = (bf16[256,128]{1,0:T(8,128)(2,1)S(1)}, bf16[256,128]{1,0:T(8,128)(2,1)S(1)}, u32[]{:S(2)}, u32[]{:S(2)}) collective-permute-start(bf16[256,128]{1,0:T(8,128)(2,1)S(1)} %copy-done), channel_id=1, source_target_pairs={{0,18},{1,19},{2,44},{3,45},{4,10},{5,11},{6,36},{7,37},{8,16},{9,... | collective-permute-start | bytes 196616 | tf_op jit(solution)/shard_map/ppermute | solution.py:34
  86.7 9.9 %collective-permute-start.8 = (bf16[4,384,128]{2,1,0:T(8,128)(2,1)S(1)}, bf16[4,384,128]{2,1,0:T(8,128)(2,1)S(1)}, u32[]{:S(2)}, u32[]{:S(2)}) collective-permute-start(bf16[4,384,128]{2,1,0:T(8,128)(2,1)S(1)} %shard_map.65), channel_id=1, source_target_pairs={{0,96},{1,97},{2,98},{3,99},{4,100},{5,101},{6,102},{7,103},{8,104... | collective-permute-start | bytes 1179656 | tf_op jit(solution)/shard_map/ppermute | solution.py:34
  97.1 14.4 %collective-permute-start.9 = (bf16[384,128]{1,0:T(8,128)(2,1)S(1)}, bf16[384,128]{1,0:T(8,128)(2,1)S(1)}, u32[]{:S(2)}, u32[]{:S(2)}) collective-permute-start(bf16[384,128]{1,0:T(8,128)(2,1)S(1)} %get-tuple-element.9), channel_id=1, source_target_pairs={{0,0},{1,49},{2,2},{3,51},{4,4},{5,53},{6,6},{7,55},{8,8},{9,57},{... | collective-permute-start | bytes 294920 | tf_op jit(solution)/shard_map/ppermute | solution.py:34
  99.1 12.4 %collective-permute-start.10 = (bf16[384,128]{1,0:T(8,128)(2,1)S(1)}, bf16[384,128]{1,0:T(8,128)(2,1)S(1)}, u32[]{:S(2)}, u32[]{:S(2)}) collective-permute-start(bf16[384,128]{1,0:T(8,128)(2,1)S(1)} %get-tuple-element.10), channel_id=1, source_target_pairs={{0,24},{1,73},{2,26},{3,75},{4,28},{5,77},{6,30},{7,79},{8,32},{9,... | collective-permute-start | bytes 294920 | tf_op jit(solution)/shard_map/ppermute | solution.py:34
  102.9 8.6 %collective-permute-start.11 = (bf16[384,128]{1,0:T(8,128)(2,1)S(1)}, bf16[384,128]{1,0:T(8,128)(2,1)S(1)}, u32[]{:S(2)}, u32[]{:S(2)}) collective-permute-start(bf16[384,128]{1,0:T(8,128)(2,1)S(1)} %get-tuple-element.11), channel_id=1, source_target_pairs={{0,48},{1,1},{2,50},{3,3},{4,52},{5,5},{6,54},{7,7},{8,56},{9,9},{... | collective-permute-start | bytes 294920 | tf_op jit(solution)/shard_map/ppermute | solution.py:34
  109.3 7.5 %collective-permute-start.12 = (bf16[384,128]{1,0:T(8,128)(2,1)S(1)}, bf16[384,128]{1,0:T(8,128)(2,1)S(1)}, u32[]{:S(2)}, u32[]{:S(2)}) collective-permute-start(bf16[384,128]{1,0:T(8,128)(2,1)S(1)} %get-tuple-element.12), channel_id=1, source_target_pairs={{0,72},{1,25},{2,74},{3,27},{4,76},{5,29},{6,78},{7,31},{8,80},{9,... | collective-permute-start | bytes 294920 | tf_op jit(solution)/shard_map/ppermute | solution.py:34

commit v8 on v4

--- a/solution.py
+++ b/solution.py
@@ -32,6 +32,13 @@
 
 def move(value, f):
     return lax.ppermute(value, AXES, table(f))
+
+
+ROUNDS = (2, 1, 3, 0)
+
+
+def turn(x, l):
+    return l * (3 - 2 * (x % 2))
 
 
 def spread(h, k, x, z, l):
@@ -121,7 +128,7 @@
 
 def total_kernel(place, keep, taken, *outs):
     for r, out in enumerate(outs):
-        i = (r + place[3]) % X
+        i = (ROUNDS[r] + place[3]) % X
         out[...] = (keep[i] + taken[i].astype(jnp.float32)).astype(out.dtype)
 
 
@@ -141,10 +148,12 @@
     copies = []
     for i, piece in enumerate(pieces):
         t = place[4 + start + i]
+        b = t // 2
+        a = (t + b) % 2
         for j in range(3):
             wide[i, j] = piece[j * WIDTH : (j + 1) * WIDTH, :].astype(jnp.float32)
             copies.append(
-                pltpu.make_async_copy(wide.at[i, j], out.at[j, t % 2, t // 2], sems.at[i, j])
+                pltpu.make_async_copy(wide.at[i, j], out.at[j, a, b], sems.at[i, j])
             )
             copies[-1].start()
     for copy in copies:
@@ -172,8 +181,8 @@
     pool, col = lax.axis_index("pool"), lax.axis_index("col")
     k, x, l = pool % K, col // (Z * L), col % L
     place = jnp.stack(
-        [1 - k, k, 6 * (x // 2) + x % 2, 2 * l]
-        + [(x - 2 * k - r) % X for r in range(X)]
+        [1 - k, k, 6 * (x // 2) + x % 2, turn(x, l)]
+        + [(x - 2 * k - r) % X for r in ROUNDS]
     ).astype(jnp.int32)
 
     around = []
@@ -200,7 +209,9 @@
         home.append(
             move(
                 total[r],
-                lambda h, k, x, z, l, r=r: (h, x // 2, x + r + 2 * l, z, l ^ k),
+                lambda h, k, x, z, l, r=r: (
+                    h, x // 2, x + ROUNDS[r] + turn(x, l), z, l ^ k
+                ),
             )
         )
     most = settle(place, 0, home[:3])

time: 116 us -> 117 us (level)
  no operation moved by 1% of the time
where the time goes in v8:
time: 117 us; the launch traced here: 116 us
  starting transfers between devices  70.1 us (60%)
  blocking collectives  24.8 us (21%)
  waiting for transfers between devices  12 us (10%)
  Pallas kernels  7.97 us (7%)
    ppermute x13, starting transfers between devices, move(): return lax.ppermute(value, AXES, table(f))  70.1 us
    all_gather x1, blocking collectives, blocks(): rows = lax.all_gather(sent, 'col', axis=0, axis_index_groups=Z_GROUPS)  24.8 us
    ppermute x13, waiting for transfers between devices, move(): return lax.ppermute(value, AXES, table(f))  12 us
    pallas_call x2, Pallas kernels, settle(): pl.pallas_call(functools.partial(settle_kernel, start, count), out_shape=...  2.68 us
    pallas_call x1, Pallas kernels, scaled_block(): pl.pallas_call(scale_kernel, out_shape=jax.ShapeDtypeStruct(block.shape,...  2.36 us
  transfers between devices with their start and end apart: 13, of which 6 were waited for; matrix products, arithmetic and copies ran while one was open for 1% of the time, Pallas kernels for 4%

profile of v8, /device:TPU:1, one launch (start us, length us, event | category | flops | bytes accessed | tf_op | source)
XLA Modules:
  0.0 116.2 jit_solution(17569990667207103052)
XLA Ops:
  0.0 8.3 %collective-permute-start.2 = (bf16[256,128]{1,0:T(8,128)(2,1)}, bf16[256,128]{1,0:T(8,128)(2,1)S(1)}, u32[]{:S(2)}, u32[]{:S(2)}) collective-permute-start(bf16[256,128]{1,0:T(8,128)(2,1)} %block.1), channel_id=1, source_target_pairs={{0,384},{1,385},{2,386},{3,387},{4,388},{5,389},{6,390},{7,391},{8... | collective-permute-start | bytes 196616 | tf_op jit(solution)/shard_map/ppermute | solution.py:34
  8.3 2.0 %collective-permute-start.1 = (bf16[256,128]{1,0:T(8,128)(2,1)}, bf16[256,128]{1,0:T(8,128)(2,1)S(1)}, u32[]{:S(2)}, u32[]{:S(2)}) collective-permute-start(bf16[256,128]{1,0:T(8,128)(2,1)} %block.1), channel_id=1, source_target_pairs={{0,576},{1,577},{2,578},{3,579},{4,580},{5,581},{6,582},{7,583},{8... | collective-permute-start | bytes 196616 | tf_op jit(solution)/shard_map/ppermute | solution.py:34
  10.2 4.2 %collective-permute-start.3 = (bf16[256,128]{1,0:T(8,128)(2,1)}, bf16[256,128]{1,0:T(8,128)(2,1)S(1)}, u32[]{:S(2)}, u32[]{:S(2)}) collective-permute-start(bf16[256,128]{1,0:T(8,128)(2,1)} %block.1), channel_id=1, source_target_pairs={{0,192},{1,193},{2,194},{3,195},{4,196},{5,197},{6,198},{7,199},{8... | collective-permute-start | bytes 196616 | tf_op jit(solution)/shard_map/ppermute | solution.py:34
  14.5 0.9 constant_dynamic-update-slice_fusion.3
  15.3 0.0 collective-permute-done.1
  15.3 0.0 collective-permute-done.2
  15.4 2.4 %collective-permute-done.3 = bf16[256,128]{1,0:T(8,128)(2,1)S(1)} collective-permute-done((bf16[256,128]{1,0:T(8,128)(2,1)}, bf16[256,128]{1,0:T(8,128)(2,1)S(1)}, u32[]{:S(2)}, u32[]{:S(2)}) %collective-permute-start.3) | collective-permute-done | bytes 65568 | tf_op jit(solution)/shard_map/ppermute | solution.py:34
  17.8 3.7 %collective-permute-start.4 = (bf16[1024,128]{1,0:T(8,128)(2,1)S(1)}, bf16[1024,128]{1,0:T(8,128)(2,1)S(1)}, u32[]{:S(2)}, u32[]{:S(2)}) collective-permute-start(bf16[1024,128]{1,0:T(8,128)(2,1)S(1)} %constant_dynamic-update-slice_fusion), channel_id=1, source_target_pairs={{0,1},{1,0},{2,3},{3,2},{4,5},{5,4},{6,7},{7,6},{8,9},{9,8},{10,11... | collective-permute-start | bytes 786440 | tf_op jit(solution)/shard_map/ppermute | solution.py:34
  21.5 4.0 %collective-permute-done.4 = bf16[1024,128]{1,0:T(8,128)(2,1)S(1)} collective-permute-done((bf16[1024,128]{1,0:T(8,128)(2,1)S(1)}, bf16[1024,128]{1,0:T(8,128)(2,1)S(1)}, u32[]{:S(2)}, u32[]{:S(2)}) %collective-permute-start.4) | collective-permute-done | bytes 262176 | tf_op jit(solution)/shard_map/ppermute | solution.py:34
  25.5 0.1 pad_maximum_fusion.c0
  25.5 3.7 %collective-permute-start.7 = (bf16[2,1024,128]{2,1,0:T(8,128)(2,1)S(1)}, bf16[2,1024,128]{2,1,0:T(8,128)(2,1)S(1)}, u32[]{:S(2)}, u32[]{:S(2)}) collective-permute-start(bf16[2,1024,128]{2,1,0:T(8,128)(2,1)S(1)} %pad_maximum_fusion.c0), channel_id=1, source_target_pairs={{0,24},{1,25},{2,26},{3,27},{4,28},{5,29},{6,30},{7,31},{8,32},{9,... | collective-permute-start | bytes 1572872 | tf_op jit(solution)/shard_map/ppermute | solution.py:34
  29.3 4.4 %collective-permute-start.6 = (bf16[2,1024,128]{2,1,0:T(8,128)(2,1)S(1)}, bf16[2,1024,128]{2,1,0:T(8,128)(2,1)S(1)}, u32[]{:S(2)}, u32[]{:S(2)}) collective-permute-start(bf16[2,1024,128]{2,1,0:T(8,128)(2,1)S(1)} %pad_maximum_fusion.c0), channel_id=1, source_target_pairs={{0,48},{1,49},{2,50},{3,51},{4,52},{5,53},{6,54},{7,55},{8,56},{9,... | collective-permute-start | bytes 1572872 | tf_op jit(solution)/shard_map/ppermute | solution.py:34
  33.6 3.1 %collective-permute-start.5 = (bf16[2,1024,128]{2,1,0:T(8,128)(2,1)S(1)}, bf16[2,1024,128]{2,1,0:T(8,128)(2,1)S(1)}, u32[]{:S(2)}, u32[]{:S(2)}) collective-permute-start(bf16[2,1024,128]{2,1,0:T(8,128)(2,1)S(1)} %pad_maximum_fusion.c0), channel_id=1, source_target_pairs={{0,72},{1,73},{2,74},{3,75},{4,76},{5,77},{6,78},{7,79},{8,80},{9,... | collective-permute-start | bytes 1572872 | tf_op jit(solution)/shard_map/ppermute | solution.py:34
  36.7 2.4 %scale.1 = bf16[256,128]{1,0:T(8,128)(2,1)} custom-call(f32[1,4,4096]{2,1,0:T(4,128)} %energy.1, s32[1,4,4096]{2,1,0:T(4,128)} %occupied.1, s32[1,256]{1,0:T(1,128)} %first.1, s32[1,256]{1,0:T(1,128)} %second.1, s32[1,256]{1,0:T(1,128)} %kpoint.1, bf16[256,128]{1,0:T(8,128)(2,1)} %block.1), custom_call_target="tpu_custom_call" | custom-call | flops 400000000 | bytes 300000 | tf_op jit(solution)/shard_map/scale/pallas_call | solution.py:88
  39.1 14.3 %collective-permute-start = (bf16[256,128]{1,0:T(8,128)(2,1)}, bf16[256,128]{1,0:T(8,128)(2,1)S(1)}, u32[]{:S(2)}, u32[]{:S(2)}) collective-permute-start(bf16[256,128]{1,0:T(8,128)(2,1)} %scale.1), channel_id=1, source_target_pairs={{0,18},{1,19},{2,44},{3,45},{4,10},{5,11},{6,36},{7,37},{8,16},{9,... | collective-permute-start | bytes 196616 | tf_op jit(solution)/shard_map/ppermute | solution.py:34
  53.5 0.1 stack.44.place
  53.6 1.4 %collective-permute-done = bf16[256,128]{1,0:T(8,128)(2,1)S(1)} collective-permute-done((bf16[256,128]{1,0:T(8,128)(2,1)}, bf16[256,128]{1,0:T(8,128)(2,1)S(1)}, u32[]{:S(2)}, u32[]{:S(2)}) %collective-permute-start) | collective-permute-done | bytes 65568 | tf_op jit(solution)/shard_map/ppermute | solution.py:34
  55.0 24.8 %all-gather = bf16[3072,128]{1,0:T(8,128)(2,1)S(1)} all-gather(bf16[256,128]{1,0:T(8,128)(2,1)S(1)} %collective-permute-done), channel_id=2, replica_groups={{0,2,4,6,8,10,12,14,16,18,20,22},{1,3,5,7,9,11,13,15,17,19,21,23},{24,2..., dimensions={0}, use_global_device_ids=true | all-gather | bytes 851968 | tf_op jit(solution)/shard_map/all_gather | solution.py:201
  79.8 0.0 collective-permute-done.7.c3
  79.8 0.0 collective-permute-done.6.c2
  79.8 0.0 collective-permute-done.5.c1
  79.8 1.2 shard_map.65
  80.9 11.4 %collective-permute-start.8 = (bf16[4,384,128]{2,1,0:T(8,128)(2,1)S(1)}, bf16[4,384,128]{2,1,0:T(8,128)(2,1)S(1)}, u32[]{:S(2)}, u32[]{:S(2)}) collective-permute-start(bf16[4,384,128]{2,1,0:T(8,128)(2,1)S(1)} %shard_map.65), channel_id=1, source_target_pairs={{0,96},{1,97},{2,98},{3,99},{4,100},{5,101},{6,102},{7,103},{8,104... | collective-permute-start | bytes 1179656 | tf_op jit(solution)/shard_map/ppermute | solution.py:34
  92.3 1.2 shard_map.64.keep
  93.5 0.2 collective-permute-done.8.taken
  93.7 0.6 total.1
  94.3 4.8 %collective-permute-start.10 = (bf16[384,128]{1,0:T(8,128)(2,1)S(1)}, bf16[384,128]{1,0:T(8,128)(2,1)S(1)}, u32[]{:S(2)}, u32[]{:S(2)}) collective-permute-start(bf16[384,128]{1,0:T(8,128)(2,1)S(1)} %get-tuple-element.10), channel_id=1, source_target_pairs={{0,48},{1,25},{2,50},{3,27},{4,52},{5,29},{6,54},{7,31},{8,56},{9,... | collective-permute-start | bytes 294920 | tf_op jit(solution)/shard_map/ppermute | solution.py:34
  99.0 4.1 %collective-permute-start.11 = (bf16[384,128]{1,0:T(8,128)(2,1)S(1)}, bf16[384,128]{1,0:T(8,128)(2,1)S(1)}, u32[]{:S(2)}, u32[]{:S(2)}) collective-permute-start(bf16[384,128]{1,0:T(8,128)(2,1)S(1)} %get-tuple-element.11), channel_id=1, source_target_pairs={{0,24},{1,1},{2,26},{3,3},{4,28},{5,5},{6,30},{7,7},{8,32},{9,9},{... | collective-permute-start | bytes 294920 | tf_op jit(solution)/shard_map/ppermute | solution.py:34
  103.2 4.3 %collective-permute-start.12 = (bf16[384,128]{1,0:T(8,128)(2,1)S(1)}, bf16[384,128]{1,0:T(8,128)(2,1)S(1)}, u32[]{:S(2)}, u32[]{:S(2)}) collective-permute-start(bf16[384,128]{1,0:T(8,128)(2,1)S(1)} %get-tuple-element.12), channel_id=1, source_target_pairs={{0,72},{1,49},{2,74},{3,51},{4,76},{5,53},{6,78},{7,55},{8,80},{9,... | collective-permute-start | bytes 294920 | tf_op jit(solution)/shard_map/ppermute | solution.py:34
  107.5 1.9 %collective-permute-start.9 = (bf16[384,128]{1,0:T(8,128)(2,1)S(1)}, bf16[384,128]{1,0:T(8,128)(2,1)S(1)}, u32[]{:S(2)}, u32[]{:S(2)}) collective-permute-start(bf16[384,128]{1,0:T(8,128)(2,1)S(1)} %get-tuple-element.9), channel_id=1, source_target_pairs={{0,0},{1,73},{2,2},{3,75},{4,4},{5,77},{6,6},{7,79},{8,8},{9,81},{... | collective-permute-start | bytes 294920 | tf_op jit(solution)/shard_map/ppermute | solution.py:34
  109.4 0.0 collective-permute-done.10.refs_0_
  109.5 0.0 collective-permute-done.11.refs_1_
  109.5 1.5 %collective-permute-done.12.refs_2_ = bf16[384,128]{1,0:T(8,128)(2,1)S(1)} collective-permute-done((bf16[384,128]{1,0:T(8,128)(2,1)S(1)}, bf16[384,128]{1,0:T(8,128)(2,1)S(1)}, u32[]{:S(2)}, u32[]{:S(2)}) %collective-permute-start.12) | collective-permute-done | bytes 98336 | tf_op jit(solution)/shard_map/ppermute | solution.py:34
  110.9 1.4 %shard_map.66.refs_1_ = f32[3,2,2,128,128]{4,3,2,1,0:T(8,128)} custom-call(s32[8]{0:T(128)S(1)} %stack.44.place, bf16[384,128]{1,0:T(8,128)(2,1)S(1)} %collective-permute-done.10.refs_0_, bf16[384,128]{1,0:T(8,128)(2,1)S(1)} %collective-permute-done.11.refs_1_, bf16[384,128]{1,0:T(8,128)(2,1)S(1)} %collective-permute-done.12.refs_2_), custom_call_target="tpu_custom_call" | custom-call | tf_op jit(solution)/shard_map/pallas_call | solution.py:166
  112.4 2.6 %collective-permute-done.9.refs_0_ = bf16[384,128]{1,0:T(8,128)(2,1)S(1)} collective-permute-done((bf16[384,128]{1,0:T(8,128)(2,1)S(1)}, bf16[384,128]{1,0:T(8,128)(2,1)S(1)}, u32[]{:S(2)}, u32[]{:S(2)}) %collective-permute-start.9) | collective-permute-done | bytes 98336 | tf_op jit(solution)/shard_map/ppermute | solution.py:34
  115.0 1.3 %shard_map.67 = f32[3,2,2,128,128]{4,3,2,1,0:T(8,128)} custom-call(s32[8]{0:T(128)S(1)} %stack.44.place, bf16[384,128]{1,0:T(8,128)(2,1)S(1)} %collective-permute-done.9.refs_0_, f32[3,2,2,128,128]{4,3,2,1,0:T(8,128)} %shard_map.66.refs_1_), custom_call_target="tpu_custom_call", output_to_operand_aliasing={{}: (2, {})} | custom-call | tf_op jit(solution)/shard_map/pallas_call | solution.py:166
  (3 shorter events, 0.0 us)
Async XLA Ops:
  0.0 15.3 %collective-permute-start.2 = (bf16[256,128]{1,0:T(8,128)(2,1)}, bf16[256,128]{1,0:T(8,128)(2,1)S(1)}, u32[]{:S(2)}, u32[]{:S(2)}) collective-permute-start(bf16[256,128]{1,0:T(8,128)(2,1)} %block.1), channel_id=1, source_target_pairs={{0,384},{1,385},{2,386},{3,387},{4,388},{5,389},{6,390},{7,391},{8... | collective-permute-start | bytes 196616 | tf_op jit(solution)/shard_map/ppermute | solution.py:34
  8.3 7.1 %collective-permute-start.1 = (bf16[256,128]{1,0:T(8,128)(2,1)}, bf16[256,128]{1,0:T(8,128)(2,1)S(1)}, u32[]{:S(2)}, u32[]{:S(2)}) collective-permute-start(bf16[256,128]{1,0:T(8,128)(2,1)} %block.1), channel_id=1, source_target_pairs={{0,576},{1,577},{2,578},{3,579},{4,580},{5,581},{6,582},{7,583},{8... | collective-permute-start | bytes 196616 | tf_op jit(solution)/shard_map/ppermute | solution.py:34
  10.2 7.5 %collective-permute-start.3 = (bf16[256,128]{1,0:T(8,128)(2,1)}, bf16[256,128]{1,0:T(8,128)(2,1)S(1)}, u32[]{:S(2)}, u32[]{:S(2)}) collective-permute-start(bf16[256,128]{1,0:T(8,128)(2,1)} %block.1), channel_id=1, source_target_pairs={{0,192},{1,193},{2,194},{3,195},{4,196},{5,197},{6,198},{7,199},{8... | collective-permute-start | bytes 196616 | tf_op jit(solution)/shard_map/ppermute | solution.py:34
  17.8 7.7 %collective-permute-start.4 = (bf16[1024,128]{1,0:T(8,128)(2,1)S(1)}, bf16[1024,128]{1,0:T(8,128)(2,1)S(1)}, u32[]{:S(2)}, u32[]{:S(2)}) collective-permute-start(bf16[1024,128]{1,0:T(8,128)(2,1)S(1)} %constant_dynamic-update-slice_fusion), channel_id=1, source_target_pairs={{0,1},{1,0},{2,3},{3,2},{4,5},{5,4},{6,7},{7,6},{8,9},{9,8},{10,11... | collective-permute-start | bytes 786440 | tf_op jit(solution)/shard_map/ppermute | solution.py:34
  25.5 54.3 %collective-permute-start.7 = (bf16[2,1024,128]{2,1,0:T(8,128)(2,1)S(1)}, bf16[2,1024,128]{2,1,0:T(8,128)(2,1)S(1)}, u32[]{:S(2)}, u32[]{:S(2)}) collective-permute-start(bf16[2,1024,128]{2,1,0:T(8,128)(2,1)S(1)} %pad_maximum_fusion.c0), channel_id=1, source_target_pairs={{0,24},{1,25},{2,26},{3,27},{4,28},{5,29},{6,30},{7,31},{8,32},{9,... | collective-permute-start | bytes 1572872 | tf_op jit(solution)/shard_map/ppermute | solution.py:34
  29.3 50.5 %collective-permute-start.6 = (bf16[2,1024,128]{2,1,0:T(8,128)(2,1)S(1)}, bf16[2,1024,128]{2,1,0:T(8,128)(2,1)S(1)}, u32[]{:S(2)}, u32[]{:S(2)}) collective-permute-start(bf16[2,1024,128]{2,1,0:T(8,128)(2,1)S(1)} %pad_maximum_fusion.c0), channel_id=1, source_target_pairs={{0,48},{1,49},{2,50},{3,51},{4,52},{5,53},{6,54},{7,55},{8,56},{9,... | collective-permute-start | bytes 1572872 | tf_op jit(solution)/shard_map/ppermute | solution.py:34
  33.6 46.2 %collective-permute-start.5 = (bf16[2,1024,128]{2,1,0:T(8,128)(2,1)S(1)}, bf16[2,1024,128]{2,1,0:T(8,128)(2,1)S(1)}, u32[]{:S(2)}, u32[]{:S(2)}) collective-permute-start(bf16[2,1024,128]{2,1,0:T(8,128)(2,1)S(1)} %pad_maximum_fusion.c0), channel_id=1, source_target_pairs={{0,72},{1,73},{2,74},{3,75},{4,76},{5,77},{6,78},{7,79},{8,80},{9,... | collective-permute-start | bytes 1572872 | tf_op jit(solution)/shard_map/ppermute | solution.py:34
  39.1 15.9 %collective-permute-start = (bf16[256,128]{1,0:T(8,128)(2,1)}, bf16[256,128]{1,0:T(8,128)(2,1)S(1)}, u32[]{:S(2)}, u32[]{:S(2)}) collective-permute-start(bf16[256,128]{1,0:T(8,128)(2,1)} %scale.1), channel_id=1, source_target_pairs={{0,18},{1,19},{2,44},{3,45},{4,10},{5,11},{6,36},{7,37},{8,16},{9,... | collective-permute-start | bytes 196616 | tf_op jit(solution)/shard_map/ppermute | solution.py:34
  80.9 12.7 %collective-permute-start.8 = (bf16[4,384,128]{2,1,0:T(8,128)(2,1)S(1)}, bf16[4,384,128]{2,1,0:T(8,128)(2,1)S(1)}, u32[]{:S(2)}, u32[]{:S(2)}) collective-permute-start(bf16[4,384,128]{2,1,0:T(8,128)(2,1)S(1)} %shard_map.65), channel_id=1, source_target_pairs={{0,96},{1,97},{2,98},{3,99},{4,100},{5,101},{6,102},{7,103},{8,104... | collective-permute-start | bytes 1179656 | tf_op jit(solution)/shard_map/ppermute | solution.py:34
  94.3 15.2 %collective-permute-start.10 = (bf16[384,128]{1,0:T(8,128)(2,1)S(1)}, bf16[384,128]{1,0:T(8,128)(2,1)S(1)}, u32[]{:S(2)}, u32[]{:S(2)}) collective-permute-start(bf16[384,128]{1,0:T(8,128)(2,1)S(1)} %get-tuple-element.10), channel_id=1, source_target_pairs={{0,48},{1,25},{2,50},{3,27},{4,52},{5,29},{6,54},{7,31},{8,56},{9,... | collective-permute-start | bytes 294920 | tf_op jit(solution)/shard_map/ppermute | solution.py:34
  99.0 10.4 %collective-permute-start.11 = (bf16[384,128]{1,0:T(8,128)(2,1)S(1)}, bf16[384,128]{1,0:T(8,128)(2,1)S(1)}, u32[]{:S(2)}, u32[]{:S(2)}) collective-permute-start(bf16[384,128]{1,0:T(8,128)(2,1)S(1)} %get-tuple-element.11), channel_id=1, source_target_pairs={{0,24},{1,1},{2,26},{3,3},{4,28},{5,5},{6,30},{7,7},{8,32},{9,9},{... | collective-permute-start | bytes 294920 | tf_op jit(solution)/shard_map/ppermute | solution.py:34
  103.2 7.8 %collective-permute-start.12 = (bf16[384,128]{1,0:T(8,128)(2,1)S(1)}, bf16[384,128]{1,0:T(8,128)(2,1)S(1)}, u32[]{:S(2)}, u32[]{:S(2)}) collective-permute-start(bf16[384,128]{1,0:T(8,128)(2,1)S(1)} %get-tuple-element.12), channel_id=1, source_target_pairs={{0,72},{1,49},{2,74},{3,51},{4,76},{5,53},{6,78},{7,55},{8,80},{9,... | collective-permute-start | bytes 294920 | tf_op jit(solution)/shard_map/ppermute | solution.py:34
  107.5 7.5 %collective-permute-start.9 = (bf16[384,128]{1,0:T(8,128)(2,1)S(1)}, bf16[384,128]{1,0:T(8,128)(2,1)S(1)}, u32[]{:S(2)}, u32[]{:S(2)}) collective-permute-start(bf16[384,128]{1,0:T(8,128)(2,1)S(1)} %get-tuple-element.9), channel_id=1, source_target_pairs={{0,0},{1,73},{2,2},{3,75},{4,4},{5,77},{6,6},{7,79},{8,8},{9,81},{... | collective-permute-start | bytes 294920 | tf_op jit(solution)/shard_map/ppermute | solution.py:34

commit v9 on v2

--- a/solution.py
+++ b/solution.py
@@ -82,6 +82,21 @@
     )(energy, occupied, first, second, kpoint, block)
 
 
+def join_kernel(*refs):
+    for i, part in enumerate(refs[:-1]):
+        refs[-1][i] = part[...]
+
+
+def join(parts):
+    return pl.pallas_call(
+        join_kernel,
+        out_shape=jax.ShapeDtypeStruct((len(parts),) + parts[0].shape, parts[0].dtype),
+        in_specs=[pl.BlockSpec(memory_space=pltpu.VMEM)] * len(parts),
+        out_specs=pl.BlockSpec(memory_space=pltpu.VMEM),
+        compiler_params=pltpu.CompilerParams(vmem_limit_bytes=8 * 2**20),
+    )(*parts)
+
+
 def product_kernel(side, place, rows, c0, c1, c2, c3, out):
     which = place[side]
     left = jnp.concatenate(
@@ -166,9 +181,9 @@
         scaled,
         lambda h, k, x, z, l: (x, k, z // 3, z + 3 * SHIFT[(h - x) % H], l),
     )
-    own = jnp.concatenate([pair_matrix] + around, axis=0)
+    own = join([pair_matrix] + around).reshape(H * PAIRS, WIDTH)
     other = move(own, lambda h, k, x, z, l: (h, k, x, z, 1 - l))
-    both = jnp.stack([own, other])
+    both = join([own, other])
     columns = [both]
     for s in range(1, X):
         columns.append(move(both, lambda h, k, x, z, l, s=s: (h, k, x - s, z, l)))

time: 117 us -> 118 us (level)
  transfers between devices with their start and end apart: 13 -> 13, of which waited for: 6 -> 7; matrix products, arithmetic and copies ran while one was open for 1% -> 0% of each run, Pallas kernels for 3% -> 3%
where the time goes in v9:
time: 118 us
  starting transfers between devices  68.5 us (58%)
  blocking collectives  27.5 us (23%)
  waiting for transfers between devices  13.6 us (12%)
  Pallas kernels  6.8 us (6%)
    ppermute x13, starting transfers between devices, move(): return lax.ppermute(value, AXES, table(f))  68.5 us
    all_gather x1, blocking collectives, blocks(): rows = lax.all_gather(sent, 'col', axis=0, axis_index_groups=Z_GROUPS)  27.5 us
    ppermute x13, waiting for transfers between devices, move(): return lax.ppermute(value, AXES, table(f))  13.6 us
  transfers between devices with their start and end apart: 13, of which 7 were waited for; matrix products, arithmetic and copies ran while one was open for 0% of the time, Pallas kernels for 3%

profile of v9, /device:TPU:1, one launch (start us, length us, event | category | flops | bytes accessed | tf_op | source)
XLA Modules:
  0.0 117.5 jit_solution(5928716364025225161)
XLA Ops:
  0.0 8.3 %collective-permute-start.2 = (bf16[256,128]{1,0:T(8,128)(2,1)}, bf16[256,128]{1,0:T(8,128)(2,1)S(1)}, u32[]{:S(2)}, u32[]{:S(2)}) collective-permute-start(bf16[256,128]{1,0:T(8,128)(2,1)} %refs_0_.1), channel_id=1, source_target_pairs={{0,384},{1,385},{2,386},{3,387},{4,388},{5,389},{6,390},{7,391},{8... | collective-permute-start | bytes 196616 | tf_op jit(solution)/shard_map/ppermute | solution.py:34
  8.3 2.0 %collective-permute-start.1 = (bf16[256,128]{1,0:T(8,128)(2,1)}, bf16[256,128]{1,0:T(8,128)(2,1)S(1)}, u32[]{:S(2)}, u32[]{:S(2)}) collective-permute-start(bf16[256,128]{1,0:T(8,128)(2,1)} %refs_0_.1), channel_id=1, source_target_pairs={{0,576},{1,577},{2,578},{3,579},{4,580},{5,581},{6,582},{7,583},{8... | collective-permute-start | bytes 196616 | tf_op jit(solution)/shard_map/ppermute | solution.py:34
  10.2 4.2 %collective-permute-start.3 = (bf16[256,128]{1,0:T(8,128)(2,1)}, bf16[256,128]{1,0:T(8,128)(2,1)S(1)}, u32[]{:S(2)}, u32[]{:S(2)}) collective-permute-start(bf16[256,128]{1,0:T(8,128)(2,1)} %refs_0_.1), channel_id=1, source_target_pairs={{0,192},{1,193},{2,194},{3,195},{4,196},{5,197},{6,198},{7,199},{8... | collective-permute-start | bytes 196616 | tf_op jit(solution)/shard_map/ppermute | solution.py:34
  14.5 0.0 collective-permute-done.2.refs_2_
  14.5 0.7 collective-permute-done.1.refs_1_
  15.2 2.6 %collective-permute-done.3.refs_3_ = bf16[256,128]{1,0:T(8,128)(2,1)S(1)} collective-permute-done((bf16[256,128]{1,0:T(8,128)(2,1)}, bf16[256,128]{1,0:T(8,128)(2,1)S(1)}, u32[]{:S(2)}, u32[]{:S(2)}) %collective-permute-start.3) | collective-permute-done | bytes 65568 | tf_op jit(solution)/shard_map/ppermute | solution.py:34
  17.7 0.0 copy-start
  17.8 0.8 copy-done
  18.6 3.7 %collective-permute-start.4 = (bf16[1024,128]{1,0:T(8,128)(2,1)S(1)}, bf16[1024,128]{1,0:T(8,128)(2,1)S(1)}, u32[]{:S(2)}, u32[]{:S(2)}) collective-permute-start(bf16[1024,128]{1,0:T(8,128)(2,1)S(1)} %bitcast.13), channel_id=1, source_target_pairs={{0,1},{1,0},{2,3},{3,2},{4,5},{5,4},{6,7},{7,6},{8,9},{9,8},{10,11... | collective-permute-start | bytes 786440 | tf_op jit(solution)/shard_map/ppermute | solution.py:34
  22.3 3.7 %collective-permute-done.4.refs_1_ = bf16[1024,128]{1,0:T(8,128)(2,1)S(1)} collective-permute-done((bf16[1024,128]{1,0:T(8,128)(2,1)S(1)}, bf16[1024,128]{1,0:T(8,128)(2,1)S(1)}, u32[]{:S(2)}, u32[]{:S(2)}) %collective-permute-start.4) | collective-permute-done | bytes 262176 | tf_op jit(solution)/shard_map/ppermute | solution.py:34
  26.1 4.0 %collective-permute-start.7 = (bf16[2,1024,128]{2,1,0:T(8,128)(2,1)S(1)}, bf16[2,1024,128]{2,1,0:T(8,128)(2,1)S(1)}, u32[]{:S(2)}, u32[]{:S(2)}) collective-permute-start(bf16[2,1024,128]{2,1,0:T(8,128)(2,1)S(1)} %shard_map.65.c0), channel_id=1, source_target_pairs={{0,24},{1,25},{2,26},{3,27},{4,28},{5,29},{6,30},{7,31},{8,32},{9,... | collective-permute-start | bytes 1572872 | tf_op jit(solution)/shard_map/ppermute | solution.py:34
  30.1 4.4 %collective-permute-start.6 = (bf16[2,1024,128]{2,1,0:T(8,128)(2,1)S(1)}, bf16[2,1024,128]{2,1,0:T(8,128)(2,1)S(1)}, u32[]{:S(2)}, u32[]{:S(2)}) collective-permute-start(bf16[2,1024,128]{2,1,0:T(8,128)(2,1)S(1)} %shard_map.65.c0), channel_id=1, source_target_pairs={{0,48},{1,49},{2,50},{3,51},{4,52},{5,53},{6,54},{7,55},{8,56},{9,... | collective-permute-start | bytes 1572872 | tf_op jit(solution)/shard_map/ppermute | solution.py:34
  34.5 3.1 %collective-permute-start.5 = (bf16[2,1024,128]{2,1,0:T(8,128)(2,1)S(1)}, bf16[2,1024,128]{2,1,0:T(8,128)(2,1)S(1)}, u32[]{:S(2)}, u32[]{:S(2)}) collective-permute-start(bf16[2,1024,128]{2,1,0:T(8,128)(2,1)S(1)} %shard_map.65.c0), channel_id=1, source_target_pairs={{0,72},{1,73},{2,74},{3,75},{4,76},{5,77},{6,78},{7,79},{8,80},{9,... | collective-permute-start | bytes 1572872 | tf_op jit(solution)/shard_map/ppermute | solution.py:34
  37.5 2.4 %scale.1 = bf16[256,128]{1,0:T(8,128)(2,1)} custom-call(f32[1,4,4096]{2,1,0:T(4,128)} %energy.1, s32[1,4,4096]{2,1,0:T(4,128)} %occupied.1, s32[1,256]{1,0:T(1,128)} %first.1, s32[1,256]{1,0:T(1,128)} %second.1, s32[1,256]{1,0:T(1,128)} %kpoint.1, bf16[256,128]{1,0:T(8,128)(2,1)} %refs_0_.1), custom_call_target="tpu_custom_call" | custom-call | flops 400000000 | bytes 300000 | tf_op jit(solution)/shard_map/scale/pallas_call | solution.py:76
  39.9 14.8 %collective-permute-start = (bf16[256,128]{1,0:T(8,128)(2,1)}, bf16[256,128]{1,0:T(8,128)(2,1)S(1)}, u32[]{:S(2)}, u32[]{:S(2)}) collective-permute-start(bf16[256,128]{1,0:T(8,128)(2,1)} %scale.1), channel_id=1, source_target_pairs={{0,12},{1,13},{2,14},{3,15},{4,16},{5,17},{6,42},{7,43},{8,44},{9,... | collective-permute-start | bytes 196616 | tf_op jit(solution)/shard_map/ppermute | solution.py:34
  54.9 0.1 stack.35.place
  54.9 1.4 %collective-permute-done = bf16[256,128]{1,0:T(8,128)(2,1)S(1)} collective-permute-done((bf16[256,128]{1,0:T(8,128)(2,1)}, bf16[256,128]{1,0:T(8,128)(2,1)S(1)}, u32[]{:S(2)}, u32[]{:S(2)}) %collective-permute-start) | collective-permute-done | bytes 65568 | tf_op jit(solution)/shard_map/ppermute | solution.py:34
  56.4 27.5 %all-gather = bf16[3072,128]{1,0:T(8,128)(2,1)S(1)} all-gather(bf16[256,128]{1,0:T(8,128)(2,1)S(1)} %collective-permute-done), channel_id=2, replica_groups={{0,2,4,6,8,10,12,14,16,18,20,22},{1,3,5,7,9,11,13,15,17,19,21,23},{24,2..., dimensions={0}, use_global_device_ids=true | all-gather | bytes 851968 | tf_op jit(solution)/shard_map/all_gather | solution.py:190
  83.8 0.0 collective-permute-done.7.c3
  83.8 0.0 collective-permute-done.6.c2
  83.8 0.0 collective-permute-done.5.c1
  83.9 1.1 shard_map.67
  85.0 11.5 %collective-permute-start.8 = (bf16[4,384,128]{2,1,0:T(8,128)(2,1)S(1)}, bf16[4,384,128]{2,1,0:T(8,128)(2,1)S(1)}, u32[]{:S(2)}, u32[]{:S(2)}) collective-permute-start(bf16[4,384,128]{2,1,0:T(8,128)(2,1)S(1)} %shard_map.67), channel_id=1, source_target_pairs={{0,96},{1,97},{2,98},{3,99},{4,100},{5,101},{6,102},{7,103},{8,104... | collective-permute-start | bytes 1179656 | tf_op jit(solution)/shard_map/ppermute | solution.py:34
  96.5 1.1 shard_map.66.keep
  97.6 0.2 collective-permute-done.8.taken
  97.8 0.6 total.1
  98.4 3.6 %collective-permute-start.9 = (bf16[384,128]{1,0:T(8,128)(2,1)S(1)}, bf16[384,128]{1,0:T(8,128)(2,1)S(1)}, u32[]{:S(2)}, u32[]{:S(2)}) collective-permute-start(bf16[384,128]{1,0:T(8,128)(2,1)S(1)} %get-tuple-element.9), channel_id=1, source_target_pairs={{0,0},{1,49},{2,2},{3,51},{4,4},{5,53},{6,6},{7,55},{8,8},{9,57},{... | collective-permute-start | bytes 294920 | tf_op jit(solution)/shard_map/ppermute | solution.py:34
  102.0 2.8 %collective-permute-start.10 = (bf16[384,128]{1,0:T(8,128)(2,1)S(1)}, bf16[384,128]{1,0:T(8,128)(2,1)S(1)}, u32[]{:S(2)}, u32[]{:S(2)}) collective-permute-start(bf16[384,128]{1,0:T(8,128)(2,1)S(1)} %get-tuple-element.10), channel_id=1, source_target_pairs={{0,24},{1,73},{2,26},{3,75},{4,28},{5,77},{6,30},{7,79},{8,32},{9,... | collective-permute-start | bytes 294920 | tf_op jit(solution)/shard_map/ppermute | solution.py:34
  104.8 3.8 %collective-permute-start.11 = (bf16[384,128]{1,0:T(8,128)(2,1)S(1)}, bf16[384,128]{1,0:T(8,128)(2,1)S(1)}, u32[]{:S(2)}, u32[]{:S(2)}) collective-permute-start(bf16[384,128]{1,0:T(8,128)(2,1)S(1)} %get-tuple-element.11), channel_id=1, source_target_pairs={{0,48},{1,1},{2,50},{3,3},{4,52},{5,5},{6,54},{7,7},{8,56},{9,9},{... | collective-permute-start | bytes 294920 | tf_op jit(solution)/shard_map/ppermute | solution.py:34
  108.6 2.5 %collective-permute-start.12 = (bf16[384,128]{1,0:T(8,128)(2,1)S(1)}, bf16[384,128]{1,0:T(8,128)(2,1)S(1)}, u32[]{:S(2)}, u32[]{:S(2)}) collective-permute-start(bf16[384,128]{1,0:T(8,128)(2,1)S(1)} %get-tuple-element.12), channel_id=1, source_target_pairs={{0,72},{1,25},{2,74},{3,27},{4,76},{5,29},{6,78},{7,31},{8,80},{9,... | collective-permute-start | bytes 294920 | tf_op jit(solution)/shard_map/ppermute | solution.py:34
  111.1 0.0 collective-permute-done.9.f0
  111.1 0.0 collective-permute-done.10.f1
  111.1 1.1 collective-permute-done.11.f2
  112.2 3.8 %collective-permute-done.12.f3 = bf16[384,128]{1,0:T(8,128)(2,1)S(1)} collective-permute-done((bf16[384,128]{1,0:T(8,128)(2,1)S(1)}, bf16[384,128]{1,0:T(8,128)(2,1)S(1)}, u32[]{:S(2)}, u32[]{:S(2)}) %collective-permute-start.12) | collective-permute-done | bytes 98336 | tf_op jit(solution)/shard_map/ppermute | solution.py:34
  116.0 1.5 %assemble.1 = f32[2,3,2,128,128]{4,3,2,1,0:T(8,128)} custom-call(s32[8]{0:T(128)S(1)} %stack.35.place, bf16[384,128]{1,0:T(8,128)(2,1)S(1)} %collective-permute-done.9.f0, bf16[384,128]{1,0:T(8,128)(2,1)S(1)} %collective-permute-done.10.f1, bf16[384,128]{1,0:T(8,128)(2,1)S(1)} %collective-permute-done.11.f2, bf16[384,128]{1,0:T(8,128)(2,1)S(1)} %collective-permute-done.12.f3), custom_call_target="tpu_custom_call" | custom-call | tf_op jit(solution)/shard_map/assemble/pallas_call | solution.py:157
  (2 shorter events, 0.1 us)
Async XLA Ops:
  0.0 14.5 %collective-permute-start.2 = (bf16[256,128]{1,0:T(8,128)(2,1)}, bf16[256,128]{1,0:T(8,128)(2,1)S(1)}, u32[]{:S(2)}, u32[]{:S(2)}) collective-permute-start(bf16[256,128]{1,0:T(8,128)(2,1)} %refs_0_.1), channel_id=1, source_target_pairs={{0,384},{1,385},{2,386},{3,387},{4,388},{5,389},{6,390},{7,391},{8... | collective-permute-start | bytes 196616 | tf_op jit(solution)/shard_map/ppermute | solution.py:34
  8.3 6.9 %collective-permute-start.1 = (bf16[256,128]{1,0:T(8,128)(2,1)}, bf16[256,128]{1,0:T(8,128)(2,1)S(1)}, u32[]{:S(2)}, u32[]{:S(2)}) collective-permute-start(bf16[256,128]{1,0:T(8,128)(2,1)} %refs_0_.1), channel_id=1, source_target_pairs={{0,576},{1,577},{2,578},{3,579},{4,580},{5,581},{6,582},{7,583},{8... | collective-permute-start | bytes 196616 | tf_op jit(solution)/shard_map/ppermute | solution.py:34
  10.2 7.5 %collective-permute-start.3 = (bf16[256,128]{1,0:T(8,128)(2,1)}, bf16[256,128]{1,0:T(8,128)(2,1)S(1)}, u32[]{:S(2)}, u32[]{:S(2)}) collective-permute-start(bf16[256,128]{1,0:T(8,128)(2,1)} %refs_0_.1), channel_id=1, source_target_pairs={{0,192},{1,193},{2,194},{3,195},{4,196},{5,197},{6,198},{7,199},{8... | collective-permute-start | bytes 196616 | tf_op jit(solution)/shard_map/ppermute | solution.py:34
  17.7 0.8 copy-start
  18.6 7.5 %collective-permute-start.4 = (bf16[1024,128]{1,0:T(8,128)(2,1)S(1)}, bf16[1024,128]{1,0:T(8,128)(2,1)S(1)}, u32[]{:S(2)}, u32[]{:S(2)}) collective-permute-start(bf16[1024,128]{1,0:T(8,128)(2,1)S(1)} %bitcast.13), channel_id=1, source_target_pairs={{0,1},{1,0},{2,3},{3,2},{4,5},{5,4},{6,7},{7,6},{8,9},{9,8},{10,11... | collective-permute-start | bytes 786440 | tf_op jit(solution)/shard_map/ppermute | solution.py:34
  26.1 57.7 %collective-permute-start.7 = (bf16[2,1024,128]{2,1,0:T(8,128)(2,1)S(1)}, bf16[2,1024,128]{2,1,0:T(8,128)(2,1)S(1)}, u32[]{:S(2)}, u32[]{:S(2)}) collective-permute-start(bf16[2,1024,128]{2,1,0:T(8,128)(2,1)S(1)} %shard_map.65.c0), channel_id=1, source_target_pairs={{0,24},{1,25},{2,26},{3,27},{4,28},{5,29},{6,30},{7,31},{8,32},{9,... | collective-permute-start | bytes 1572872 | tf_op jit(solution)/shard_map/ppermute | solution.py:34
  30.1 53.8 %collective-permute-start.6 = (bf16[2,1024,128]{2,1,0:T(8,128)(2,1)S(1)}, bf16[2,1024,128]{2,1,0:T(8,128)(2,1)S(1)}, u32[]{:S(2)}, u32[]{:S(2)}) collective-permute-start(bf16[2,1024,128]{2,1,0:T(8,128)(2,1)S(1)} %shard_map.65.c0), channel_id=1, source_target_pairs={{0,48},{1,49},{2,50},{3,51},{4,52},{5,53},{6,54},{7,55},{8,56},{9,... | collective-permute-start | bytes 1572872 | tf_op jit(solution)/shard_map/ppermute | solution.py:34
  34.5 49.4 %collective-permute-start.5 = (bf16[2,1024,128]{2,1,0:T(8,128)(2,1)S(1)}, bf16[2,1024,128]{2,1,0:T(8,128)(2,1)S(1)}, u32[]{:S(2)}, u32[]{:S(2)}) collective-permute-start(bf16[2,1024,128]{2,1,0:T(8,128)(2,1)S(1)} %shard_map.65.c0), channel_id=1, source_target_pairs={{0,72},{1,73},{2,74},{3,75},{4,76},{5,77},{6,78},{7,79},{8,80},{9,... | collective-permute-start | bytes 1572872 | tf_op jit(solution)/shard_map/ppermute | solution.py:34
  39.9 16.5 %collective-permute-start = (bf16[256,128]{1,0:T(8,128)(2,1)}, bf16[256,128]{1,0:T(8,128)(2,1)S(1)}, u32[]{:S(2)}, u32[]{:S(2)}) collective-permute-start(bf16[256,128]{1,0:T(8,128)(2,1)} %scale.1), channel_id=1, source_target_pairs={{0,12},{1,13},{2,14},{3,15},{4,16},{5,17},{6,42},{7,43},{8,44},{9,... | collective-permute-start | bytes 196616 | tf_op jit(solution)/shard_map/ppermute | solution.py:34
  85.0 12.8 %collective-permute-start.8 = (bf16[4,384,128]{2,1,0:T(8,128)(2,1)S(1)}, bf16[4,384,128]{2,1,0:T(8,128)(2,1)S(1)}, u32[]{:S(2)}, u32[]{:S(2)}) collective-permute-start(bf16[4,384,128]{2,1,0:T(8,128)(2,1)S(1)} %shard_map.67), channel_id=1, source_target_pairs={{0,96},{1,97},{2,98},{3,99},{4,100},{5,101},{6,102},{7,103},{8,104... | collective-permute-start | bytes 1179656 | tf_op jit(solution)/shard_map/ppermute | solution.py:34
  98.4 12.6 %collective-permute-start.9 = (bf16[384,128]{1,0:T(8,128)(2,1)S(1)}, bf16[384,128]{1,0:T(8,128)(2,1)S(1)}, u32[]{:S(2)}, u32[]{:S(2)}) collective-permute-start(bf16[384,128]{1,0:T(8,128)(2,1)S(1)} %get-tuple-element.9), channel_id=1, source_target_pairs={{0,0},{1,49},{2,2},{3,51},{4,4},{5,53},{6,6},{7,55},{8,8},{9,57},{... | collective-permute-start | bytes 294920 | tf_op jit(solution)/shard_map/ppermute | solution.py:34
  102.0 9.1 %collective-permute-start.10 = (bf16[384,128]{1,0:T(8,128)(2,1)S(1)}, bf16[384,128]{1,0:T(8,128)(2,1)S(1)}, u32[]{:S(2)}, u32[]{:S(2)}) collective-permute-start(bf16[384,128]{1,0:T(8,128)(2,1)S(1)} %get-tuple-element.10), channel_id=1, source_target_pairs={{0,24},{1,73},{2,26},{3,75},{4,28},{5,77},{6,30},{7,79},{8,32},{9,... | collective-permute-start | bytes 294920 | tf_op jit(solution)/shard_map/ppermute | solution.py:34
  104.8 7.4 %collective-permute-start.11 = (bf16[384,128]{1,0:T(8,128)(2,1)S(1)}, bf16[384,128]{1,0:T(8,128)(2,1)S(1)}, u32[]{:S(2)}, u32[]{:S(2)}) collective-permute-start(bf16[384,128]{1,0:T(8,128)(2,1)S(1)} %get-tuple-element.11), channel_id=1, source_target_pairs={{0,48},{1,1},{2,50},{3,3},{4,52},{5,5},{6,54},{7,7},{8,56},{9,9},{... | collective-permute-start | bytes 294920 | tf_op jit(solution)/shard_map/ppermute | solution.py:34
  108.6 7.5 %collective-permute-start.12 = (bf16[384,128]{1,0:T(8,128)(2,1)S(1)}, bf16[384,128]{1,0:T(8,128)(2,1)S(1)}, u32[]{:S(2)}, u32[]{:S(2)}) collective-permute-start(bf16[384,128]{1,0:T(8,128)(2,1)S(1)} %get-tuple-element.12), channel_id=1, source_target_pairs={{0,72},{1,25},{2,74},{3,27},{4,76},{5,29},{6,78},{7,31},{8,80},{9,... | collective-permute-start | bytes 294920 | tf_op jit(solution)/shard_map/ppermute | solution.py:34

commit v10 on v2

--- a/solution.py
+++ b/solution.py
@@ -34,7 +34,22 @@
     return lax.ppermute(value, AXES, table(f))
 
 
-Z_GROUPS = [[x * Z * L + z * L + l for z in range(Z)] for x in range(X) for l in range(L)]
+def half(k, z):
+    return k ^ (z % 2)
+
+
+Z_GROUPS = [
+    [at(h, half(n, z), x, z, l) for z in range(Z)]
+    for h in range(H)
+    for n in range(K)
+    for x in range(X)
+    for l in range(L)
+]
+
+
+def spread(h, k, x, z, l):
+    to = (z + 3 * SHIFT[(h - x) % H]) % Z
+    return x, half(k, to), z // 3, to, l
 
 
 def scale_kernel(energy, occupied, first, second, kpoint, block, out, energies, filled):
@@ -157,22 +172,19 @@
     ).astype(jnp.int32)
 
     around = []
-    for s in range(1, H):
-        around.append(move(pair_matrix, lambda h, k, x, z, l, s=s: (h - s, k, x, z, l)))
+    for s in range(H):
+        around.append(move(pair_matrix, lambda h, k, x, z, l, s=s: (h - s, half(k, z), x, z, l)))
     scaled = scaled_block(
         band_energy, occupation, pair_first, pair_second, pair_kpoint, pair_matrix
     )
-    sent = move(
-        scaled,
-        lambda h, k, x, z, l: (x, k, z // 3, z + 3 * SHIFT[(h - x) % H], l),
-    )
-    own = jnp.concatenate([pair_matrix] + around, axis=0)
+    sent = move(scaled, spread)
+    own = jnp.concatenate(around, axis=0)
     other = move(own, lambda h, k, x, z, l: (h, k, x, z, 1 - l))
     both = jnp.stack([own, other])
     columns = [both]
     for s in range(1, X):
         columns.append(move(both, lambda h, k, x, z, l, s=s: (h, k, x - s, z, l)))
-    rows = lax.all_gather(sent, "col", axis=0, axis_index_groups=Z_GROUPS)
+    rows = lax.all_gather(sent, AXES, axis=0, axis_index_groups=Z_GROUPS)
 
     give = product(0, place, rows, columns, jnp.bfloat16)
     taken = move(give, lambda h, k, x, z, l: (h, 1 - k, x, z, l))

time: 117 us -> 118 us (level)
  starting transfers between devices: 68.2 us -> 58.7 us
  blocking collectives: 27.5 us -> 35.6 us
  waiting for transfers between devices: 12.9 us -> 15.6 us
    ppermute x13 -> x14, starting transfers between devices: 68.2 us -> 58.7 us  [move(): return lax.ppermute(value, AXES, table(f))]
    all_gather x1, blocking collectives: 27.5 us -> 35.6 us  [blocks(): rows = lax.all_gather(sent, AXES, axis=0, axis_index_groups=Z_GROUPS)]
    ppermute x13 -> x14, waiting for transfers between devices: 12.9 us -> 15.6 us  [move(): return lax.ppermute(value, AXES, table(f))]
  transfers between devices with their start and end apart: 13 -> 14, of which waited for: 6 -> 6; matrix products, arithmetic and copies ran while one was open for 1% -> 0% of each run, Pallas kernels for 3% -> 3%
where the time goes in v10:
time: 118 us; the launch traced here: 117 us
  starting transfers between devices  58.7 us (50%)
  blocking collectives  35.6 us (30%)
  waiting for transfers between devices  15.6 us (13%)
  Pallas kernels  6.74 us (6%)
    ppermute x14, starting transfers between devices, move(): return lax.ppermute(value, AXES, table(f))  58.7 us
    all_gather x1, blocking collectives, blocks(): rows = lax.all_gather(sent, AXES, axis=0, axis_index_groups=Z_GROUPS)  35.6 us
    ppermute x14, waiting for transfers between devices, move(): return lax.ppermute(value, AXES, table(f))  15.6 us
  transfers between devices with their start and end apart: 14, of which 6 were waited for; matrix products, arithmetic and copies ran while one was open for 0% of the time, Pallas kernels for 3%

profile of v10, /device:TPU:1, one launch (start us, length us, event | category | flops | bytes accessed | tf_op | source)
XLA Modules:
  0.0 117.2 jit_solution(4602742830891755643)
XLA Ops:
  0.0 1.5 %collective-permute-start.1 = (bf16[256,128]{1,0:T(8,128)(2,1)}, bf16[256,128]{1,0:T(8,128)(2,1)S(1)}, u32[]{:S(2)}, u32[]{:S(2)}) collective-permute-start(bf16[256,128]{1,0:T(8,128)(2,1)} %block.1), channel_id=1, source_target_pairs={{0,0},{1,1},{2,98},{3,99},{4,4},{5,5},{6,102},{7,103},{8,8},{9,9},... | collective-permute-start | bytes 196616 | tf_op jit(solution)/shard_map/ppermute | solution.py:34
  1.5 6.7 %collective-permute-start.2 = (bf16[256,128]{1,0:T(8,128)(2,1)}, bf16[256,128]{1,0:T(8,128)(2,1)S(1)}, u32[]{:S(2)}, u32[]{:S(2)}) collective-permute-start(bf16[256,128]{1,0:T(8,128)(2,1)} %block.1), channel_id=1, source_target_pairs={{0,576},{1,577},{2,674},{3,675},{4,580},{5,581},{6,678},{7,679},{8... | collective-permute-start | bytes 196616 | tf_op jit(solution)/shard_map/ppermute | solution.py:34
  8.2 1.9 %collective-permute-start.4 = (bf16[256,128]{1,0:T(8,128)(2,1)}, bf16[256,128]{1,0:T(8,128)(2,1)S(1)}, u32[]{:S(2)}, u32[]{:S(2)}) collective-permute-start(bf16[256,128]{1,0:T(8,128)(2,1)} %block.1), channel_id=1, source_target_pairs={{0,192},{1,193},{2,290},{3,291},{4,196},{5,197},{6,294},{7,295},{8... | collective-permute-start | bytes 196616 | tf_op jit(solution)/shard_map/ppermute | solution.py:34
  10.1 5.8 %collective-permute-start.3 = (bf16[256,128]{1,0:T(8,128)(2,1)}, bf16[256,128]{1,0:T(8,128)(2,1)S(1)}, u32[]{:S(2)}, u32[]{:S(2)}) collective-permute-start(bf16[256,128]{1,0:T(8,128)(2,1)} %block.1), channel_id=1, source_target_pairs={{0,384},{1,385},{2,482},{3,483},{4,388},{5,389},{6,486},{7,487},{8... | collective-permute-start | bytes 196616 | tf_op jit(solution)/shard_map/ppermute | solution.py:34
  16.0 0.0 collective-permute-done.1
  16.0 0.0 collective-permute-done.2
  16.0 3.5 %collective-permute-done.3 = bf16[256,128]{1,0:T(8,128)(2,1)S(1)} collective-permute-done((bf16[256,128]{1,0:T(8,128)(2,1)}, bf16[256,128]{1,0:T(8,128)(2,1)S(1)}, u32[]{:S(2)}, u32[]{:S(2)}) %collective-permute-start.3) | collective-permute-done | bytes 65568 | tf_op jit(solution)/shard_map/ppermute | solution.py:34
  19.5 0.0 collective-permute-done.4
  19.5 2.1 %collective-permute-start.5 = (bf16[1024,128]{1,0:T(8,128)(2,1)S(1)}, bf16[1024,128]{1,0:T(8,128)(2,1)S(1)}, u32[]{:S(2)}, u32[]{:S(2)}) collective-permute-start(bf16[1024,128]{1,0:T(8,128)(2,1)S(1)} %constant_dynamic-update-slice_fusion), channel_id=1, source_target_pairs={{0,1},{1,0},{2,3},{3,2},{4,5},{5,4},{6,7},{7,6},{8,9},{9,8},{10,11... | collective-permute-start | bytes 786440 | tf_op jit(solution)/shard_map/ppermute | solution.py:34
  21.6 5.0 %collective-permute-done.5 = bf16[1024,128]{1,0:T(8,128)(2,1)S(1)} collective-permute-done((bf16[1024,128]{1,0:T(8,128)(2,1)S(1)}, bf16[1024,128]{1,0:T(8,128)(2,1)S(1)}, u32[]{:S(2)}, u32[]{:S(2)}) %collective-permute-start.5) | collective-permute-done | bytes 262176 | tf_op jit(solution)/shard_map/ppermute | solution.py:34
  26.6 0.1 pad_maximum_fusion.c0
  26.7 4.4 %collective-permute-start.8 = (bf16[2,1024,128]{2,1,0:T(8,128)(2,1)S(1)}, bf16[2,1024,128]{2,1,0:T(8,128)(2,1)S(1)}, u32[]{:S(2)}, u32[]{:S(2)}) collective-permute-start(bf16[2,1024,128]{2,1,0:T(8,128)(2,1)S(1)} %pad_maximum_fusion.c0), channel_id=1, source_target_pairs={{0,24},{1,25},{2,26},{3,27},{4,28},{5,29},{6,30},{7,31},{8,32},{9,... | collective-permute-start | bytes 1572872 | tf_op jit(solution)/shard_map/ppermute | solution.py:34
  31.1 4.4 %collective-permute-start.7 = (bf16[2,1024,128]{2,1,0:T(8,128)(2,1)S(1)}, bf16[2,1024,128]{2,1,0:T(8,128)(2,1)S(1)}, u32[]{:S(2)}, u32[]{:S(2)}) collective-permute-start(bf16[2,1024,128]{2,1,0:T(8,128)(2,1)S(1)} %pad_maximum_fusion.c0), channel_id=1, source_target_pairs={{0,48},{1,49},{2,50},{3,51},{4,52},{5,53},{6,54},{7,55},{8,56},{9,... | collective-permute-start | bytes 1572872 | tf_op jit(solution)/shard_map/ppermute | solution.py:34
  35.5 3.1 %collective-permute-start.6 = (bf16[2,1024,128]{2,1,0:T(8,128)(2,1)S(1)}, bf16[2,1024,128]{2,1,0:T(8,128)(2,1)S(1)}, u32[]{:S(2)}, u32[]{:S(2)}) collective-permute-start(bf16[2,1024,128]{2,1,0:T(8,128)(2,1)S(1)} %pad_maximum_fusion.c0), channel_id=1, source_target_pairs={{0,72},{1,73},{2,74},{3,75},{4,76},{5,77},{6,78},{7,79},{8,80},{9,... | collective-permute-start | bytes 1572872 | tf_op jit(solution)/shard_map/ppermute | solution.py:34
  38.5 2.3 %scale.1 = bf16[256,128]{1,0:T(8,128)(2,1)} custom-call(f32[1,4,4096]{2,1,0:T(4,128)} %energy.1, s32[1,4,4096]{2,1,0:T(4,128)} %occupied.1, s32[1,256]{1,0:T(1,128)} %first.1, s32[1,256]{1,0:T(1,128)} %second.1, s32[1,256]{1,0:T(1,128)} %kpoint.1, bf16[256,128]{1,0:T(8,128)(2,1)} %block.1), custom_call_target="tpu_custom_call" | custom-call | flops 400000000 | bytes 300000 | tf_op jit(solution)/shard_map/scale/pallas_call | solution.py:91
  40.9 14.8 %collective-permute-start = (bf16[256,128]{1,0:T(8,128)(2,1)}, bf16[256,128]{1,0:T(8,128)(2,1)S(1)}, u32[]{:S(2)}, u32[]{:S(2)}) collective-permute-start(bf16[256,128]{1,0:T(8,128)(2,1)} %scale.1), channel_id=1, source_target_pairs={{0,12},{1,13},{2,110},{3,111},{4,16},{5,17},{6,138},{7,139},{8,44}... | collective-permute-start | bytes 196616 | tf_op jit(solution)/shard_map/ppermute | solution.py:34
  55.9 0.1 stack.44.place
  56.0 1.4 %collective-permute-done = bf16[256,128]{1,0:T(8,128)(2,1)S(1)} collective-permute-done((bf16[256,128]{1,0:T(8,128)(2,1)}, bf16[256,128]{1,0:T(8,128)(2,1)S(1)}, u32[]{:S(2)}, u32[]{:S(2)}) %collective-permute-start) | collective-permute-done | bytes 65568 | tf_op jit(solution)/shard_map/ppermute | solution.py:34
  57.4 35.6 %all-gather = bf16[3072,128]{1,0:T(8,128)(2,1)S(1)} all-gather(bf16[256,128]{1,0:T(8,128)(2,1)S(1)} %collective-permute-done), channel_id=2, replica_groups={{0,98,4,102,8,106,12,110,16,114,20,118},{1,99,5,103,9,107,13,111,17,115..., dimensions={0}, use_global_device_ids=true | all-gather | bytes 851968 | tf_op jit(solution)/shard_map/all_gather | solution.py:187
  92.9 0.0 collective-permute-done.8.c3
  92.9 0.0 collective-permute-done.7.c2
  93.0 0.0 collective-permute-done.6.c1
  93.0 1.2 shard_map.65
  94.1 1.9 %collective-permute-start.9 = (bf16[4,384,128]{2,1,0:T(8,128)(2,1)S(1)}, bf16[4,384,128]{2,1,0:T(8,128)(2,1)S(1)}, u32[]{:S(2)}, u32[]{:S(2)}) collective-permute-start(bf16[4,384,128]{2,1,0:T(8,128)(2,1)S(1)} %shard_map.65), channel_id=1, source_target_pairs={{0,96},{1,97},{2,98},{3,99},{4,100},{5,101},{6,102},{7,103},{8,104... | collective-permute-start | bytes 1179656 | tf_op jit(solution)/shard_map/ppermute | solution.py:34
  96.0 1.1 shard_map.64.keep
  97.2 0.5 collective-permute-done.9.taken
  97.7 0.6 total.1
  98.4 3.0 %collective-permute-start.10 = (bf16[384,128]{1,0:T(8,128)(2,1)S(1)}, bf16[384,128]{1,0:T(8,128)(2,1)S(1)}, u32[]{:S(2)}, u32[]{:S(2)}) collective-permute-start(bf16[384,128]{1,0:T(8,128)(2,1)S(1)} %get-tuple-element.9), channel_id=1, source_target_pairs={{0,0},{1,49},{2,2},{3,51},{4,4},{5,53},{6,6},{7,55},{8,8},{9,57},{... | collective-permute-start | bytes 294920 | tf_op jit(solution)/shard_map/ppermute | solution.py:34
  101.4 2.3 %collective-permute-start.11 = (bf16[384,128]{1,0:T(8,128)(2,1)S(1)}, bf16[384,128]{1,0:T(8,128)(2,1)S(1)}, u32[]{:S(2)}, u32[]{:S(2)}) collective-permute-start(bf16[384,128]{1,0:T(8,128)(2,1)S(1)} %get-tuple-element.10), channel_id=1, source_target_pairs={{0,24},{1,73},{2,26},{3,75},{4,28},{5,77},{6,30},{7,79},{8,32},{9,... | collective-permute-start | bytes 294920 | tf_op jit(solution)/shard_map/ppermute | solution.py:34
  103.7 4.5 %collective-permute-start.12 = (bf16[384,128]{1,0:T(8,128)(2,1)S(1)}, bf16[384,128]{1,0:T(8,128)(2,1)S(1)}, u32[]{:S(2)}, u32[]{:S(2)}) collective-permute-start(bf16[384,128]{1,0:T(8,128)(2,1)S(1)} %get-tuple-element.11), channel_id=1, source_target_pairs={{0,48},{1,1},{2,50},{3,3},{4,52},{5,5},{6,54},{7,7},{8,56},{9,9},{... | collective-permute-start | bytes 294920 | tf_op jit(solution)/shard_map/ppermute | solution.py:34
  108.2 2.3 %collective-permute-start.13 = (bf16[384,128]{1,0:T(8,128)(2,1)S(1)}, bf16[384,128]{1,0:T(8,128)(2,1)S(1)}, u32[]{:S(2)}, u32[]{:S(2)}) collective-permute-start(bf16[384,128]{1,0:T(8,128)(2,1)S(1)} %get-tuple-element.12), channel_id=1, source_target_pairs={{0,72},{1,25},{2,74},{3,27},{4,76},{5,29},{6,78},{7,31},{8,80},{9,... | collective-permute-start | bytes 294920 | tf_op jit(solution)/shard_map/ppermute | solution.py:34
  110.5 0.0 collective-permute-done.10.f0
  110.5 0.0 collective-permute-done.11.f1
  110.5 0.7 collective-permute-done.12.f2
  111.2 4.5 %collective-permute-done.13.f3 = bf16[384,128]{1,0:T(8,128)(2,1)S(1)} collective-permute-done((bf16[384,128]{1,0:T(8,128)(2,1)S(1)}, bf16[384,128]{1,0:T(8,128)(2,1)S(1)}, u32[]{:S(2)}, u32[]{:S(2)}) %collective-permute-start.13) | collective-permute-done | bytes 98336 | tf_op jit(solution)/shard_map/ppermute | solution.py:34
  115.7 1.5 %assemble.1 = f32[2,3,2,128,128]{4,3,2,1,0:T(8,128)} custom-call(s32[8]{0:T(128)S(1)} %stack.44.place, bf16[384,128]{1,0:T(8,128)(2,1)S(1)} %collective-permute-done.10.f0, bf16[384,128]{1,0:T(8,128)(2,1)S(1)} %collective-permute-done.11.f1, bf16[384,128]{1,0:T(8,128)(2,1)S(1)} %collective-permute-done.12.f2, bf16[384,128]{1,0:T(8,128)(2,1)S(1)} %collective-permute-done.13.f3), custom_call_target="tpu_custom_call" | custom-call | tf_op jit(solution)/shard_map/assemble/pallas_call | solution.py:157
  (4 shorter events, 0.0 us)
Async XLA Ops:
  0.0 16.0 %collective-permute-start.1 = (bf16[256,128]{1,0:T(8,128)(2,1)}, bf16[256,128]{1,0:T(8,128)(2,1)S(1)}, u32[]{:S(2)}, u32[]{:S(2)}) collective-permute-start(bf16[256,128]{1,0:T(8,128)(2,1)} %block.1), channel_id=1, source_target_pairs={{0,0},{1,1},{2,98},{3,99},{4,4},{5,5},{6,102},{7,103},{8,8},{9,9},... | collective-permute-start | bytes 196616 | tf_op jit(solution)/shard_map/ppermute | solution.py:34
  1.5 14.5 %collective-permute-start.2 = (bf16[256,128]{1,0:T(8,128)(2,1)}, bf16[256,128]{1,0:T(8,128)(2,1)S(1)}, u32[]{:S(2)}, u32[]{:S(2)}) collective-permute-start(bf16[256,128]{1,0:T(8,128)(2,1)} %block.1), channel_id=1, source_target_pairs={{0,576},{1,577},{2,674},{3,675},{4,580},{5,581},{6,678},{7,679},{8... | collective-permute-start | bytes 196616 | tf_op jit(solution)/shard_map/ppermute | solution.py:34
  8.2 11.3 %collective-permute-start.4 = (bf16[256,128]{1,0:T(8,128)(2,1)}, bf16[256,128]{1,0:T(8,128)(2,1)S(1)}, u32[]{:S(2)}, u32[]{:S(2)}) collective-permute-start(bf16[256,128]{1,0:T(8,128)(2,1)} %block.1), channel_id=1, source_target_pairs={{0,192},{1,193},{2,290},{3,291},{4,196},{5,197},{6,294},{7,295},{8... | collective-permute-start | bytes 196616 | tf_op jit(solution)/shard_map/ppermute | solution.py:34
  10.1 9.4 %collective-permute-start.3 = (bf16[256,128]{1,0:T(8,128)(2,1)}, bf16[256,128]{1,0:T(8,128)(2,1)S(1)}, u32[]{:S(2)}, u32[]{:S(2)}) collective-permute-start(bf16[256,128]{1,0:T(8,128)(2,1)} %block.1), channel_id=1, source_target_pairs={{0,384},{1,385},{2,482},{3,483},{4,388},{5,389},{6,486},{7,487},{8... | collective-permute-start | bytes 196616 | tf_op jit(solution)/shard_map/ppermute | solution.py:34
  19.5 7.1 %collective-permute-start.5 = (bf16[1024,128]{1,0:T(8,128)(2,1)S(1)}, bf16[1024,128]{1,0:T(8,128)(2,1)S(1)}, u32[]{:S(2)}, u32[]{:S(2)}) collective-permute-start(bf16[1024,128]{1,0:T(8,128)(2,1)S(1)} %constant_dynamic-update-slice_fusion), channel_id=1, source_target_pairs={{0,1},{1,0},{2,3},{3,2},{4,5},{5,4},{6,7},{7,6},{8,9},{9,8},{10,11... | collective-permute-start | bytes 786440 | tf_op jit(solution)/shard_map/ppermute | solution.py:34
  26.7 66.3 %collective-permute-start.8 = (bf16[2,1024,128]{2,1,0:T(8,128)(2,1)S(1)}, bf16[2,1024,128]{2,1,0:T(8,128)(2,1)S(1)}, u32[]{:S(2)}, u32[]{:S(2)}) collective-permute-start(bf16[2,1024,128]{2,1,0:T(8,128)(2,1)S(1)} %pad_maximum_fusion.c0), channel_id=1, source_target_pairs={{0,24},{1,25},{2,26},{3,27},{4,28},{5,29},{6,30},{7,31},{8,32},{9,... | collective-permute-start | bytes 1572872 | tf_op jit(solution)/shard_map/ppermute | solution.py:34
  31.1 61.8 %collective-permute-start.7 = (bf16[2,1024,128]{2,1,0:T(8,128)(2,1)S(1)}, bf16[2,1024,128]{2,1,0:T(8,128)(2,1)S(1)}, u32[]{:S(2)}, u32[]{:S(2)}) collective-permute-start(bf16[2,1024,128]{2,1,0:T(8,128)(2,1)S(1)} %pad_maximum_fusion.c0), channel_id=1, source_target_pairs={{0,48},{1,49},{2,50},{3,51},{4,52},{5,53},{6,54},{7,55},{8,56},{9,... | collective-permute-start | bytes 1572872 | tf_op jit(solution)/shard_map/ppermute | solution.py:34
  35.5 57.5 %collective-permute-start.6 = (bf16[2,1024,128]{2,1,0:T(8,128)(2,1)S(1)}, bf16[2,1024,128]{2,1,0:T(8,128)(2,1)S(1)}, u32[]{:S(2)}, u32[]{:S(2)}) collective-permute-start(bf16[2,1024,128]{2,1,0:T(8,128)(2,1)S(1)} %pad_maximum_fusion.c0), channel_id=1, source_target_pairs={{0,72},{1,73},{2,74},{3,75},{4,76},{5,77},{6,78},{7,79},{8,80},{9,... | collective-permute-start | bytes 1572872 | tf_op jit(solution)/shard_map/ppermute | solution.py:34
  40.9 16.5 %collective-permute-start = (bf16[256,128]{1,0:T(8,128)(2,1)}, bf16[256,128]{1,0:T(8,128)(2,1)S(1)}, u32[]{:S(2)}, u32[]{:S(2)}) collective-permute-start(bf16[256,128]{1,0:T(8,128)(2,1)} %scale.1), channel_id=1, source_target_pairs={{0,12},{1,13},{2,110},{3,111},{4,16},{5,17},{6,138},{7,139},{8,44}... | collective-permute-start | bytes 196616 | tf_op jit(solution)/shard_map/ppermute | solution.py:34
  94.1 3.6 %collective-permute-start.9 = (bf16[4,384,128]{2,1,0:T(8,128)(2,1)S(1)}, bf16[4,384,128]{2,1,0:T(8,128)(2,1)S(1)}, u32[]{:S(2)}, u32[]{:S(2)}) collective-permute-start(bf16[4,384,128]{2,1,0:T(8,128)(2,1)S(1)} %shard_map.65), channel_id=1, source_target_pairs={{0,96},{1,97},{2,98},{3,99},{4,100},{5,101},{6,102},{7,103},{8,104... | collective-permute-start | bytes 1179656 | tf_op jit(solution)/shard_map/ppermute | solution.py:34
  98.4 12.1 %collective-permute-start.10 = (bf16[384,128]{1,0:T(8,128)(2,1)S(1)}, bf16[384,128]{1,0:T(8,128)(2,1)S(1)}, u32[]{:S(2)}, u32[]{:S(2)}) collective-permute-start(bf16[384,128]{1,0:T(8,128)(2,1)S(1)} %get-tuple-element.9), channel_id=1, source_target_pairs={{0,0},{1,49},{2,2},{3,51},{4,4},{5,53},{6,6},{7,55},{8,8},{9,57},{... | collective-permute-start | bytes 294920 | tf_op jit(solution)/shard_map/ppermute | solution.py:34
  101.4 9.1 %collective-permute-start.11 = (bf16[384,128]{1,0:T(8,128)(2,1)S(1)}, bf16[384,128]{1,0:T(8,128)(2,1)S(1)}, u32[]{:S(2)}, u32[]{:S(2)}) collective-permute-start(bf16[384,128]{1,0:T(8,128)(2,1)S(1)} %get-tuple-element.10), channel_id=1, source_target_pairs={{0,24},{1,73},{2,26},{3,75},{4,28},{5,77},{6,30},{7,79},{8,32},{9,... | collective-permute-start | bytes 294920 | tf_op jit(solution)/shard_map/ppermute | solution.py:34
  103.7 7.4 %collective-permute-start.12 = (bf16[384,128]{1,0:T(8,128)(2,1)S(1)}, bf16[384,128]{1,0:T(8,128)(2,1)S(1)}, u32[]{:S(2)}, u32[]{:S(2)}) collective-permute-start(bf16[384,128]{1,0:T(8,128)(2,1)S(1)} %get-tuple-element.11), channel_id=1, source_target_pairs={{0,48},{1,1},{2,50},{3,3},{4,52},{5,5},{6,54},{7,7},{8,56},{9,9},{... | collective-permute-start | bytes 294920 | tf_op jit(solution)/shard_map/ppermute | solution.py:34
  108.2 7.5 %collective-permute-start.13 = (bf16[384,128]{1,0:T(8,128)(2,1)S(1)}, bf16[384,128]{1,0:T(8,128)(2,1)S(1)}, u32[]{:S(2)}, u32[]{:S(2)}) collective-permute-start(bf16[384,128]{1,0:T(8,128)(2,1)S(1)} %get-tuple-element.12), channel_id=1, source_target_pairs={{0,72},{1,25},{2,74},{3,27},{4,76},{5,29},{6,78},{7,31},{8,80},{9,... | collective-permute-start | bytes 294920 | tf_op jit(solution)/shard_map/ppermute | solution.py:34

commit v11 on v3

--- a/solution.py
+++ b/solution.py
@@ -88,6 +88,21 @@
     )(energy, occupied, first, second, kpoint, block)
 
 
+def join_kernel(*refs):
+    for i, part in enumerate(refs[:-1]):
+        refs[-1][i] = part[...]
+
+
+def join(parts):
+    return pl.pallas_call(
+        join_kernel,
+        out_shape=jax.ShapeDtypeStruct((len(parts),) + parts[0].shape, parts[0].dtype),
+        in_specs=[pl.BlockSpec(memory_space=pltpu.VMEM)] * len(parts),
+        out_specs=pl.BlockSpec(memory_space=pltpu.VMEM),
+        compiler_params=pltpu.CompilerParams(vmem_limit_bytes=8 * 2**20),
+    )(*parts)
+
+
 def product_kernel(side, place, rows, c0, c1, c2, c3, out):
     which = place[side]
 
@@ -183,7 +198,7 @@
     )
     sent = move(scaled, spread)
     other = move(own, lambda h, k, x, z, l: (h, k, x, z, 1 - l))
-    both = jnp.stack([own, other])
+    both = join([own, other])
     columns = [both]
     for s in range(1, X):
         columns.append(move(both, lambda h, k, x, z, l, s=s: (h, k, x - s, z, l)))

time: 114 us -> 114 us (level)
  no operation moved by 1% of the time
where the time goes in v11:
time: 114 us; the launch traced here: 113 us
  starting transfers between devices  54.6 us (48%)
  blocking collectives  40.2 us (35%)
  waiting for transfers between devices  11.6 us (10%)
  Pallas kernels  6.78 us (6%)
    ppermute x10, starting transfers between devices, move(): return lax.ppermute(value, AXES, table(f))  54.6 us
    all_gather x1, blocking collectives, blocks(): rows = lax.all_gather(sent, 'col', axis=0, axis_index_groups=Z_GROUPS)  25.2 us
    all_gather x1, blocking collectives, blocks(): lax.all_gather(pair_matrix, 'pool', axis=0, tiled=True, axis_index_groups...  15 us
    ppermute x10, waiting for transfers between devices, move(): return lax.ppermute(value, AXES, table(f))  11.6 us
    pallas_call x1, Pallas kernels, scaled_block(): pl.pallas_call(scale_kernel, out_shape=jax.ShapeDtypeStruct(block.shape,...  2.35 us
    pallas_call x2, Pallas kernels, product(): pl.pallas_call(functools.partial(product_kernel, side), out_shape=jax.Sha...  2.3 us
  transfers between devices with their start and end apart: 10, of which 5 were waited for; matrix products, arithmetic and copies ran while one was open for 0% of the time, Pallas kernels for 3%

profile of v11, /device:TPU:1, one launch (start us, length us, event | category | flops | bytes accessed | tf_op | source)
XLA Modules:
  0.0 113.5 jit_solution(5212207746707673705)
XLA Ops:
  0.0 15.0 %all_gather.11.refs_0_ = bf16[1024,128]{1,0:T(8,128)(2,1)S(1)} all-gather(bf16[256,128]{1,0:T(8,128)(2,1)} %block.1), channel_id=1, replica_groups={{0,192,384,576},{96,288,480,672},{1,193,385,577},{97,289,481,673},{2,19..., dimensions={0}, use_global_device_ids=true | all-gather | bytes 327680 | tf_op jit(solution)/shard_map/all_gather | solution.py:193
  15.0 2.2 %collective-permute-start.1 = (bf16[1024,128]{1,0:T(8,128)(2,1)S(1)}, bf16[1024,128]{1,0:T(8,128)(2,1)S(1)}, u32[]{:S(2)}, u32[]{:S(2)}) collective-permute-start(bf16[1024,128]{1,0:T(8,128)(2,1)S(1)} %all_gather.11.refs_0_), channel_id=1, source_target_pairs={{0,1},{1,0},{2,3},{3,2},{4,5},{5,4},{6,7},{7,6},{8,9},{9,8},{10,11... | collective-permute-start | bytes 786440 | tf_op jit(solution)/shard_map/ppermute | solution.py:34
  17.2 4.9 %collective-permute-done.1.refs_1_ = bf16[1024,128]{1,0:T(8,128)(2,1)S(1)} collective-permute-done((bf16[1024,128]{1,0:T(8,128)(2,1)S(1)}, bf16[1024,128]{1,0:T(8,128)(2,1)S(1)}, u32[]{:S(2)}, u32[]{:S(2)}) %collective-permute-start.1) | collective-permute-done | bytes 262176 | tf_op jit(solution)/shard_map/ppermute | solution.py:34
  22.2 3.0 %collective-permute-start.4 = (bf16[2,1024,128]{2,1,0:T(8,128)(2,1)S(1)}, bf16[2,1024,128]{2,1,0:T(8,128)(2,1)S(1)}, u32[]{:S(2)}, u32[]{:S(2)}) collective-permute-start(bf16[2,1024,128]{2,1,0:T(8,128)(2,1)S(1)} %shard_map.64.c0), channel_id=1, source_target_pairs={{0,24},{1,25},{2,26},{3,27},{4,28},{5,29},{6,30},{7,31},{8,32},{9,... | collective-permute-start | bytes 1572872 | tf_op jit(solution)/shard_map/ppermute | solution.py:34
  25.2 4.4 %collective-permute-start.3 = (bf16[2,1024,128]{2,1,0:T(8,128)(2,1)S(1)}, bf16[2,1024,128]{2,1,0:T(8,128)(2,1)S(1)}, u32[]{:S(2)}, u32[]{:S(2)}) collective-permute-start(bf16[2,1024,128]{2,1,0:T(8,128)(2,1)S(1)} %shard_map.64.c0), channel_id=1, source_target_pairs={{0,48},{1,49},{2,50},{3,51},{4,52},{5,53},{6,54},{7,55},{8,56},{9,... | collective-permute-start | bytes 1572872 | tf_op jit(solution)/shard_map/ppermute | solution.py:34
  29.6 3.1 %collective-permute-start.2 = (bf16[2,1024,128]{2,1,0:T(8,128)(2,1)S(1)}, bf16[2,1024,128]{2,1,0:T(8,128)(2,1)S(1)}, u32[]{:S(2)}, u32[]{:S(2)}) collective-permute-start(bf16[2,1024,128]{2,1,0:T(8,128)(2,1)S(1)} %shard_map.64.c0), channel_id=1, source_target_pairs={{0,72},{1,73},{2,74},{3,75},{4,76},{5,77},{6,78},{7,79},{8,80},{9,... | collective-permute-start | bytes 1572872 | tf_op jit(solution)/shard_map/ppermute | solution.py:34
  32.7 2.4 %scale.1 = bf16[256,128]{1,0:T(8,128)(2,1)} custom-call(f32[1,4,4096]{2,1,0:T(4,128)} %energy.1, s32[1,4,4096]{2,1,0:T(4,128)} %occupied.1, s32[1,256]{1,0:T(1,128)} %first.1, s32[1,256]{1,0:T(1,128)} %second.1, s32[1,256]{1,0:T(1,128)} %kpoint.1, bf16[256,128]{1,0:T(8,128)(2,1)} %block.1), custom_call_target="tpu_custom_call" | custom-call | flops 400000000 | bytes 300000 | tf_op jit(solution)/shard_map/scale/pallas_call | solution.py:82
  35.0 14.3 %collective-permute-start = (bf16[256,128]{1,0:T(8,128)(2,1)}, bf16[256,128]{1,0:T(8,128)(2,1)S(1)}, u32[]{:S(2)}, u32[]{:S(2)}) collective-permute-start(bf16[256,128]{1,0:T(8,128)(2,1)} %scale.1), channel_id=1, source_target_pairs={{0,18},{1,19},{2,44},{3,45},{4,10},{5,11},{6,36},{7,37},{8,16},{9,... | collective-permute-start | bytes 196616 | tf_op jit(solution)/shard_map/ppermute | solution.py:34
  49.5 0.1 stack.39.place
  49.5 1.4 %collective-permute-done = bf16[256,128]{1,0:T(8,128)(2,1)S(1)} collective-permute-done((bf16[256,128]{1,0:T(8,128)(2,1)}, bf16[256,128]{1,0:T(8,128)(2,1)S(1)}, u32[]{:S(2)}, u32[]{:S(2)}) %collective-permute-start) | collective-permute-done | bytes 65568 | tf_op jit(solution)/shard_map/ppermute | solution.py:34
  50.9 25.2 %all-gather = bf16[3072,128]{1,0:T(8,128)(2,1)S(1)} all-gather(bf16[256,128]{1,0:T(8,128)(2,1)S(1)} %collective-permute-done), channel_id=2, replica_groups={{0,2,4,6,8,10,12,14,16,18,20,22},{1,3,5,7,9,11,13,15,17,19,21,23},{24,2..., dimensions={0}, use_global_device_ids=true | all-gather | bytes 851968 | tf_op jit(solution)/shard_map/all_gather | solution.py:205
  76.1 0.0 collective-permute-done.4.c3
  76.1 0.0 collective-permute-done.3.c2
  76.1 0.0 collective-permute-done.2.c1
  76.1 1.2 %shard_map.66 = bf16[4,384,128]{2,1,0:T(8,128)(2,1)S(1)} custom-call(s32[9]{0:T(128)S(1)} %stack.39.place, bf16[12,256,128]{2,1,0:T(8,128)(2,1)S(1)} %bitcast.11, bf16[2,1024,128]{2,1,0:T(8,128)(2,1)S(1)} %shard_map.64.c0, bf16[2,1024,128]{2,1,0:T(8,128)(2,1)S(1)} %collective-permute-done.2.c1, bf16[2,1024,128]{2,1,0:T(8,128)(2,1)S(1)} %collective-permute-done.3.c2, ...), custom_call_target="tpu_custom_call" | custom-call | flops 400000000 | bytes 3000000 | tf_op jit(solution)/shard_map/pallas_call | solution.py:139
  77.3 13.0 %collective-permute-start.5 = (bf16[4,384,128]{2,1,0:T(8,128)(2,1)S(1)}, bf16[4,384,128]{2,1,0:T(8,128)(2,1)S(1)}, u32[]{:S(2)}, u32[]{:S(2)}) collective-permute-start(bf16[4,384,128]{2,1,0:T(8,128)(2,1)S(1)} %shard_map.66), channel_id=1, source_target_pairs={{0,96},{1,97},{2,98},{3,99},{4,100},{5,101},{6,102},{7,103},{8,104... | collective-permute-start | bytes 1179656 | tf_op jit(solution)/shard_map/ppermute | solution.py:34
  90.2 1.1 %shard_map.65.keep = f32[4,384,128]{2,1,0:T(8,128)S(1)} custom-call(s32[9]{0:T(128)S(1)} %stack.39.place, bf16[12,256,128]{2,1,0:T(8,128)(2,1)S(1)} %bitcast.12, bf16[2,1024,128]{2,1,0:T(8,128)(2,1)S(1)} %shard_map.64.c0, bf16[2,1024,128]{2,1,0:T(8,128)(2,1)S(1)} %collective-permute-done.2.c1, bf16[2,1024,128]{2,1,0:T(8,128)(2,1)S(1)} %collective-permute-done.3.c2, ...), custom_call_target="tpu_custom_call" | custom-call | flops 400000000 | bytes 3000000 | tf_op jit(solution)/shard_map/pallas_call | solution.py:139
  91.4 0.2 collective-permute-done.5.taken
  91.6 0.6 total.1
  92.2 2.8 %collective-permute-start.6 = (bf16[384,128]{1,0:T(8,128)(2,1)S(1)}, bf16[384,128]{1,0:T(8,128)(2,1)S(1)}, u32[]{:S(2)}, u32[]{:S(2)}) collective-permute-start(bf16[384,128]{1,0:T(8,128)(2,1)S(1)} %get-tuple-element.9), channel_id=1, source_target_pairs={{0,0},{1,49},{2,2},{3,51},{4,4},{5,53},{6,6},{7,55},{8,8},{9,57},{... | collective-permute-start | bytes 294920 | tf_op jit(solution)/shard_map/ppermute | solution.py:34
  95.0 5.7 %collective-permute-start.7 = (bf16[384,128]{1,0:T(8,128)(2,1)S(1)}, bf16[384,128]{1,0:T(8,128)(2,1)S(1)}, u32[]{:S(2)}, u32[]{:S(2)}) collective-permute-start(bf16[384,128]{1,0:T(8,128)(2,1)S(1)} %get-tuple-element.10), channel_id=1, source_target_pairs={{0,24},{1,73},{2,26},{3,75},{4,28},{5,77},{6,30},{7,79},{8,32},{9,... | collective-permute-start | bytes 294920 | tf_op jit(solution)/shard_map/ppermute | solution.py:34
  100.8 3.8 %collective-permute-start.8 = (bf16[384,128]{1,0:T(8,128)(2,1)S(1)}, bf16[384,128]{1,0:T(8,128)(2,1)S(1)}, u32[]{:S(2)}, u32[]{:S(2)}) collective-permute-start(bf16[384,128]{1,0:T(8,128)(2,1)S(1)} %get-tuple-element.11), channel_id=1, source_target_pairs={{0,48},{1,1},{2,50},{3,3},{4,52},{5,5},{6,54},{7,7},{8,56},{9,9},{... | collective-permute-start | bytes 294920 | tf_op jit(solution)/shard_map/ppermute | solution.py:34
  104.5 2.3 %collective-permute-start.9 = (bf16[384,128]{1,0:T(8,128)(2,1)S(1)}, bf16[384,128]{1,0:T(8,128)(2,1)S(1)}, u32[]{:S(2)}, u32[]{:S(2)}) collective-permute-start(bf16[384,128]{1,0:T(8,128)(2,1)S(1)} %get-tuple-element.12), channel_id=1, source_target_pairs={{0,72},{1,25},{2,74},{3,27},{4,76},{5,29},{6,78},{7,31},{8,80},{9,... | collective-permute-start | bytes 294920 | tf_op jit(solution)/shard_map/ppermute | solution.py:34
  106.9 0.0 collective-permute-done.6.f0
  106.9 0.0 collective-permute-done.7.f1
  106.9 1.3 %collective-permute-done.8.f2 = bf16[384,128]{1,0:T(8,128)(2,1)S(1)} collective-permute-done((bf16[384,128]{1,0:T(8,128)(2,1)S(1)}, bf16[384,128]{1,0:T(8,128)(2,1)S(1)}, u32[]{:S(2)}, u32[]{:S(2)}) %collective-permute-start.8) | collective-permute-done | bytes 98336 | tf_op jit(solution)/shard_map/ppermute | solution.py:34
  108.2 3.8 %collective-permute-done.9.f3 = bf16[384,128]{1,0:T(8,128)(2,1)S(1)} collective-permute-done((bf16[384,128]{1,0:T(8,128)(2,1)S(1)}, bf16[384,128]{1,0:T(8,128)(2,1)S(1)}, u32[]{:S(2)}, u32[]{:S(2)}) %collective-permute-start.9) | collective-permute-done | bytes 98336 | tf_op jit(solution)/shard_map/ppermute | solution.py:34
  112.0 1.5 %assemble.1 = f32[3,2,2,128,128]{4,3,2,1,0:T(8,128)} custom-call(s32[9]{0:T(128)S(1)} %stack.39.place, bf16[384,128]{1,0:T(8,128)(2,1)S(1)} %collective-permute-done.6.f0, bf16[384,128]{1,0:T(8,128)(2,1)S(1)} %collective-permute-done.7.f1, bf16[384,128]{1,0:T(8,128)(2,1)S(1)} %collective-permute-done.8.f2, bf16[384,128]{1,0:T(8,128)(2,1)S(1)} %collective-permute-done.9.f3), custom_call_target="tpu_custom_call" | custom-call | tf_op jit(solution)/shard_map/assemble/pallas_call | solution.py:174
  (1 shorter events, 0.0 us)
Async XLA Ops:
  15.0 7.1 %collective-permute-start.1 = (bf16[1024,128]{1,0:T(8,128)(2,1)S(1)}, bf16[1024,128]{1,0:T(8,128)(2,1)S(1)}, u32[]{:S(2)}, u32[]{:S(2)}) collective-permute-start(bf16[1024,128]{1,0:T(8,128)(2,1)S(1)} %all_gather.11.refs_0_), channel_id=1, source_target_pairs={{0,1},{1,0},{2,3},{3,2},{4,5},{5,4},{6,7},{7,6},{8,9},{9,8},{10,11... | collective-permute-start | bytes 786440 | tf_op jit(solution)/shard_map/ppermute | solution.py:34
  22.2 53.9 %collective-permute-start.4 = (bf16[2,1024,128]{2,1,0:T(8,128)(2,1)S(1)}, bf16[2,1024,128]{2,1,0:T(8,128)(2,1)S(1)}, u32[]{:S(2)}, u32[]{:S(2)}) collective-permute-start(bf16[2,1024,128]{2,1,0:T(8,128)(2,1)S(1)} %shard_map.64.c0), channel_id=1, source_target_pairs={{0,24},{1,25},{2,26},{3,27},{4,28},{5,29},{6,30},{7,31},{8,32},{9,... | collective-permute-start | bytes 1572872 | tf_op jit(solution)/shard_map/ppermute | solution.py:34
  25.2 50.9 %collective-permute-start.3 = (bf16[2,1024,128]{2,1,0:T(8,128)(2,1)S(1)}, bf16[2,1024,128]{2,1,0:T(8,128)(2,1)S(1)}, u32[]{:S(2)}, u32[]{:S(2)}) collective-permute-start(bf16[2,1024,128]{2,1,0:T(8,128)(2,1)S(1)} %shard_map.64.c0), channel_id=1, source_target_pairs={{0,48},{1,49},{2,50},{3,51},{4,52},{5,53},{6,54},{7,55},{8,56},{9,... | collective-permute-start | bytes 1572872 | tf_op jit(solution)/shard_map/ppermute | solution.py:34
  29.6 46.5 %collective-permute-start.2 = (bf16[2,1024,128]{2,1,0:T(8,128)(2,1)S(1)}, bf16[2,1024,128]{2,1,0:T(8,128)(2,1)S(1)}, u32[]{:S(2)}, u32[]{:S(2)}) collective-permute-start(bf16[2,1024,128]{2,1,0:T(8,128)(2,1)S(1)} %shard_map.64.c0), channel_id=1, source_target_pairs={{0,72},{1,73},{2,74},{3,75},{4,76},{5,77},{6,78},{7,79},{8,80},{9,... | collective-permute-start | bytes 1572872 | tf_op jit(solution)/shard_map/ppermute | solution.py:34
  35.0 15.9 %collective-permute-start = (bf16[256,128]{1,0:T(8,128)(2,1)}, bf16[256,128]{1,0:T(8,128)(2,1)S(1)}, u32[]{:S(2)}, u32[]{:S(2)}) collective-permute-start(bf16[256,128]{1,0:T(8,128)(2,1)} %scale.1), channel_id=1, source_target_pairs={{0,18},{1,19},{2,44},{3,45},{4,10},{5,11},{6,36},{7,37},{8,16},{9,... | collective-permute-start | bytes 196616 | tf_op jit(solution)/shard_map/ppermute | solution.py:34
  77.3 14.3 %collective-permute-start.5 = (bf16[4,384,128]{2,1,0:T(8,128)(2,1)S(1)}, bf16[4,384,128]{2,1,0:T(8,128)(2,1)S(1)}, u32[]{:S(2)}, u32[]{:S(2)}) collective-permute-start(bf16[4,384,128]{2,1,0:T(8,128)(2,1)S(1)} %shard_map.66), channel_id=1, source_target_pairs={{0,96},{1,97},{2,98},{3,99},{4,100},{5,101},{6,102},{7,103},{8,104... | collective-permute-start | bytes 1179656 | tf_op jit(solution)/shard_map/ppermute | solution.py:34
  92.2 14.7 %collective-permute-start.6 = (bf16[384,128]{1,0:T(8,128)(2,1)S(1)}, bf16[384,128]{1,0:T(8,128)(2,1)S(1)}, u32[]{:S(2)}, u32[]{:S(2)}) collective-permute-start(bf16[384,128]{1,0:T(8,128)(2,1)S(1)} %get-tuple-element.9), channel_id=1, source_target_pairs={{0,0},{1,49},{2,2},{3,51},{4,4},{5,53},{6,6},{7,55},{8,8},{9,57},{... | collective-permute-start | bytes 294920 | tf_op jit(solution)/shard_map/ppermute | solution.py:34
  95.0 11.9 %collective-permute-start.7 = (bf16[384,128]{1,0:T(8,128)(2,1)S(1)}, bf16[384,128]{1,0:T(8,128)(2,1)S(1)}, u32[]{:S(2)}, u32[]{:S(2)}) collective-permute-start(bf16[384,128]{1,0:T(8,128)(2,1)S(1)} %get-tuple-element.10), channel_id=1, source_target_pairs={{0,24},{1,73},{2,26},{3,75},{4,28},{5,77},{6,30},{7,79},{8,32},{9,... | collective-permute-start | bytes 294920 | tf_op jit(solution)/shard_map/ppermute | solution.py:34
  100.8 7.4 %collective-permute-start.8 = (bf16[384,128]{1,0:T(8,128)(2,1)S(1)}, bf16[384,128]{1,0:T(8,128)(2,1)S(1)}, u32[]{:S(2)}, u32[]{:S(2)}) collective-permute-start(bf16[384,128]{1,0:T(8,128)(2,1)S(1)} %get-tuple-element.11), channel_id=1, source_target_pairs={{0,48},{1,1},{2,50},{3,3},{4,52},{5,5},{6,54},{7,7},{8,56},{9,9},{... | collective-permute-start | bytes 294920 | tf_op jit(solution)/shard_map/ppermute | solution.py:34
  104.5 7.5 %collective-permute-start.9 = (bf16[384,128]{1,0:T(8,128)(2,1)S(1)}, bf16[384,128]{1,0:T(8,128)(2,1)S(1)}, u32[]{:S(2)}, u32[]{:S(2)}) collective-permute-start(bf16[384,128]{1,0:T(8,128)(2,1)S(1)} %get-tuple-element.12), channel_id=1, source_target_pairs={{0,72},{1,25},{2,74},{3,27},{4,76},{5,29},{6,78},{7,31},{8,80},{9,... | collective-permute-start | bytes 294920 | tf_op jit(solution)/shard_map/ppermute | solution.py:34
